TPU v7x, 128 devices: a whole 4x4x4 slice. The times are simulated.
128 devices in a mesh: dp: 4 (over z), expert: 32 (over x, y, core).
Axes of the slice: x: 4, y: 4, z: 4, core: 2. Of those that a mesh axis runs over, the one named last changes fastest.
Arguments:
- grad_parts: bfloat16 [4, 128, 128, 2048], P('dp', 'expert'), may hold values from -6 to 6
- first_moment: float32 [128, 128, 2048], P('expert', None, 'dp'), may hold values from -4 to 4
- second_moment: float32 [128, 128, 2048], P('expert', None, 'dp'), may hold values from 0.05 to 2
- master_weight: float32 [128, 128, 2048], P('expert', None, 'dp'), may hold values from -6 to 6
- old_owner: int32 [104], replicated, may hold values from 0 to 25, as said below
- new_owner: int32 [104], replicated, may hold values from 0 to 31, as said below
Outputs:
- new_master: float32 [192, 128, 2048], P('expert', None, 'dp')
- new_first: float32 [192, 128, 2048], P('expert', None, 'dp')
- new_second: float32 [192, 128, 2048], P('expert', None, 'dp')
- new_params: bfloat16 [192, 128, 2048], P('expert')
Inputs may be any that keep to these rules, and one draw needn't show every extreme that they name: `old_owner`: tiles are owned by devices 0 to 25 of the expert axis, exactly 4 each; the other devices own none, and their slots of the old-layout arrays are never read. `new_owner`: each device owns at most 6 tiles and some own exactly 6; the tiles of one old owner go to different new owners.
All inputs are finite; a program needn't handle non-finite values.
Results may differ from a plain program's by a relative error of at most 0.0085.
Values may be sent and summed in bfloat16 or wider, within the bound.
No kernel may reach another device: no remote copies, remote signals or barrier semaphores. Data moves between devices by JAX's collectives and lax.ppermute only.
A program may use at most 128 MiB of HBM per device.

v0:
```python
import jax
import jax.numpy as jnp
from jax import lax
from jax.sharding import PartitionSpec as P


def slot_ranks(owner, count):
    matches = (owner[:, None] == jnp.arange(count, dtype=jnp.int32)[None, :]).astype(jnp.int32)
    before = jnp.cumsum(matches, axis=0) - matches
    return jnp.sum(before * matches, axis=1)


def adam_step(gradient, moment_one, moment_two, weight):
    moment_one = 0.9 * moment_one + 0.1 * gradient
    moment_two = 0.95 * moment_two + 0.05 * gradient * gradient
    update = moment_one / (1.0 - 0.9**50) / (jnp.sqrt(moment_two / (1.0 - 0.95**50)) + 1e-08)
    weight = weight - 0.05 * (update + 0.1 * weight)
    return (weight, moment_one, moment_two)


def shards(grad_parts, first_moment, second_moment, master_weight, old_owner, new_owner):
    peer_count = lax.axis_size("expert")
    device = lax.axis_index("expert")
    old_slots = first_moment.shape[0]
    new_slots = min(old_slots + old_slots // 2, peer_count - peer_count // 5)
    old_rank = slot_ranks(old_owner, peer_count)
    new_rank = slot_ranks(new_owner, peer_count)
    targets = jnp.arange(peer_count, dtype=jnp.int32)
    outgoing = (old_owner == device)[:, None] & (new_owner[:, None] == targets[None, :])
    send_has = jnp.sum(outgoing.astype(jnp.int32), axis=0) > 0
    send_slot = jnp.sum(jnp.where(outgoing, old_rank[:, None], 0), axis=0)
    slot_ids = jnp.arange(new_slots, dtype=jnp.int32)
    wanted = (new_owner == device)[:, None] & (new_rank[:, None] == slot_ids[None, :])
    recv_has = jnp.sum(wanted.astype(jnp.int32), axis=0) > 0
    recv_source = jnp.sum(jnp.where(wanted, old_owner[:, None], 0), axis=0)

    def to_peers(values):
        return jnp.where(send_has[:, None, None], values[send_slot], 0.0)

    def from_peers(values):
        return jnp.where(recv_has[:, None, None], values[recv_source], 0.0)

    summed = lax.psum_scatter(grad_parts[0], "dp", scatter_dimension=2, tiled=True).astype(
        jnp.float32
    )
    weight, moment_one, moment_two = adam_step(summed, first_moment, second_moment, master_weight)
    results = (
        lax.all_to_all(
            to_peers(weight).astype(jnp.bfloat16), "expert", split_axis=0, concat_axis=0, tiled=True
        ).astype(jnp.float32),
        lax.all_to_all(
            to_peers(moment_one).astype(jnp.bfloat16),
            "expert",
            split_axis=0,
            concat_axis=0,
            tiled=True,
        ).astype(jnp.float32),
        lax.all_to_all(
            to_peers(moment_two).astype(jnp.bfloat16),
            "expert",
            split_axis=0,
            concat_axis=0,
            tiled=True,
        ).astype(jnp.float32),
    )
    new_master = from_peers(results[0])
    new_first = from_peers(results[1])
    new_second = from_peers(results[2])
    new_params = lax.all_gather(new_master.astype(jnp.bfloat16), "dp", axis=2, tiled=True)
    return (new_master, new_first, new_second, new_params)


def solution(mesh):
    placed = (
        P("dp", "expert", None, None),
        P("expert", None, "dp"),
        P("expert", None, "dp"),
        P("expert", None, "dp"),
        P(),
        P(),
    )
    return jax.shard_map(
        shards,
        mesh=mesh,
        in_specs=placed,
        out_specs=(
            P("expert", None, "dp"),
            P("expert", None, "dp"),
            P("expert", None, "dp"),
            P("expert", None, None),
        ),
        check_vma=False,
    )
```

profile of v0, /device:TPU:1, one launch (start us, length us, event | category | flops | bytes accessed | tf_op | source)
XLA Modules:
  0.0 297.9 jit_solution(7554008019410971334)
XLA Ops:
  7.9 0.7 fusion.2
  8.8 0.7 fusion.4
  9.7 0.8 select_reduce_fusion.1
  10.5 0.7 broadcast_compare_fusion.2
  11.2 0.9 convert_reduce_fusion
  12.1 31.5 %reduce-scatter.2.cloned.1.call-done = bf16[4,128,512]{2,1,0:T(8,128)(2,1)} async-done(((bf16[4,128,2048]{2,1,0:T(8,128)(2,1)}), bf16[4,128,512]{2,1,0:T(8,128)(2,1)}) %reduce-scatter.2.cloned.1.call-update) | async-done | bytes 524304 | tf_op jit(solution)/shard_map/reduce_scatter | solution.py:43
  43.6 3.0 multiply_subtract_fusion
  46.6 2.8 gather_fusion
  49.3 2.7 gather_fusion.2
  52.1 2.8 gather_fusion.4
  54.9 7.9 %select_convert_fusion = (bf16[32,128,512]{2,1,0:T(8,128)(2,1)}, bf16[32,128,512]{2,1,0:T(8,128)(2,1)S(1)}, bf16[32,128,512]{2,1,0:T(8,128)(2,1)S(1)}) fusion(bf16[32,128,512]{2,1,0:T(8,128)(2,1)} %gather_fusion.4, pred[32]{0:T(512)(128)(4,1)S(1)} %broadcast_compare_fusion, bf16[32,128,512]{2,1,0:T(8,128)(2,1)} %gather_fusion.2, ...), kind=kLoop, calls=%fused_computation.6 | loop fusion | flops 6291456 | bytes 25165856 | tf_op jit(solution)/shard_map/convert_element_type | solution.py:59
  62.8 58.0 %all_to_all.15 = bf16[32,128,512]{2,1,0:T(8,128)(2,1)} all-to-all(bf16[32,128,512]{2,1,0:T(8,128)(2,1)S(1)} %get-tuple-element.20), channel_id=1, replica_groups=mesh['dp'=4,'expert'=32] {'expert'}, dimensions={0} | all-to-all | bytes 8388608 | tf_op jit(solution)/shard_map/all_to_all | solution.py:48
  120.7 54.5 %all_to_all.16 = bf16[32,128,512]{2,1,0:T(8,128)(2,1)} all-to-all(bf16[32,128,512]{2,1,0:T(8,128)(2,1)S(1)} %get-tuple-element.19), channel_id=1, replica_groups=mesh['dp'=4,'expert'=32] {'expert'}, dimensions={0} | all-to-all | bytes 8388608 | tf_op jit(solution)/shard_map/all_to_all | solution.py:51
  175.2 4.8 %all-to-all-start.2 = ((bf16[32,128,512]{2,1,0:T(8,128)(2,1)}), bf16[32,128,512]{2,1,0:T(8,128)(2,1)}, u32[]{:S(2)}, u32[]{:S(2)}) async-start(bf16[32,128,512]{2,1,0:T(8,128)(2,1)} %get-tuple-element.18), calls=%async_computation.3 | async-start | bytes 8388608 | tf_op jit(solution)/shard_map/all_to_all | solution.py:58
  180.2 6.6 %convert_element_type.42 = f32[32,128,512]{2,1,0:T(8,128)} convert(bf16[32,128,512]{2,1,0:T(8,128)(2,1)} %all_to_all.15) | non-fusion elementwise | flops 2097152 | bytes 12582912 | tf_op jit(solution)/shard_map/convert_element_type | solution.py:50
  186.8 4.0 %gather_fusion.1 = f32[6,128,512]{2,1,0:T(8,128)S(1)} fusion(f32[32,128,512]{2,1,0:T(8,128)} %convert_element_type.42, s32[1024]{0:T(1024)S(1)} %pad_clamp_fusion), kind=kCustom, calls=%fused_computation.1 | custom fusion | bytes 3145752 | tf_op jit(solution)/shard_map/gather | solution.py:41
  190.8 6.6 %convert_element_type.44 = f32[32,128,512]{2,1,0:T(8,128)} convert(bf16[32,128,512]{2,1,0:T(8,128)(2,1)} %all_to_all.16) | non-fusion elementwise | flops 2097152 | bytes 12582912 | tf_op jit(solution)/shard_map/convert_element_type | solution.py:57
  197.4 4.0 %gather_fusion.3 = f32[6,128,512]{2,1,0:T(8,128)S(1)} fusion(f32[32,128,512]{2,1,0:T(8,128)} %convert_element_type.44, s32[1024]{0:T(1024)S(1)} %pad_clamp_fusion), kind=kCustom, calls=%fused_computation.3 | custom fusion | bytes 3145752 | tf_op jit(solution)/shard_map/gather | solution.py:41
  201.4 30.8 %all-to-all-done.2 = bf16[32,128,512]{2,1,0:T(8,128)(2,1)} async-done(((bf16[32,128,512]{2,1,0:T(8,128)(2,1)}), bf16[32,128,512]{2,1,0:T(8,128)(2,1)}, u32[]{:S(2)}, u32[]{:S(2)}) %all-to-all-start.2) | async-done | bytes 4194336 | tf_op jit(solution)/shard_map/all_to_all | solution.py:58
  232.2 6.6 %convert_element_type.46 = f32[32,128,512]{2,1,0:T(8,128)} convert(bf16[32,128,512]{2,1,0:T(8,128)(2,1)} %all-to-all-done.2) | non-fusion elementwise | flops 2097152 | bytes 12582912 | tf_op jit(solution)/shard_map/convert_element_type | solution.py:64
  238.8 5.2 %gather_fusion.5 = f32[6,128,512]{2,1,0:T(8,128)} fusion(f32[32,128,512]{2,1,0:T(8,128)} %convert_element_type.46, s32[1024]{0:T(1024)S(1)} %pad_clamp_fusion), kind=kCustom, calls=%fused_computation.5 | custom fusion | bytes 3145752 | tf_op jit(solution)/shard_map/gather | solution.py:41
  243.9 4.1 %broadcast_select_fusion = (f32[6,128,512]{2,1,0:T(8,128)}, f32[6,128,512]{2,1,0:T(8,128)}, bf16[6,128,512]{2,1,0:T(8,128)(2,1)}, f32[6,128,512]{2,1,0:T(8,128)}) fusion(f32[6,128,512]{2,1,0:T(8,128)} %gather_fusion.5, pred[6]{0:T(512)(128)(4,1)S(1)} %broadcast_compare_fusion.1, f32[6,128,512]{2,1,0:T(8,128)S(1)} %gather_fusion.3, ...), kind=kLoop, calls=%fused_computation.14 | loop fusion | flops 1572864 | bytes 10223622 | tf_op jit(solution)/shard_map/jit(_where)/select_n | solution.py:41
  248.1 39.1 %all-gather.2.cloned.1.call-done = bf16[6,128,2048]{2,1,0:T(8,128)(2,1)} async-done(((bf16[6,128,512]{2,1,0:T(8,128)(2,1)}), bf16[6,128,2048]{2,1,0:T(8,128)(2,1)}) %all-gather.2.cloned.1.call-update) | async-done | bytes 3145744 | tf_op jit(solution)/shard_map/all_gather | solution.py:69
  287.1 4.0 %copy.11 = bf16[6,128,2048]{2,1,0:T(8,128)(2,1)} copy(bf16[6,128,2048]{2,1,0:T(8,128)(2,1)} %all-gather.2.cloned.1.call-done) | data formatting | bytes 6291456
  (15 shorter events, 1.3 us)
Async XLA Ops:
  7.2 36.4 %reduce-scatter.2.cloned.1.call-start = ((), (), s32[]{:S(2)}) async-start(), calls=%async_computation.4 | async-start | bytes 2621440 | tf_op jit(solution)/shard_map/reduce_scatter | solution.py:43
  175.2 4.8 %copy-start = (s32[104]{0:T(128)S(1)}, s32[104]{0:T(128)}, u32[]{:S(2)}) copy-start(s32[104]{0:T(128)} %param.10) | copy-start | bytes 1252
  175.2 57.0 %all-to-all-start.2 = ((bf16[32,128,512]{2,1,0:T(8,128)(2,1)}), bf16[32,128,512]{2,1,0:T(8,128)(2,1)}, u32[]{:S(2)}, u32[]{:S(2)}) async-start(bf16[32,128,512]{2,1,0:T(8,128)(2,1)} %get-tuple-element.18), calls=%async_computation.3 | async-start | bytes 8388608 | tf_op jit(solution)/shard_map/all_to_all | solution.py:58
  180.0 107.2 %all-gather.2.cloned.1.call-start = ((), (), s32[]{:S(2)}) async-start(), calls=%async_computation.5 | async-start | bytes 3932160 | tf_op jit(solution)/shard_map/all_gather | solution.py:69
Sparse Core Ops, SparseCore 0:
  10.4 33.1 reduce-scatter.1
  248.2 38.9 all-gather.1
where the time goes:
time: 299 us; the launch traced here: 298 us
  blocking collectives  112 us (37%)
  waiting for transfers between devices  102 us (34%)
  other arithmetic  39 us (13%)
  local copies, waits for them, and re-layouts  25.5 us (9%)
  between operations  14.1 us (5%)
  starting transfers between devices  4.85 us (2%)
    all_to_all x1, blocking collectives, shards(): lax.all_to_all(to_peers(weight).astype(jnp.bfloat16), 'expert', split_axi...  58 us
    all_to_all x1, blocking collectives, shards(): lax.all_to_all(to_peers(moment_one).astype(jnp.bfloat16), 'expert', split...  54.5 us
    all_gather x1, waiting for transfers between devices, shards(): lax.all_gather(new_master.astype(jnp.bfloat16), 'dp', axis=2, tiled=True)  39.1 us
    reduce_scatter x1, waiting for transfers between devices, shards(): lax.psum_scatter(grad_parts[0], 'dp', scatter_dimension=2, tiled=True)  31.5 us
    all_to_all x1, waiting for transfers between devices, shards(): lax.all_to_all(to_peers(moment_two).astype(jnp.bfloat16), 'expert', split...  30.8 us
    convert_element_type x3, other arithmetic, shards(): results = (lax.all_to_all(to_peers(weight).astype(jnp.bfloat16), 'expert'...  19.7 us
    gather x3, local copies, waits for them, and re-layouts, from_peers(): return jnp.where(recv_has[:, None, None], values[recv_source], 0.0)  13.2 us
    gather x3, local copies, waits for them, and re-layouts, to_peers(): return jnp.where(send_has[:, None, None], values[send_slot], 0.0)  8.3 us
  transfers between devices with their start and end apart: 3, of which 3 were waited for; matrix products, arithmetic and copies ran while one was open for 9% of the time, Pallas kernels for 0%

commit v1 on v0

v1 whole, which is shorter than its diff:
```python
import jax
import jax.numpy as jnp
from jax import lax
from jax.experimental import pallas as pl
from jax.experimental.pallas import tpu as pltpu
from jax.sharding import PartitionSpec as P

BF16 = jnp.bfloat16
F32 = jnp.float32
PEERS = 32
OLD = 4
NEW = 6
PR, PC = 8, 256
STEPS = 4


def route_kernel(old_ref, new_ref, table_ref, old_count, new_count):
    def clear_counts(i, _):
        old_count[i] = 0
        new_count[i] = 0
        return 0

    def clear_table(i, _):
        table_ref[i] = -1
        return 0

    lax.fori_loop(0, PEERS, clear_counts, 0)
    lax.fori_loop(0, PEERS * NEW, clear_table, 0)

    def place(t, _):
        o = old_ref[t]
        n = new_ref[t]
        a = old_count[o]
        b = new_count[n]
        table_ref[n * NEW + b] = o * OLD + a
        old_count[o] = a + 1
        new_count[n] = b + 1
        return 0

    lax.fori_loop(0, old_ref.shape[0], place, 0)


def route(old_owner, new_owner):
    smem = pl.BlockSpec(memory_space=pltpu.SMEM)
    return pl.pallas_call(
        route_kernel,
        out_shape=jax.ShapeDtypeStruct((PEERS * NEW,), jnp.int32),
        in_specs=[smem, smem],
        out_specs=smem,
        scratch_shapes=[pltpu.SMEM((PEERS,), jnp.int32), pltpu.SMEM((PEERS,), jnp.int32)],
        name="route",
    )(old_owner, new_owner)


def pack_state_kernel(m1_ref, m2_ref, w_ref, out_ref):
    for k, ref in enumerate((m1_ref, m2_ref, w_ref)):
        for r in range(ref.shape[1] // PR):
            for c in range(2):
                piece = ref[:, r * PR : (r + 1) * PR, c * PC : (c + 1) * PC]
                out_ref[2 * r + c, :, k] = piece.astype(BF16)


def pack_state(m1, m2, w):
    rows = 128 // STEPS
    block = pl.BlockSpec((OLD, rows, 512), lambda i: (0, i, 0))
    return pl.pallas_call(
        pack_state_kernel,
        grid=(STEPS,),
        out_shape=jax.ShapeDtypeStruct((PEERS, OLD, 3, PR, PC), BF16),
        in_specs=[block] * 3,
        out_specs=pl.BlockSpec((PEERS // STEPS, OLD, 3, PR, PC), lambda i: (i, 0, 0, 0, 0)),
        name="pack_state",
    )(m1, m2, w)


def pack_grad_kernel(g_ref, out_ref):
    for r in range(g_ref.shape[1] // PR):
        for c in range(2):
            out_ref[2 * r + c] = g_ref[:, r * PR : (r + 1) * PR, c * PC : (c + 1) * PC]


def pack_grad(g):
    return pl.pallas_call(
        pack_grad_kernel,
        out_shape=jax.ShapeDtypeStruct((PEERS, OLD, PR, PC), BF16),
        name="pack_grad",
    )(g)


def adam_step(gradient, moment_one, moment_two, weight):
    moment_one = 0.9 * moment_one + 0.1 * gradient
    moment_two = 0.95 * moment_two + 0.05 * gradient * gradient
    update = moment_one / (1.0 - 0.9**50) / (jnp.sqrt(moment_two / (1.0 - 0.95**50)) + 1e-08)
    weight = weight - 0.05 * (update + 0.1 * weight)
    return (weight, moment_one, moment_two)


def update_kernel(table_ref, state_ref, grad_ref, weight_ref, moments_ref):
    def owner(d, _):
        for s in range(NEW):
            row = table_ref[d * NEW + s]
            has = row >= 0
            row = jnp.maximum(row, 0)
            gradient = grad_ref[row].astype(F32)
            m1 = state_ref[row, 0].astype(F32)
            m2 = state_ref[row, 1].astype(F32)
            w = state_ref[row, 2].astype(F32)
            w, m1, m2 = adam_step(gradient, m1, m2, w)
            weight_ref[d, s] = jnp.where(has, w, 0.0).astype(BF16)
            moments_ref[d, s, 0] = jnp.where(has, m1, 0.0).astype(BF16)
            moments_ref[d, s, 1] = jnp.where(has, m2, 0.0).astype(BF16)
        return 0

    lax.fori_loop(0, PEERS, owner, 0)


def update(table, state, grad):
    vmem = pl.BlockSpec(memory_space=pltpu.VMEM)
    return pl.pallas_call(
        update_kernel,
        out_shape=(
            jax.ShapeDtypeStruct((PEERS, NEW, PR, PC), BF16),
            jax.ShapeDtypeStruct((PEERS, NEW, 2, PR, PC), BF16),
        ),
        in_specs=[pl.BlockSpec(memory_space=pltpu.SMEM), vmem, vmem],
        out_specs=(vmem, vmem),
        compiler_params=pltpu.CompilerParams(vmem_limit_bytes=32 * 1024 * 1024),
        name="update",
    )(table, state, grad)


def unpack_state_kernel(w_ref, m_ref, w_out, m1_out, m2_out):
    for r in range(w_out.shape[1] // PR):
        for c in range(2):
            at = (slice(None), slice(r * PR, (r + 1) * PR), slice(c * PC, (c + 1) * PC))
            w_out[at] = w_ref[2 * r + c].astype(F32)
            m1_out[at] = m_ref[2 * r + c, :, 0].astype(F32)
            m2_out[at] = m_ref[2 * r + c, :, 1].astype(F32)


def unpack_state(w, m):
    rows = 128 // STEPS
    out = jax.ShapeDtypeStruct((NEW, 128, 512), F32)
    return pl.pallas_call(
        unpack_state_kernel,
        grid=(STEPS,),
        out_shape=(out, out, out),
        in_specs=[
            pl.BlockSpec((PEERS // STEPS, NEW, PR, PC), lambda i: (i, 0, 0, 0)),
            pl.BlockSpec((PEERS // STEPS, NEW, 2, PR, PC), lambda i: (i, 0, 0, 0, 0)),
        ],
        out_specs=[pl.BlockSpec((NEW, rows, 512), lambda i: (0, i, 0))] * 3,
        name="unpack_state",
    )(w, m)


def unpack_params_kernel(w_ref, out_ref):
    for z in range(w_ref.shape[0]):
        for r in range(out_ref.shape[1] // PR):
            for c in range(2):
                lanes = slice(z * 512 + c * PC, z * 512 + (c + 1) * PC)
                out_ref[:, r * PR : (r + 1) * PR, lanes] = w_ref[z, 2 * r + c]


def unpack_params(w):
    rows = 128 // STEPS
    n = w.shape[0]
    return pl.pallas_call(
        unpack_params_kernel,
        grid=(STEPS,),
        out_shape=jax.ShapeDtypeStruct((NEW, 128, 512 * n), BF16),
        in_specs=[pl.BlockSpec((n, PEERS // STEPS, NEW, PR, PC), lambda i: (0, i, 0, 0, 0))],
        out_specs=pl.BlockSpec((NEW, rows, 512 * n), lambda i: (0, i, 0)),
        name="unpack_params",
    )(w)


def exchange(values):
    return lax.all_to_all(values, "expert", split_axis=0, concat_axis=0, tiled=True)


def shards(grad_parts, first_moment, second_moment, master_weight, old_owner, new_owner):
    summed = lax.psum_scatter(grad_parts[0], "dp", scatter_dimension=2, tiled=True)
    table = route(old_owner, new_owner)
    state = exchange(pack_state(first_moment, second_moment, master_weight))
    grad = exchange(pack_grad(summed))
    weight, moments = update(
        table,
        state.reshape(PEERS * OLD, 3, PR, PC),
        grad.reshape(PEERS * OLD, PR, PC),
    )
    weight = exchange(weight)
    weight, moments = lax.optimization_barrier((weight, moments))
    moments = exchange(moments)
    gathered = lax.all_gather(weight, "dp", axis=0, tiled=False)
    new_master, new_first, new_second = unpack_state(weight, moments)
    new_params = unpack_params(gathered)
    return (new_master, new_first, new_second, new_params)


def solution(mesh):
    placed = (
        P("dp", "expert", None, None),
        P("expert", None, "dp"),
        P("expert", None, "dp"),
        P("expert", None, "dp"),
        P(),
        P(),
    )
    return jax.shard_map(
        shards,
        mesh=mesh,
        in_specs=placed,
        out_specs=(
            P("expert", None, "dp"),
            P("expert", None, "dp"),
            P("expert", None, "dp"),
            P("expert", None, None),
        ),
        check_vma=False,
    )
```

time: 299 us -> 135 us (0.45)
  blocking collectives: 112 us -> 44.5 us
  waiting for transfers between devices: 102 us -> 36.7 us
  other arithmetic: 39 us -> 0 us
  local copies, waits for them, and re-layouts: 25.5 us -> 1.82 us
  Pallas kernels: 0 us -> 20.8 us
  starting transfers between devices: 4.85 us -> 16.1 us
    all_to_all x2, blocking collectives: 112 us -> 44.5 us  [exchange(): lax.all_to_all(values, 'expert', split_axis=0, concat_axis=0, tiled=True)]
    all_gather x1, waiting for transfers between devices: 39.1 us -> 4.77 us  [shards(): gathered = lax.all_gather(weight, 'dp', axis=0, tiled=False)]
    convert_element_type x6 -> x0, other arithmetic: 29 us -> none  [the longest x3 19.7 us: shards(): results = (lax.all_to_all(to_peers(weight).astype(jnp.bfloat16), 'expert'...]
    all_to_all x1 -> x2, waiting for transfers between devices: 30.8 us -> 7.97 us  [exchange(): lax.all_to_all(values, 'expert', split_axis=0, concat_axis=0, tiled=True)]
    gather x6 -> x0, local copies, waits for them, and re-layouts: 21.5 us -> none  [the longest x3 13.2 us: from_peers(): return jnp.where(recv_has[:, None, None], values[recv_source], 0.0)]
    pallas_call x0 -> x6, Pallas kernels: none -> 20.8 us  [the longest x1 4.44 us: unpack_state(): pl.pallas_call(unpack_state_kernel, grid=(STEPS,), out_shape=(out, out, o...]
    all_to_all x1 -> x2, starting transfers between devices: 4.77 us -> 16.1 us  [exchange(): lax.all_to_all(values, 'expert', split_axis=0, concat_axis=0, tiled=True)]
    reduce_scatter x1, waiting for transfers between devices: 31.5 us -> 23.2 us  [shards(): lax.psum_scatter(grad_parts[0], 'dp', scatter_dimension=2, tiled=True)]
  transfers between devices with their start and end apart: 3 -> 4, of which waited for: 3 -> 3; matrix products, arithmetic and copies ran while one was open for 9% -> 0% of each run, Pallas kernels for 0% -> 10%
where the time goes in v1:
time: 135 us; the launch traced here: 134 us
  blocking collectives  44.5 us (33%)
  waiting for transfers between devices  36.7 us (27%)
  Pallas kernels  20.8 us (15%)
  starting transfers between devices  16.1 us (12%)
  between operations  14.1 us (10%)
  local copies, waits for them, and re-layouts  1.82 us (1%)
    all_to_all x2, blocking collectives, exchange(): lax.all_to_all(values, 'expert', split_axis=0, concat_axis=0, tiled=True)  44.5 us
    reduce_scatter x1, waiting for transfers between devices, shards(): lax.psum_scatter(grad_parts[0], 'dp', scatter_dimension=2, tiled=True)  23.2 us
    all_to_all x2, starting transfers between devices, exchange(): lax.all_to_all(values, 'expert', split_axis=0, concat_axis=0, tiled=True)  16.1 us
    all_to_all x2, waiting for transfers between devices, exchange(): lax.all_to_all(values, 'expert', split_axis=0, concat_axis=0, tiled=True)  7.97 us
    all_gather x1, waiting for transfers between devices, shards(): gathered = lax.all_gather(weight, 'dp', axis=0, tiled=False)  4.77 us
    pallas_call x1, Pallas kernels, unpack_state(): pl.pallas_call(unpack_state_kernel, grid=(STEPS,), out_shape=(out, out, o...  4.44 us
    pallas_call x1, Pallas kernels, unpack_params(): pl.pallas_call(unpack_params_kernel, grid=(STEPS,), out_shape=jax.ShapeDt...  4.22 us
    pallas_call x1, Pallas kernels, pack_state(): pl.pallas_call(pack_state_kernel, grid=(STEPS,), out_shape=jax.ShapeDtype...  3.86 us
  transfers between devices with their start and end apart: 4, of which 3 were waited for; matrix products, arithmetic and copies ran while one was open for 0% of the time, Pallas kernels for 10%

profile of v1, /device:TPU:1, one launch (start us, length us, event | category | flops | bytes accessed | tf_op | source)
XLA Modules:
  0.0 134.0 jit_solution(3834927804608635909)
XLA Ops:
  7.2 0.0 reduce-scatter.2.cloned.1.call-start
  7.2 0.7 reduce-scatter.2.cloned.1.call-update
  7.9 3.9 %pack_state.1 = bf16[32,4,3,8,256]{4,3,2,1,0:T(8,128)(2,1)} custom-call(f32[4,128,512]{2,1,0:T(8,128)} %m1_ref.1, f32[4,128,512]{2,1,0:T(8,128)} %m2_ref.1, f32[4,128,512]{2,1,0:T(8,128)} %w_ref.1), custom_call_target="tpu_custom_call" | custom-call | tf_op jit(solution)/shard_map/pack_state/pallas_call | solution.py:66
  11.8 8.6 %all-to-all-start = ((bf16[32,4,3,8,256]{4,3,2,1,0:T(8,128)(2,1)}), bf16[32,4,3,8,256]{4,3,2,1,0:T(8,128)(2,1)S(1)}, u32[]{:S(2)}, u32[]{:S(2)}) async-start(bf16[32,4,3,8,256]{4,3,2,1,0:T(8,128)(2,1)} %pack_state.1), calls=%async_computation | async-start | bytes 3145728 | tf_op jit(solution)/shard_map/all_to_all | solution.py:179
  20.4 23.2 %reduce-scatter.2.cloned.1.call-done.g_ref = bf16[4,128,512]{2,1,0:T(8,128)(2,1)} async-done(((bf16[4,128,2048]{2,1,0:T(8,128)(2,1)}), bf16[4,128,512]{2,1,0:T(8,128)(2,1)}) %reduce-scatter.2.cloned.1.call-update) | async-done | bytes 524304 | tf_op jit(solution)/shard_map/reduce_scatter | solution.py:183
  43.6 1.9 %pack_grad.1 = bf16[32,4,8,256]{3,2,1,0:T(8,128)(2,1)} custom-call(bf16[4,128,512]{2,1,0:T(8,128)(2,1)} %reduce-scatter.2.cloned.1.call-done.g_ref), custom_call_target="tpu_custom_call" | custom-call | tf_op jit(solution)/shard_map/pack_grad/pallas_call | solution.py:83
  45.5 0.0 all-to-all-done
  45.5 7.5 %all-to-all-start.1 = ((bf16[32,4,8,256]{3,2,1,0:T(8,128)(2,1)}), bf16[32,4,8,256]{3,2,1,0:T(8,128)(2,1)S(1)}, u32[]{:S(2)}, u32[]{:S(2)}) async-start(bf16[32,4,8,256]{3,2,1,0:T(8,128)(2,1)} %pack_grad.1), calls=%async_computation.2 | async-start | bytes 1048576 | tf_op jit(solution)/shard_map/all_to_all | solution.py:179
  52.9 0.0 all-gather.3.cloned.1.call-start
  53.0 3.6 %route.1.table_ref = s32[192]{0:T(256)} custom-call(s32[104]{0:T(128)} %old_ref.1, s32[104]{0:T(128)} %new_ref.1), custom_call_target="tpu_custom_call" | custom-call | tf_op jit(solution)/shard_map/route/pallas_call | solution.py:45
  56.6 8.0 %all-to-all-done.1 = bf16[32,4,8,256]{3,2,1,0:T(8,128)(2,1)S(1)} async-done(((bf16[32,4,8,256]{3,2,1,0:T(8,128)(2,1)}), bf16[32,4,8,256]{3,2,1,0:T(8,128)(2,1)S(1)}, u32[]{:S(2)}, u32[]{:S(2)}) %all-to-all-start.1) | async-done | bytes 524320 | tf_op jit(solution)/shard_map/all_to_all | solution.py:179
  64.6 0.0 copy-start.2
  64.6 0.7 copy-done.2
  65.2 2.8 %update.1 = (bf16[32,6,8,256]{3,2,1,0:T(8,128)(2,1)S(1)}, bf16[32,6,2,8,256]{4,3,2,1,0:T(8,128)(2,1)S(1)}) custom-call(s32[192]{0:T(256)S(1)} %copy-done.2, bf16[128,3,8,256]{3,2,1,0:T(8,128)(2,1)S(1)} %bitcast.4, bf16[128,8,256]{2,1,0:T(8,128)(2,1)S(1)} %bitcast.5), custom_call_target="tpu_custom_call" | custom-call | tf_op jit(solution)/shard_map/update/pallas_call | solution.py:119
  68.0 0.0 copy-start
  68.1 1.1 copy-done
  69.2 0.0 copy-start.1
  69.2 17.9 %all_to_all.20.w_ref = bf16[32,6,8,256]{3,2,1,0:T(8,128)(2,1)} all-to-all(bf16[32,6,8,256]{3,2,1,0:T(8,128)(2,1)S(1)} %get-tuple-element.11), channel_id=1, replica_groups=mesh['dp'=4,'expert'=32] {'expert'}, dimensions={0} | all-to-all | bytes 1572864 | tf_op jit(solution)/shard_map/all_to_all | solution.py:179
  87.1 0.0 all-gather.3.cloned.1.call-update
  87.1 0.0 copy-done.1
  87.1 26.6 %all_to_all.21.m_ref = bf16[32,6,2,8,256]{4,3,2,1,0:T(8,128)(2,1)} all-to-all(bf16[32,6,2,8,256]{4,3,2,1,0:T(8,128)(2,1)S(1)} %copy-done.1), channel_id=1, replica_groups=mesh['dp'=4,'expert'=32] {'expert'}, dimensions={0} | all-to-all | bytes 3145728 | tf_op jit(solution)/shard_map/all_to_all | solution.py:179
  113.7 4.4 %unpack_state.1 = (f32[6,128,512]{2,1,0:T(8,128)}, f32[6,128,512]{2,1,0:T(8,128)}, f32[6,128,512]{2,1,0:T(8,128)}) custom-call(bf16[32,6,8,256]{3,2,1,0:T(8,128)(2,1)} %all_to_all.20.w_ref, bf16[32,6,2,8,256]{4,3,2,1,0:T(8,128)(2,1)} %all_to_all.21.m_ref), custom_call_target="tpu_custom_call" | custom-call | tf_op jit(solution)/shard_map/unpack_state/pallas_call | solution.py:144
  118.1 4.8 %all-gather.3.cloned.1.call-done = bf16[128,6,8,256]{3,2,1,0:T(8,128)(2,1)} async-done(((bf16[32,6,8,256]{3,2,1,0:T(8,128)(2,1)}), bf16[128,6,8,256]{3,2,1,0:T(8,128)(2,1)}) %all-gather.3.cloned.1.call-update) | async-done | bytes 3145744 | tf_op jit(solution)/shard_map/all_gather | solution.py:195
  122.9 4.2 %unpack_params.1 = bf16[6,128,2048]{2,1,0:T(8,128)(2,1)} custom-call(bf16[4,32,6,8,256]{4,3,2,1,0:T(8,128)(2,1)} %bitcast.6), custom_call_target="tpu_custom_call" | custom-call | tf_op jit(solution)/shard_map/unpack_params/pallas_call | solution.py:168
Async XLA Ops:
  7.2 36.4 %reduce-scatter.2.cloned.1.call-start = ((), (), s32[]{:S(2)}) async-start(), calls=%async_computation.5 | async-start | bytes 2621440 | tf_op jit(solution)/shard_map/reduce_scatter | solution.py:183
  11.8 33.7 %all-to-all-start = ((bf16[32,4,3,8,256]{4,3,2,1,0:T(8,128)(2,1)}), bf16[32,4,3,8,256]{4,3,2,1,0:T(8,128)(2,1)S(1)}, u32[]{:S(2)}, u32[]{:S(2)}) async-start(bf16[32,4,3,8,256]{4,3,2,1,0:T(8,128)(2,1)} %pack_state.1), calls=%async_computation | async-start | bytes 3145728 | tf_op jit(solution)/shard_map/all_to_all | solution.py:179
  45.5 19.1 %all-to-all-start.1 = ((bf16[32,4,8,256]{3,2,1,0:T(8,128)(2,1)}), bf16[32,4,8,256]{3,2,1,0:T(8,128)(2,1)S(1)}, u32[]{:S(2)}, u32[]{:S(2)}) async-start(bf16[32,4,8,256]{3,2,1,0:T(8,128)(2,1)} %pack_grad.1), calls=%async_computation.2 | async-start | bytes 1048576 | tf_op jit(solution)/shard_map/all_to_all | solution.py:179
  52.9 70.0 %all-gather.3.cloned.1.call-start = ((), (), s32[]{:S(2)}) async-start(), calls=%async_computation.6 | async-start | bytes 3932160 | tf_op jit(solution)/shard_map/all_gather | solution.py:195
  64.6 0.7 copy-start.2
  68.0 1.1 copy-start
  69.2 17.9 %copy-start.1 = (bf16[32,6,2,8,256]{4,3,2,1,0:T(8,128)(2,1)S(1)}, bf16[32,6,2,8,256]{4,3,2,1,0:T(8,128)(2,1)}, u32[]{:S(2)}) copy-start(bf16[32,6,2,8,256]{4,3,2,1,0:T(8,128)(2,1)} %copy-done) | copy-start | bytes 4718596
Sparse Core Ops, SparseCore 0:
  10.4 33.1 reduce-scatter.1
  87.2 35.6 all-gather.2

commit v2 on v1

--- a/solution.py
+++ b/solution.py
@@ -1,3 +1,5 @@
+import functools
+
 import jax
 import jax.numpy as jnp
 from jax import lax
@@ -12,6 +14,7 @@
 NEW = 6
 PR, PC = 8, 256
 STEPS = 4
+VMEM = pl.BlockSpec(memory_space=pltpu.VMEM)
 
 
 def route_kernel(old_ref, new_ref, table_ref, old_count, new_count):
@@ -73,18 +76,57 @@
     )(m1, m2, w)
 
 
-def pack_grad_kernel(g_ref, out_ref):
-    for r in range(g_ref.shape[1] // PR):
-        for c in range(2):
-            out_ref[2 * r + c] = g_ref[:, r * PR : (r + 1) * PR, c * PC : (c + 1) * PC]
-
-
-def pack_grad(g):
-    return pl.pallas_call(
-        pack_grad_kernel,
+def pack_halves_kernel(ahead, me_ref, *refs):
+    del me_ref
+    for g_ref, a_ref, b_ref in zip(refs[:ahead], refs[ahead::2], refs[ahead + 1 :: 2]):
+        for r in range(g_ref.shape[2] // PR):
+            for c in range(2):
+                rows, lanes = slice(r * PR, (r + 1) * PR), slice(c * PC, (c + 1) * PC)
+                a_ref[2 * r + c] = g_ref[:, 0, rows, lanes]
+                b_ref[2 * r + c] = g_ref[:, 1, rows, lanes]
+
+
+def shard_block(steps, ahead):
+    return pl.BlockSpec((OLD, 2, 64 // steps, 512), lambda i, me: (0, 0, i, (me[0] + ahead) % 4))
+
+
+def half_block(steps, slots):
+    return pl.BlockSpec((PEERS // 2 // steps, slots, PR, PC), lambda i, me: (i, 0, 0, 0))
+
+
+def pack_halves(me, g, aheads, name):
+    steps = 2
+    n = len(aheads)
+    half = jax.ShapeDtypeStruct((PEERS // 2, OLD, PR, PC), BF16)
+    return pl.pallas_call(
+        functools.partial(pack_halves_kernel, n),
+        grid_spec=pltpu.PrefetchScalarGridSpec(
+            num_scalar_prefetch=1,
+            grid=(steps,),
+            in_specs=[shard_block(steps, k) for k in aheads],
+            out_specs=[half_block(steps, OLD)] * (2 * n),
+        ),
+        out_shape=[half] * (2 * n),
+        name=name,
+    )(me, *([g] * n))
+
+
+def sum_grad_kernel(own_a, own_b, ua, ub, da, db, out_ref):
+    half = PEERS // 2
+    for h, refs in enumerate(((own_a, ua, da), (own_b, ub, db))):
+        for j in range(half):
+            own, up, down = (ref[j].astype(F32) for ref in refs)
+            out_ref[h * half + j] = (own + up + down).astype(BF16)
+
+
+def sum_grad(*halves):
+    return pl.pallas_call(
+        sum_grad_kernel,
         out_shape=jax.ShapeDtypeStruct((PEERS, OLD, PR, PC), BF16),
-        name="pack_grad",
-    )(g)
+        in_specs=[VMEM] * 6,
+        out_specs=VMEM,
+        name="sum_grad",
+    )(*halves)
 
 
 def adam_step(gradient, moment_one, moment_two, weight):
@@ -129,50 +171,98 @@
     )(table, state, grad)
 
 
-def unpack_state_kernel(w_ref, m_ref, w_out, m1_out, m2_out):
-    for r in range(w_out.shape[1] // PR):
+def unpack_own_kernel(me_ref, w_ref, w_out, out_ref):
+    del me_ref
+    n = w_out.shape[1] // PR
+    for r in range(n):
         for c in range(2):
-            at = (slice(None), slice(r * PR, (r + 1) * PR), slice(c * PC, (c + 1) * PC))
-            w_out[at] = w_ref[2 * r + c].astype(F32)
-            m1_out[at] = m_ref[2 * r + c, :, 0].astype(F32)
-            m2_out[at] = m_ref[2 * r + c, :, 1].astype(F32)
-
-
-def unpack_state(w, m):
+            rows, lanes = slice(r * PR, (r + 1) * PR), slice(c * PC, (c + 1) * PC)
+            piece = w_ref[2 * r + c]
+            w_out[:, rows, lanes] = piece.astype(F32)
+            out_ref[:, rows, lanes] = piece
+
+
+def unpack_own(me, w):
+    rows = 128 // STEPS
+    return pl.pallas_call(
+        unpack_own_kernel,
+        grid_spec=pltpu.PrefetchScalarGridSpec(
+            num_scalar_prefetch=1,
+            grid=(STEPS,),
+            in_specs=[pl.BlockSpec((PEERS // STEPS, NEW, PR, PC), lambda i, me: (i, 0, 0, 0))],
+            out_specs=[
+                pl.BlockSpec((NEW, rows, 512), lambda i, me: (0, i, 0)),
+                pl.BlockSpec((NEW, rows, 512), lambda i, me: (0, i, me[0])),
+            ],
+        ),
+        out_shape=(
+            jax.ShapeDtypeStruct((NEW, 128, 512), F32),
+            jax.ShapeDtypeStruct((NEW, 128, 2048), BF16),
+        ),
+        name="unpack_own",
+    )(me, w)
+
+
+def unpack_moments_kernel(m_ref, m1_out, m2_out):
+    for r in range(m1_out.shape[1] // PR):
+        for c in range(2):
+            rows, lanes = slice(r * PR, (r + 1) * PR), slice(c * PC, (c + 1) * PC)
+            m1_out[:, rows, lanes] = m_ref[2 * r + c, :, 0].astype(F32)
+            m2_out[:, rows, lanes] = m_ref[2 * r + c, :, 1].astype(F32)
+
+
+def unpack_moments(m):
     rows = 128 // STEPS
     out = jax.ShapeDtypeStruct((NEW, 128, 512), F32)
     return pl.pallas_call(
-        unpack_state_kernel,
+        unpack_moments_kernel,
         grid=(STEPS,),
-        out_shape=(out, out, out),
-        in_specs=[
-            pl.BlockSpec((PEERS // STEPS, NEW, PR, PC), lambda i: (i, 0, 0, 0)),
-            pl.BlockSpec((PEERS // STEPS, NEW, 2, PR, PC), lambda i: (i, 0, 0, 0, 0)),
-        ],
-        out_specs=[pl.BlockSpec((NEW, rows, 512), lambda i: (0, i, 0))] * 3,
-        name="unpack_state",
-    )(w, m)
-
-
-def unpack_params_kernel(w_ref, out_ref):
-    for z in range(w_ref.shape[0]):
-        for r in range(out_ref.shape[1] // PR):
-            for c in range(2):
-                lanes = slice(z * 512 + c * PC, z * 512 + (c + 1) * PC)
-                out_ref[:, r * PR : (r + 1) * PR, lanes] = w_ref[z, 2 * r + c]
-
-
-def unpack_params(w):
-    rows = 128 // STEPS
-    n = w.shape[0]
-    return pl.pallas_call(
-        unpack_params_kernel,
-        grid=(STEPS,),
-        out_shape=jax.ShapeDtypeStruct((NEW, 128, 512 * n), BF16),
-        in_specs=[pl.BlockSpec((n, PEERS // STEPS, NEW, PR, PC), lambda i: (0, i, 0, 0, 0))],
-        out_specs=pl.BlockSpec((NEW, rows, 512 * n), lambda i: (0, i, 0)),
-        name="unpack_params",
-    )(w)
+        out_shape=(out, out),
+        in_specs=[pl.BlockSpec((PEERS // STEPS, NEW, 2, PR, PC), lambda i: (i, 0, 0, 0, 0))],
+        out_specs=[pl.BlockSpec((NEW, rows, 512), lambda i: (0, i, 0))] * 2,
+        name="unpack_moments",
+    )(m)
+
+
+def unpack_block_kernel(me_ref, a_ref, b_ref, old_ref, out_ref):
+    del me_ref, old_ref
+    for r in range(out_ref.shape[2] // PR):
+        for c in range(2):
+            rows, lanes = slice(r * PR, (r + 1) * PR), slice(c * PC, (c + 1) * PC)
+            out_ref[:, 0, rows, lanes] = a_ref[2 * r + c]
+            out_ref[:, 1, rows, lanes] = b_ref[2 * r + c]
+
+
+def unpack_block(me, a, b, params, ahead):
+    steps = 2
+    return pl.pallas_call(
+        unpack_block_kernel,
+        grid_spec=pltpu.PrefetchScalarGridSpec(
+            num_scalar_prefetch=1,
+            grid=(steps,),
+            in_specs=[half_block(steps, NEW)] * 2 + [pl.BlockSpec(memory_space=pl.ANY)],
+            out_specs=pl.BlockSpec((NEW, 2, 64 // steps, 512), lambda i, me: (0, 0, i, (me[0] + ahead) % 4)),
+        ),
+        out_shape=jax.ShapeDtypeStruct((NEW, 2, 64, 2048), BF16),
+        input_output_aliases={3: 0},
+        name="unpack_block",
+    )(me, a, b, params)
+
+
+UP = [(i, (i + 1) % 4) for i in range(4)]
+DOWN = [(i, (i - 1) % 4) for i in range(4)]
+
+
+def send_up(x):
+    return lax.ppermute(x, "dp", UP)
+
+
+def send_down(x):
+    return lax.ppermute(x, "dp", DOWN)
+
+
+def add(x, y):
+    return (x.astype(F32) + y.astype(F32)).astype(BF16)
 
 
 def exchange(values):
@@ -180,10 +270,19 @@
 
 
 def shards(grad_parts, first_moment, second_moment, master_weight, old_owner, new_owner):
-    summed = lax.psum_scatter(grad_parts[0], "dp", scatter_dimension=2, tiled=True)
+    me = lax.axis_index("dp").astype(jnp.int32)[None]
+    g = grad_parts[0].reshape(OLD, 2, 64, 2048)
+    far_a, far_b = pack_halves(me, g, (2,), "pack_far")
+    far_up, far_down = send_up(far_a), send_down(far_b)
+    state = pack_state(first_moment, second_moment, master_weight)
+    state, g = lax.optimization_barrier((state, g))
+    state = exchange(state)
+    up_a, up_b, down_a, down_b, own_a, own_b = pack_halves(me, g, (1, 3, 0), "pack_near")
+    ub, da = send_up(up_b), send_down(down_a)
+    ua, db = send_up(add(up_a, far_up)), send_down(add(down_b, far_down))
+    state, ua, ub, da, db = lax.optimization_barrier((state, ua, ub, da, db))
+    grad = exchange(sum_grad(own_a, own_b, ua, ub, da, db))
     table = route(old_owner, new_owner)
-    state = exchange(pack_state(first_moment, second_moment, master_weight))
-    grad = exchange(pack_grad(summed))
     weight, moments = update(
         table,
         state.reshape(PEERS * OLD, 3, PR, PC),
@@ -191,10 +290,18 @@
     )
     weight = exchange(weight)
     weight, moments = lax.optimization_barrier((weight, moments))
+    wa, wb = weight[: PEERS // 2], weight[PEERS // 2 :]
+    ua, da = send_up(wa), send_down(wa)
+    ub, db = send_up(wb), send_down(wb)
+    fa, fb = send_up(ua), send_down(db)
     moments = exchange(moments)
-    gathered = lax.all_gather(weight, "dp", axis=0, tiled=False)
-    new_master, new_first, new_second = unpack_state(weight, moments)
-    new_params = unpack_params(gathered)
+    new_master, params = unpack_own(me, weight)
+    params = params.reshape(NEW, 2, 64, 2048)
+    params = unpack_block(me, ua, ub, params, 3)
+    params = unpack_block(me, da, db, params, 1)
+    new_first, new_second = unpack_moments(moments)
+    fa, fb, new_first = lax.optimization_barrier((fa, fb, new_first))
+    new_params = unpack_block(me, fa, fb, params, 2).reshape(NEW, 128, 2048)
     return (new_master, new_first, new_second, new_params)
 
 

time: 135 us -> 120 us (0.89)
  blocking collectives: 44.5 us -> 17.7 us
  starting transfers between devices: 16.1 us -> 37.7 us
  between operations: 14.1 us -> 0.8 us
  waiting for transfers between devices: 36.7 us -> 24.6 us
  Pallas kernels: 20.8 us -> 30.2 us
  local copies, waits for them, and re-layouts: 1.82 us -> 5.19 us
  other arithmetic: 0 us -> 2.06 us
    all_to_all x2 -> x1, blocking collectives: 44.5 us -> 17.7 us  [exchange(): lax.all_to_all(values, 'expert', split_axis=0, concat_axis=0, tiled=True)]
    reduce_scatter x1 -> x0, waiting for transfers between devices: 23.2 us -> none  [shards(): lax.psum_scatter(grad_parts[0], 'dp', scatter_dimension=2, tiled=True)]
    ppermute x0 -> x12, starting transfers between devices: none -> 17.2 us  [the longest x6 14.6 us: send_down(): return lax.ppermute(x, 'dp', DOWN)]
    ppermute x0 -> x12, waiting for transfers between devices: none -> 16.6 us  [the longest x6 16.6 us: send_up(): return lax.ppermute(x, 'dp', UP)]
    pallas_call x3 -> x8, Pallas kernels: 10.5 us -> 19.9 us  [the longest x3 6.01 us: unpack_block(): pl.pallas_call(unpack_block_kernel, grid_spec=pltpu.PrefetchScalarGridSpe...]
    all_gather x1 -> x0, waiting for transfers between devices: 4.77 us -> none  [shards(): gathered = lax.all_gather(weight, 'dp', axis=0, tiled=False)]
    all_to_all x2 -> x3, starting transfers between devices: 16.1 us -> 20.5 us  [exchange(): lax.all_to_all(values, 'expert', split_axis=0, concat_axis=0, tiled=True)]
    unnamed x6 -> x26, local copies, waits for them, and re-layouts: 1.82 us -> 4.24 us
  transfers between devices with their start and end apart: 4 -> 15, of which waited for: 3 -> 6; matrix products, arithmetic and copies ran while one was open for 0% -> 3% of each run, Pallas kernels for 10% -> 16%
where the time goes in v2:
time: 120 us; the launch traced here: 118 us
  starting transfers between devices  37.7 us (31%)
  Pallas kernels  30.2 us (25%)
  waiting for transfers between devices  24.6 us (20%)
  blocking collectives  17.7 us (15%)
  local copies, waits for them, and re-layouts  5.19 us (4%)
  other arithmetic  2.06 us (2%)
    all_to_all x3, starting transfers between devices, exchange(): lax.all_to_all(values, 'expert', split_axis=0, concat_axis=0, tiled=True)  20.5 us
    all_to_all x1, blocking collectives, exchange(): lax.all_to_all(values, 'expert', split_axis=0, concat_axis=0, tiled=True)  17.7 us
    ppermute x6, waiting for transfers between devices, send_up(): return lax.ppermute(x, 'dp', UP)  16.6 us
    ppermute x6, starting transfers between devices, send_down(): return lax.ppermute(x, 'dp', DOWN)  14.6 us
    all_to_all x3, waiting for transfers between devices, exchange(): lax.all_to_all(values, 'expert', split_axis=0, concat_axis=0, tiled=True)  8.02 us
    pallas_call x3, Pallas kernels, unpack_block(): pl.pallas_call(unpack_block_kernel, grid_spec=pltpu.PrefetchScalarGridSpe...  6.01 us
    unnamed x26, local copies, waits for them, and re-layouts  4.24 us
    pallas_call x2, Pallas kernels, pack_halves(): pl.pallas_call(functools.partial(pack_halves_kernel, n), grid_spec=pltpu....  4.12 us
  transfers between devices with their start and end apart: 15, of which 6 were waited for; matrix products, arithmetic and copies ran while one was open for 3% of the time, Pallas kernels for 16%

profile of v2, /device:TPU:1, one launch (start us, length us, event | category | flops | bytes accessed | tf_op | source)
XLA Modules:
  0.0 118.2 jit_solution(15415053382904141890)
XLA Ops:
  0.6 3.9 %pack_state.1 = bf16[32,4,3,8,256]{4,3,2,1,0:T(8,128)(2,1)} custom-call(f32[4,128,512]{2,1,0:T(8,128)} %m1_ref.1, f32[4,128,512]{2,1,0:T(8,128)} %m2_ref.1, f32[4,128,512]{2,1,0:T(8,128)} %w_ref.1), custom_call_target="tpu_custom_call" | custom-call | tf_op jit(solution)/shard_map/pack_state/pallas_call | solution.py:69
  4.5 8.6 %all-to-all-start = ((bf16[32,4,3,8,256]{4,3,2,1,0:T(8,128)(2,1)}), bf16[32,4,3,8,256]{4,3,2,1,0:T(8,128)(2,1)S(1)}, u32[]{:S(2)}, u32[]{:S(2)}) async-start(bf16[32,4,3,8,256]{4,3,2,1,0:T(8,128)(2,1)} %pack_state.1), calls=%async_computation | async-start | bytes 3145728 | tf_op jit(solution)/shard_map/all_to_all | solution.py:269
  13.1 1.8 %pack_far.1 = (bf16[16,4,8,256]{3,2,1,0:T(8,128)(2,1)}, bf16[16,4,8,256]{3,2,1,0:T(8,128)(2,1)}) custom-call(s32[1]{0:T(128)} %bitcast.me_ref, bf16[4,2,64,2048]{3,2,1,0:T(8,128)(2,1)} %bitcast.8), custom_call_target="tpu_custom_call" | custom-call | tf_op jit(solution)/shard_map/pack_far/pallas_call | solution.py:101
  16.5 2.1 %collective-permute-start.4 = (bf16[16,4,8,256]{3,2,1,0:T(8,128)(2,1)}, bf16[16,4,8,256]{3,2,1,0:T(8,128)(2,1)S(1)}, u32[]{:S(2)}, u32[]{:S(2)}) collective-permute-start(bf16[16,4,8,256]{3,2,1,0:T(8,128)(2,1)} %get-tuple-element.37), channel_id=1, source_target_pairs={{0,96},{32,0},{64,32},{96,64},{1,97},{33,1},{65,33},{97,65},{2,98}... | collective-permute-start | bytes 786440 | tf_op jit(solution)/shard_map/ppermute | solution.py:261
  18.7 2.3 %pack_near.1 = (bf16[16,4,8,256]{3,2,1,0:T(8,128)(2,1)}, bf16[16,4,8,256]{3,2,1,0:T(8,128)(2,1)}, bf16[16,4,8,256]{3,2,1,0:T(8,128)(2,1)}, bf16[16,4,8,256]{3,2,...) custom-call(s32[1]{0:T(128)} %bitcast.me_ref, bf16[4,2,64,2048]{3,2,1,0:T(8,128)(2,1)} %bitcast.9, ...), custom_call_target="tpu_custom_call" | custom-call | tf_op jit(solution)/shard_map/pack_near/pallas_call | solution.py:101
  21.0 2.7 %collective-permute-start.3 = (bf16[16,4,8,256]{3,2,1,0:T(8,128)(2,1)}, bf16[16,4,8,256]{3,2,1,0:T(8,128)(2,1)S(1)}, u32[]{:S(2)}, u32[]{:S(2)}) collective-permute-start(bf16[16,4,8,256]{3,2,1,0:T(8,128)(2,1)} %get-tuple-element.35), channel_id=1, source_target_pairs={{0,96},{32,0},{64,32},{96,64},{1,97},{33,1},{65,33},{97,65},{2,98}... | collective-permute-start | bytes 786440 | tf_op jit(solution)/shard_map/ppermute | solution.py:261
  27.6 2.7 %collective-permute-start.5 = (bf16[16,4,8,256]{3,2,1,0:T(8,128)(2,1)S(1)}, bf16[16,4,8,256]{3,2,1,0:T(8,128)(2,1)S(1)}, u32[]{:S(2)}, u32[]{:S(2)}) collective-permute-start(bf16[16,4,8,256]{3,2,1,0:T(8,128)(2,1)S(1)} %add_convert_fusion), channel_id=1, source_target_pairs={{0,96},{32,0},{64,32},{96,64},{1,97},{33,1},{65,33},{97,65},{2,98}... | collective-permute-start | bytes 786440 | tf_op jit(solution)/shard_map/ppermute | solution.py:261
  30.9 5.4 %collective-permute-done.1.ua = bf16[16,4,8,256]{3,2,1,0:T(8,128)(2,1)S(1)} collective-permute-done((bf16[16,4,8,256]{3,2,1,0:T(8,128)(2,1)S(1)}, bf16[16,4,8,256]{3,2,1,0:T(8,128)(2,1)S(1)}, u32[]{:S(2)}, u32[]{:S(2)}) %collective-permute-start.1) | collective-permute-done | bytes 262176 | tf_op jit(solution)/shard_map/ppermute | solution.py:257
  37.1 2.3 %sum_grad.1 = bf16[32,4,8,256]{3,2,1,0:T(8,128)(2,1)} custom-call(bf16[16,4,8,256]{3,2,1,0:T(8,128)(2,1)} %get-tuple-element.39.own_a, bf16[16,4,8,256]{3,2,1,0:T(8,128)(2,1)} %get-tuple-element.40.own_b, bf16[16,4,8,256]{3,2,1,0:T(8,128)(2,1)} %copy-done.11, bf16[16,4,8,256]{3,2,1,0:T(8,128)(2,1)} %copy-done.9, bf16[16,4,8,256]{3,2,1,0:T(8,128)(2,1)} %copy-done.10, ...), custom_call_target="tpu_custom_call" | custom-call | tf_op jit(solution)/shard_map/sum_grad/pallas_call | solution.py:123
  39.4 8.1 %all-to-all-start.1 = ((bf16[32,4,8,256]{3,2,1,0:T(8,128)(2,1)}), bf16[32,4,8,256]{3,2,1,0:T(8,128)(2,1)S(1)}, u32[]{:S(2)}, u32[]{:S(2)}) async-start(bf16[32,4,8,256]{3,2,1,0:T(8,128)(2,1)} %sum_grad.1), calls=%async_computation.1 | async-start | bytes 1048576 | tf_op jit(solution)/shard_map/all_to_all | solution.py:269
  47.5 3.6 %route.1.table_ref = s32[192]{0:T(256)} custom-call(s32[104]{0:T(128)} %old_ref.1, s32[104]{0:T(128)} %new_ref.1), custom_call_target="tpu_custom_call" | custom-call | tf_op jit(solution)/shard_map/route/pallas_call | solution.py:48
  51.1 8.0 %all-to-all-done.1 = bf16[32,4,8,256]{3,2,1,0:T(8,128)(2,1)S(1)} async-done(((bf16[32,4,8,256]{3,2,1,0:T(8,128)(2,1)}), bf16[32,4,8,256]{3,2,1,0:T(8,128)(2,1)S(1)}, u32[]{:S(2)}, u32[]{:S(2)}) %all-to-all-start.1) | async-done | bytes 524320 | tf_op jit(solution)/shard_map/all_to_all | solution.py:269
  59.8 2.8 %update.1 = (bf16[32,6,8,256]{3,2,1,0:T(8,128)(2,1)S(1)}, bf16[32,6,2,8,256]{4,3,2,1,0:T(8,128)(2,1)S(1)}) custom-call(s32[192]{0:T(256)S(1)} %copy-done.1, bf16[128,3,8,256]{3,2,1,0:T(8,128)(2,1)S(1)} %bitcast.6, bf16[128,8,256]{2,1,0:T(8,128)(2,1)S(1)} %bitcast.7), custom_call_target="tpu_custom_call" | custom-call | tf_op jit(solution)/shard_map/update/pallas_call | solution.py:161
  62.6 17.7 %all_to_all.20.w_ref = bf16[32,6,8,256]{3,2,1,0:T(8,128)(2,1)S(1)} all-to-all(bf16[32,6,8,256]{3,2,1,0:T(8,128)(2,1)S(1)} %get-tuple-element.45), channel_id=1, replica_groups=mesh['dp'=4,'expert'=32] {'expert'}, dimensions={0} | all-to-all | bytes 1572864 | tf_op jit(solution)/shard_map/all_to_all | solution.py:269
  80.3 3.8 %all-to-all-start.3 = ((bf16[32,6,2,8,256]{4,3,2,1,0:T(8,128)(2,1)}), bf16[32,6,2,8,256]{4,3,2,1,0:T(8,128)(2,1)S(1)}, u32[]{:S(2)}, u32[]{:S(2)}) async-start(bf16[32,6,2,8,256]{4,3,2,1,0:T(8,128)(2,1)} %copy-done), calls=%async_computation.3 | async-start | bytes 3145728 | tf_op jit(solution)/shard_map/all_to_all | solution.py:269
  87.8 2.7 %collective-permute-start.10 = (bf16[16,6,8,256]{3,2,1,0:T(8,128)(2,1)}, bf16[16,6,8,256]{3,2,1,0:T(8,128)(2,1)S(1)}, u32[]{:S(2)}, u32[]{:S(2)}) collective-permute-start(bf16[16,6,8,256]{3,2,1,0:T(8,128)(2,1)} %get-tuple-element.57), channel_id=1, source_target_pairs={{0,96},{32,0},{64,32},{96,64},{1,97},{33,1},{65,33},{97,65},{2,98}... | collective-permute-start | bytes 1179656 | tf_op jit(solution)/shard_map/ppermute | solution.py:261
  90.4 6.5 %collective-permute-done.6.a_ref = bf16[16,6,8,256]{3,2,1,0:T(8,128)(2,1)S(1)} collective-permute-done((bf16[16,6,8,256]{3,2,1,0:T(8,128)(2,1)}, bf16[16,6,8,256]{3,2,1,0:T(8,128)(2,1)S(1)}, u32[]{:S(2)}, u32[]{:S(2)}) %collective-permute-start.6) | collective-permute-done | bytes 393248 | tf_op jit(solution)/shard_map/ppermute | solution.py:257
  97.0 2.7 %collective-permute-start.9 = (bf16[16,6,8,256]{3,2,1,0:T(8,128)(2,1)S(1)}, bf16[16,6,8,256]{3,2,1,0:T(8,128)(2,1)S(1)}, u32[]{:S(2)}, u32[]{:S(2)}) collective-permute-start(bf16[16,6,8,256]{3,2,1,0:T(8,128)(2,1)S(1)} %collective-permute-done.8.b_ref), channel_id=1, source_target_pairs={{0,96},{32,0},{64,32},{96,64},{1,97},{33,1},{65,33},{97,65},{2,98}... | collective-permute-start | bytes 1179656 | tf_op jit(solution)/shard_map/ppermute | solution.py:261
  99.7 3.6 %unpack_own.1 = (f32[6,128,512]{2,1,0:T(8,128)}, bf16[6,128,2048]{2,1,0:T(8,128)(2,1)}) custom-call(s32[1]{0:T(128)} %bitcast.me_ref, bf16[32,6,8,256]{3,2,1,0:T(8,128)(2,1)} %copy-done.2), custom_call_target="tpu_custom_call" | custom-call | tf_op jit(solution)/shard_map/unpack_own/pallas_call | solution.py:187
  103.2 2.3 %collective-permute-done.11.b_ref = bf16[16,6,8,256]{3,2,1,0:T(8,128)(2,1)} collective-permute-done((bf16[16,6,8,256]{3,2,1,0:T(8,128)(2,1)}, bf16[16,6,8,256]{3,2,1,0:T(8,128)(2,1)}, u32[]{:S(2)}, u32[]{:S(2)}) %collective-permute-start.11) | collective-permute-done | bytes 393248 | tf_op jit(solution)/shard_map/ppermute | solution.py:257
  105.5 2.0 %unpack_block.3.old_ref = bf16[6,2,64,2048]{3,2,1,0:T(8,128)(2,1)} custom-call(s32[1]{0:T(128)} %bitcast.me_ref, bf16[16,6,8,256]{3,2,1,0:T(8,128)(2,1)} %copy-done.4, bf16[16,6,8,256]{3,2,1,0:T(8,128)(2,1)} %collective-permute-done.11.b_ref, bf16[6,2,64,2048]{3,2,1,0:T(8,128)(2,1)} %bitcast.12), custom_call_target="tpu_custom_call", output_to_operand_aliasing={{}: (3, {})} | custom-call | tf_op jit(solution)/shard_map/unpack_block/pallas_call | solution.py:238
  108.3 2.0 %unpack_block.4.old_ref = bf16[6,2,64,2048]{3,2,1,0:T(8,128)(2,1)} custom-call(s32[1]{0:T(128)} %bitcast.me_ref, bf16[16,6,8,256]{3,2,1,0:T(8,128)(2,1)} %copy-done.8, bf16[16,6,8,256]{3,2,1,0:T(8,128)(2,1)} %copy-done.5, bf16[6,2,64,2048]{3,2,1,0:T(8,128)(2,1)} %unpack_block.3.old_ref), custom_call_target="tpu_custom_call", output_to_operand_aliasing={{}: (3, {})} | custom-call | tf_op jit(solution)/shard_map/unpack_block/pallas_call | solution.py:238
  111.5 3.9 %unpack_moments.1 = (f32[6,128,512]{2,1,0:T(8,128)}, f32[6,128,512]{2,1,0:T(8,128)}) custom-call(bf16[32,6,2,8,256]{4,3,2,1,0:T(8,128)(2,1)} %copy-done.3), custom_call_target="tpu_custom_call" | custom-call | tf_op jit(solution)/shard_map/unpack_moments/pallas_call | solution.py:217
  116.2 2.0 %unpack_block.5 = bf16[6,2,64,2048]{3,2,1,0:T(8,128)(2,1)} custom-call(s32[1]{0:T(128)} %bitcast.me_ref, bf16[16,6,8,256]{3,2,1,0:T(8,128)(2,1)} %copy-done.6, bf16[16,6,8,256]{3,2,1,0:T(8,128)(2,1)} %copy-done.7, bf16[6,2,64,2048]{3,2,1,0:T(8,128)(2,1)} %unpack_block.4.old_ref), custom_call_target="tpu_custom_call", output_to_operand_aliasing={{}: (3, {})} | custom-call | tf_op jit(solution)/shard_map/unpack_block/pallas_call | solution.py:238
  (47 shorter events, 14.1 us)
Async XLA Ops:
  4.5 31.8 %all-to-all-start = ((bf16[32,4,3,8,256]{4,3,2,1,0:T(8,128)(2,1)}), bf16[32,4,3,8,256]{4,3,2,1,0:T(8,128)(2,1)S(1)}, u32[]{:S(2)}, u32[]{:S(2)}) async-start(bf16[32,4,3,8,256]{4,3,2,1,0:T(8,128)(2,1)} %pack_state.1), calls=%async_computation | async-start | bytes 3145728 | tf_op jit(solution)/shard_map/all_to_all | solution.py:269
  14.9 10.5 %collective-permute-start = (bf16[16,4,8,256]{3,2,1,0:T(8,128)(2,1)}, bf16[16,4,8,256]{3,2,1,0:T(8,128)(2,1)S(1)}, u32[]{:S(2)}, u32[]{:S(2)}) collective-permute-start(bf16[16,4,8,256]{3,2,1,0:T(8,128)(2,1)} %get-tuple-element.33), channel_id=1, source_target_pairs={{0,32},{32,64},{64,96},{96,0},{1,33},{33,65},{65,97},{97,1},{2,34}... | collective-permute-start | bytes 786440 | tf_op jit(solution)/shard_map/ppermute | solution.py:257
  16.5 10.0 %collective-permute-start.4 = (bf16[16,4,8,256]{3,2,1,0:T(8,128)(2,1)}, bf16[16,4,8,256]{3,2,1,0:T(8,128)(2,1)S(1)}, u32[]{:S(2)}, u32[]{:S(2)}) collective-permute-start(bf16[16,4,8,256]{3,2,1,0:T(8,128)(2,1)} %get-tuple-element.37), channel_id=1, source_target_pairs={{0,96},{32,0},{64,32},{96,64},{1,97},{33,1},{65,33},{97,65},{2,98}... | collective-permute-start | bytes 786440 | tf_op jit(solution)/shard_map/ppermute | solution.py:261
  21.0 10.0 %collective-permute-start.2 = (bf16[16,4,8,256]{3,2,1,0:T(8,128)(2,1)}, bf16[16,4,8,256]{3,2,1,0:T(8,128)(2,1)S(1)}, u32[]{:S(2)}, u32[]{:S(2)}) collective-permute-start(bf16[16,4,8,256]{3,2,1,0:T(8,128)(2,1)} %get-tuple-element.34), channel_id=1, source_target_pairs={{0,32},{32,64},{64,96},{96,0},{1,33},{33,65},{65,97},{97,1},{2,34}... | collective-permute-start | bytes 786440 | tf_op jit(solution)/shard_map/ppermute | solution.py:257
  21.0 10.0 %collective-permute-start.3 = (bf16[16,4,8,256]{3,2,1,0:T(8,128)(2,1)}, bf16[16,4,8,256]{3,2,1,0:T(8,128)(2,1)S(1)}, u32[]{:S(2)}, u32[]{:S(2)}) collective-permute-start(bf16[16,4,8,256]{3,2,1,0:T(8,128)(2,1)} %get-tuple-element.35), channel_id=1, source_target_pairs={{0,96},{32,0},{64,32},{96,64},{1,97},{33,1},{65,33},{97,65},{2,98}... | collective-permute-start | bytes 786440 | tf_op jit(solution)/shard_map/ppermute | solution.py:261
  26.4 9.9 %collective-permute-start.1 = (bf16[16,4,8,256]{3,2,1,0:T(8,128)(2,1)S(1)}, bf16[16,4,8,256]{3,2,1,0:T(8,128)(2,1)S(1)}, u32[]{:S(2)}, u32[]{:S(2)}) collective-permute-start(bf16[16,4,8,256]{3,2,1,0:T(8,128)(2,1)S(1)} %add_convert_fusion.1), channel_id=1, source_target_pairs={{0,32},{32,64},{64,96},{96,0},{1,33},{33,65},{65,97},{97,1},{2,34}... | collective-permute-start | bytes 786440 | tf_op jit(solution)/shard_map/ppermute | solution.py:257
  27.6 8.8 %collective-permute-start.5 = (bf16[16,4,8,256]{3,2,1,0:T(8,128)(2,1)S(1)}, bf16[16,4,8,256]{3,2,1,0:T(8,128)(2,1)S(1)}, u32[]{:S(2)}, u32[]{:S(2)}) collective-permute-start(bf16[16,4,8,256]{3,2,1,0:T(8,128)(2,1)S(1)} %add_convert_fusion), channel_id=1, source_target_pairs={{0,96},{32,0},{64,32},{96,64},{1,97},{33,1},{65,33},{97,65},{2,98}... | collective-permute-start | bytes 786440 | tf_op jit(solution)/shard_map/ppermute | solution.py:261
  30.9 5.4 %copy-start.9 = (bf16[16,4,8,256]{3,2,1,0:T(8,128)(2,1)}, bf16[16,4,8,256]{3,2,1,0:T(8,128)(2,1)S(1)}, u32[]{:S(2)}) copy-start(bf16[16,4,8,256]{3,2,1,0:T(8,128)(2,1)S(1)} %collective-permute-done.2.ub) | copy-start | bytes 786436
  30.9 5.4 %copy-start.10 = (bf16[16,4,8,256]{3,2,1,0:T(8,128)(2,1)}, bf16[16,4,8,256]{3,2,1,0:T(8,128)(2,1)S(1)}, u32[]{:S(2)}) copy-start(bf16[16,4,8,256]{3,2,1,0:T(8,128)(2,1)S(1)} %collective-permute-done.3.da) | copy-start | bytes 786436
  36.3 0.8 copy-start.12
  39.4 19.7 %all-to-all-start.1 = ((bf16[32,4,8,256]{3,2,1,0:T(8,128)(2,1)}), bf16[32,4,8,256]{3,2,1,0:T(8,128)(2,1)S(1)}, u32[]{:S(2)}, u32[]{:S(2)}) async-start(bf16[32,4,8,256]{3,2,1,0:T(8,128)(2,1)} %sum_grad.1), calls=%async_computation.1 | async-start | bytes 1048576 | tf_op jit(solution)/shard_map/all_to_all | solution.py:269
  62.6 17.7 %copy-start = (bf16[32,6,2,8,256]{4,3,2,1,0:T(8,128)(2,1)}, bf16[32,6,2,8,256]{4,3,2,1,0:T(8,128)(2,1)S(1)}, u32[]{:S(2)}) copy-start(bf16[32,6,2,8,256]{4,3,2,1,0:T(8,128)(2,1)S(1)} %get-tuple-element.49) | copy-start | bytes 4718596
  80.3 3.8 %copy-start.2 = (bf16[32,6,8,256]{3,2,1,0:T(8,128)(2,1)}, bf16[32,6,8,256]{3,2,1,0:T(8,128)(2,1)S(1)}, u32[]{:S(2)}) copy-start(bf16[32,6,8,256]{3,2,1,0:T(8,128)(2,1)S(1)} %all_to_all.20.w_ref) | copy-start | bytes 2359300
  80.3 30.0 %all-to-all-start.3 = ((bf16[32,6,2,8,256]{4,3,2,1,0:T(8,128)(2,1)}), bf16[32,6,2,8,256]{4,3,2,1,0:T(8,128)(2,1)S(1)}, u32[]{:S(2)}, u32[]{:S(2)}) async-start(bf16[32,6,2,8,256]{4,3,2,1,0:T(8,128)(2,1)} %copy-done), calls=%async_computation.3 | async-start | bytes 3145728 | tf_op jit(solution)/shard_map/all_to_all | solution.py:269
  85.1 11.9 %collective-permute-start.6 = (bf16[16,6,8,256]{3,2,1,0:T(8,128)(2,1)}, bf16[16,6,8,256]{3,2,1,0:T(8,128)(2,1)S(1)}, u32[]{:S(2)}, u32[]{:S(2)}) collective-permute-start(bf16[16,6,8,256]{3,2,1,0:T(8,128)(2,1)} %get-tuple-element.57), channel_id=1, source_target_pairs={{0,32},{32,64},{64,96},{96,0},{1,33},{33,65},{65,97},{97,1},{2,34}... | collective-permute-start | bytes 1179656 | tf_op jit(solution)/shard_map/ppermute | solution.py:257
  86.0 11.0 %collective-permute-start.8 = (bf16[16,6,8,256]{3,2,1,0:T(8,128)(2,1)}, bf16[16,6,8,256]{3,2,1,0:T(8,128)(2,1)S(1)}, u32[]{:S(2)}, u32[]{:S(2)}) collective-permute-start(bf16[16,6,8,256]{3,2,1,0:T(8,128)(2,1)} %get-tuple-element.56), channel_id=1, source_target_pairs={{0,96},{32,0},{64,32},{96,64},{1,97},{33,1},{65,33},{97,65},{2,98}... | collective-permute-start | bytes 1179656 | tf_op jit(solution)/shard_map/ppermute | solution.py:261
  87.8 17.8 %collective-permute-start.11 = (bf16[16,6,8,256]{3,2,1,0:T(8,128)(2,1)}, bf16[16,6,8,256]{3,2,1,0:T(8,128)(2,1)}, u32[]{:S(2)}, u32[]{:S(2)}) collective-permute-start(bf16[16,6,8,256]{3,2,1,0:T(8,128)(2,1)} %get-tuple-element.56), channel_id=1, source_target_pairs={{0,32},{32,64},{64,96},{96,0},{1,33},{33,65},{65,97},{97,1},{2,34}... | collective-permute-start | bytes 1179656 | tf_op jit(solution)/shard_map/ppermute | solution.py:257
  87.8 19.8 %collective-permute-start.10 = (bf16[16,6,8,256]{3,2,1,0:T(8,128)(2,1)}, bf16[16,6,8,256]{3,2,1,0:T(8,128)(2,1)S(1)}, u32[]{:S(2)}, u32[]{:S(2)}) collective-permute-start(bf16[16,6,8,256]{3,2,1,0:T(8,128)(2,1)} %get-tuple-element.57), channel_id=1, source_target_pairs={{0,96},{32,0},{64,32},{96,64},{1,97},{33,1},{65,33},{97,65},{2,98}... | collective-permute-start | bytes 1179656 | tf_op jit(solution)/shard_map/ppermute | solution.py:261
  97.0 8.5 %copy-start.4 = (bf16[16,6,8,256]{3,2,1,0:T(8,128)(2,1)}, bf16[16,6,8,256]{3,2,1,0:T(8,128)(2,1)S(1)}, u32[]{:S(2)}) copy-start(bf16[16,6,8,256]{3,2,1,0:T(8,128)(2,1)S(1)} %collective-permute-done.6.a_ref) | copy-start | bytes 1179652
  97.0 18.4 %collective-permute-start.7 = (bf16[16,6,8,256]{3,2,1,0:T(8,128)(2,1)S(1)}, bf16[16,6,8,256]{3,2,1,0:T(8,128)(2,1)S(1)}, u32[]{:S(2)}, u32[]{:S(2)}) collective-permute-start(bf16[16,6,8,256]{3,2,1,0:T(8,128)(2,1)S(1)} %collective-permute-done.6.a_ref), channel_id=1, source_target_pairs={{0,32},{32,64},{64,96},{96,0},{1,33},{33,65},{65,97},{97,1},{2,34}... | collective-permute-start | bytes 1179656 | tf_op jit(solution)/shard_map/ppermute | solution.py:257
  97.0 10.5 %copy-start.5 = (bf16[16,6,8,256]{3,2,1,0:T(8,128)(2,1)}, bf16[16,6,8,256]{3,2,1,0:T(8,128)(2,1)S(1)}, u32[]{:S(2)}) copy-start(bf16[16,6,8,256]{3,2,1,0:T(8,128)(2,1)S(1)} %collective-permute-done.8.b_ref) | copy-start | bytes 1179652
  97.0 18.3 %collective-permute-start.9 = (bf16[16,6,8,256]{3,2,1,0:T(8,128)(2,1)S(1)}, bf16[16,6,8,256]{3,2,1,0:T(8,128)(2,1)S(1)}, u32[]{:S(2)}, u32[]{:S(2)}) collective-permute-start(bf16[16,6,8,256]{3,2,1,0:T(8,128)(2,1)S(1)} %collective-permute-done.8.b_ref), channel_id=1, source_target_pairs={{0,96},{32,0},{64,32},{96,64},{1,97},{33,1},{65,33},{97,65},{2,98}... | collective-permute-start | bytes 1179656 | tf_op jit(solution)/shard_map/ppermute | solution.py:261
  110.3 1.2 copy-start.3
  115.3 0.9 copy-start.7
  (4 other events, 2.9 us)

commit v3 on v2

--- a/solution.py
+++ b/solution.py
@@ -13,7 +13,8 @@
 OLD = 4
 NEW = 6
 PR, PC = 8, 256
-STEPS = 4
+STEPS = 2
+PARAMS = pltpu.CompilerParams(vmem_limit_bytes=16 * 1024 * 1024)
 VMEM = pl.BlockSpec(memory_space=pltpu.VMEM)
 
 
@@ -51,6 +52,7 @@
         in_specs=[smem, smem],
         out_specs=smem,
         scratch_shapes=[pltpu.SMEM((PEERS,), jnp.int32), pltpu.SMEM((PEERS,), jnp.int32)],
+        compiler_params=PARAMS,
         name="route",
     )(old_owner, new_owner)
 
@@ -107,6 +109,7 @@
             out_specs=[half_block(steps, OLD)] * (2 * n),
         ),
         out_shape=[half] * (2 * n),
+        compiler_params=PARAMS,
         name=name,
     )(me, *([g] * n))
 
@@ -125,6 +128,7 @@
         out_shape=jax.ShapeDtypeStruct((PEERS, OLD, PR, PC), BF16),
         in_specs=[VMEM] * 6,
         out_specs=VMEM,
+        compiler_params=PARAMS,
         name="sum_grad",
     )(*halves)
 
@@ -132,7 +136,9 @@
 def adam_step(gradient, moment_one, moment_two, weight):
     moment_one = 0.9 * moment_one + 0.1 * gradient
     moment_two = 0.95 * moment_two + 0.05 * gradient * gradient
-    update = moment_one / (1.0 - 0.9**50) / (jnp.sqrt(moment_two / (1.0 - 0.95**50)) + 1e-08)
+    scaled_one = moment_one * (1.0 / (1.0 - 0.9**50))
+    scaled_two = moment_two * (1.0 / (1.0 - 0.95**50))
+    update = scaled_one / (jnp.sqrt(scaled_two) + 1e-08)
     weight = weight - 0.05 * (update + 0.1 * weight)
     return (weight, moment_one, moment_two)
 
@@ -166,18 +172,18 @@
         ),
         in_specs=[pl.BlockSpec(memory_space=pltpu.SMEM), vmem, vmem],
         out_specs=(vmem, vmem),
-        compiler_params=pltpu.CompilerParams(vmem_limit_bytes=32 * 1024 * 1024),
+        compiler_params=PARAMS,
         name="update",
     )(table, state, grad)
 
 
 def unpack_own_kernel(me_ref, w_ref, w_out, out_ref):
     del me_ref
-    n = w_out.shape[1] // PR
-    for r in range(n):
+    first = pl.program_id(0) * (PEERS // STEPS)
+    for r in range(w_out.shape[1] // PR):
         for c in range(2):
             rows, lanes = slice(r * PR, (r + 1) * PR), slice(c * PC, (c + 1) * PC)
-            piece = w_ref[2 * r + c]
+            piece = w_ref[first + 2 * r + c]
             w_out[:, rows, lanes] = piece.astype(F32)
             out_ref[:, rows, lanes] = piece
 
@@ -189,7 +195,7 @@
         grid_spec=pltpu.PrefetchScalarGridSpec(
             num_scalar_prefetch=1,
             grid=(STEPS,),
-            in_specs=[pl.BlockSpec((PEERS // STEPS, NEW, PR, PC), lambda i, me: (i, 0, 0, 0))],
+            in_specs=[VMEM],
             out_specs=[
                 pl.BlockSpec((NEW, rows, 512), lambda i, me: (0, i, 0)),
                 pl.BlockSpec((NEW, rows, 512), lambda i, me: (0, i, me[0])),
@@ -199,16 +205,18 @@
             jax.ShapeDtypeStruct((NEW, 128, 512), F32),
             jax.ShapeDtypeStruct((NEW, 128, 2048), BF16),
         ),
+        compiler_params=PARAMS,
         name="unpack_own",
     )(me, w)
 
 
 def unpack_moments_kernel(m_ref, m1_out, m2_out):
+    first = pl.program_id(0) * (PEERS // STEPS)
     for r in range(m1_out.shape[1] // PR):
         for c in range(2):
             rows, lanes = slice(r * PR, (r + 1) * PR), slice(c * PC, (c + 1) * PC)
-            m1_out[:, rows, lanes] = m_ref[2 * r + c, :, 0].astype(F32)
-            m2_out[:, rows, lanes] = m_ref[2 * r + c, :, 1].astype(F32)
+            m1_out[:, rows, lanes] = m_ref[first + 2 * r + c, :, 0].astype(F32)
+            m2_out[:, rows, lanes] = m_ref[first + 2 * r + c, :, 1].astype(F32)
 
 
 def unpack_moments(m):
@@ -218,33 +226,39 @@
         unpack_moments_kernel,
         grid=(STEPS,),
         out_shape=(out, out),
-        in_specs=[pl.BlockSpec((PEERS // STEPS, NEW, 2, PR, PC), lambda i: (i, 0, 0, 0, 0))],
+        in_specs=[VMEM],
         out_specs=[pl.BlockSpec((NEW, rows, 512), lambda i: (0, i, 0))] * 2,
+        compiler_params=PARAMS,
         name="unpack_moments",
     )(m)
 
 
 def unpack_block_kernel(me_ref, a_ref, b_ref, old_ref, out_ref):
     del me_ref, old_ref
-    for r in range(out_ref.shape[2] // PR):
-        for c in range(2):
-            rows, lanes = slice(r * PR, (r + 1) * PR), slice(c * PC, (c + 1) * PC)
-            out_ref[:, 0, rows, lanes] = a_ref[2 * r + c]
-            out_ref[:, 1, rows, lanes] = b_ref[2 * r + c]
+    half = pl.program_id(0)
+
+    def copy(ref):
+        for r in range(out_ref.shape[1] // PR):
+            for c in range(2):
+                rows, lanes = slice(r * PR, (r + 1) * PR), slice(c * PC, (c + 1) * PC)
+                out_ref[:, rows, lanes] = ref[2 * r + c]
+
+    pl.when(half == 0)(lambda: copy(a_ref))
+    pl.when(half == 1)(lambda: copy(b_ref))
 
 
 def unpack_block(me, a, b, params, ahead):
-    steps = 2
     return pl.pallas_call(
         unpack_block_kernel,
         grid_spec=pltpu.PrefetchScalarGridSpec(
             num_scalar_prefetch=1,
-            grid=(steps,),
-            in_specs=[half_block(steps, NEW)] * 2 + [pl.BlockSpec(memory_space=pl.ANY)],
-            out_specs=pl.BlockSpec((NEW, 2, 64 // steps, 512), lambda i, me: (0, 0, i, (me[0] + ahead) % 4)),
-        ),
-        out_shape=jax.ShapeDtypeStruct((NEW, 2, 64, 2048), BF16),
+            grid=(2,),
+            in_specs=[VMEM, VMEM, pl.BlockSpec(memory_space=pl.ANY)],
+            out_specs=pl.BlockSpec((NEW, 64, 512), lambda i, me: (0, i, (me[0] + ahead) % 4)),
+        ),
+        out_shape=jax.ShapeDtypeStruct((NEW, 128, 2048), BF16),
         input_output_aliases={3: 0},
+        compiler_params=PARAMS,
         name="unpack_block",
     )(me, a, b, params)
 
@@ -296,12 +310,11 @@
     fa, fb = send_up(ua), send_down(db)
     moments = exchange(moments)
     new_master, params = unpack_own(me, weight)
-    params = params.reshape(NEW, 2, 64, 2048)
     params = unpack_block(me, ua, ub, params, 3)
     params = unpack_block(me, da, db, params, 1)
     new_first, new_second = unpack_moments(moments)
     fa, fb, new_first = lax.optimization_barrier((fa, fb, new_first))
-    new_params = unpack_block(me, fa, fb, params, 2).reshape(NEW, 128, 2048)
+    new_params = unpack_block(me, fa, fb, params, 2)
     return (new_master, new_first, new_second, new_params)
 
 

time: 120 us -> 111 us (0.925)
  Pallas kernels: 30.2 us -> 18.5 us
  waiting for transfers between devices: 24.6 us -> 36.1 us
  local copies, waits for them, and re-layouts: 5.19 us -> 0.07 us
  other arithmetic: 2.06 us -> 0.17 us
    ppermute x6, waiting for transfers between devices: 16.6 us -> 26.6 us  [send_up(): return lax.ppermute(x, 'dp', UP)]
    unnamed x26 -> x8, local copies, waits for them, and re-layouts: 4.24 us -> 0.02 us
    pallas_call x2, Pallas kernels: 4.12 us -> 0.5 us  [pack_halves(): pl.pallas_call(functools.partial(pack_halves_kernel, n), grid_spec=pltpu....]
    pallas_call x3, Pallas kernels: 6.01 us -> 3.74 us  [unpack_block(): pl.pallas_call(unpack_block_kernel, grid_spec=pltpu.PrefetchScalarGridSpe...]
    pallas_call x1, Pallas kernels: 3.87 us -> 1.76 us  [unpack_moments(): pl.pallas_call(unpack_moments_kernel, grid=(STEPS,), out_shape=(out, out)...]
    pallas_call x1, Pallas kernels: 3.58 us -> 1.48 us  [unpack_own(): pl.pallas_call(unpack_own_kernel, grid_spec=pltpu.PrefetchScalarGridSpec(...]
    convert_element_type x2, other arithmetic: 2.06 us -> 0.17 us  [add(): return (x.astype(F32) + y.astype(F32)).astype(BF16)]
    all_to_all x3, waiting for transfers between devices: 8.02 us -> 9.48 us  [exchange(): lax.all_to_all(values, 'expert', split_axis=0, concat_axis=0, tiled=True)]
  transfers between devices with their start and end apart: 15 -> 15, of which waited for: 6 -> 9; matrix products, arithmetic and copies ran while one was open for 3% -> 0% of each run, Pallas kernels for 16% -> 8%
where the time goes in v3:
time: 111 us; the launch traced here: 110 us
  starting transfers between devices  37.1 us (33%)
  waiting for transfers between devices  36.1 us (33%)
  Pallas kernels  18.5 us (17%)
  blocking collectives  17.7 us (16%)
    ppermute x6, waiting for transfers between devices, send_up(): return lax.ppermute(x, 'dp', UP)  26.6 us
    all_to_all x3, starting transfers between devices, exchange(): lax.all_to_all(values, 'expert', split_axis=0, concat_axis=0, tiled=True)  19.4 us
    all_to_all x1, blocking collectives, exchange(): lax.all_to_all(values, 'expert', split_axis=0, concat_axis=0, tiled=True)  17.7 us
    ppermute x6, starting transfers between devices, send_down(): return lax.ppermute(x, 'dp', DOWN)  14.8 us
    all_to_all x3, waiting for transfers between devices, exchange(): lax.all_to_all(values, 'expert', split_axis=0, concat_axis=0, tiled=True)  9.48 us
    pallas_call x3, Pallas kernels, unpack_block(): pl.pallas_call(unpack_block_kernel, grid_spec=pltpu.PrefetchScalarGridSpe...  3.74 us
    pallas_call x1, Pallas kernels, update(): pl.pallas_call(update_kernel, out_shape=(jax.ShapeDtypeStruct((PEERS, NEW...  3.73 us
    pallas_call x1, Pallas kernels, route(): pl.pallas_call(route_kernel, out_shape=jax.ShapeDtypeStruct((PEERS * NEW,...  3.5 us
  transfers between devices with their start and end apart: 15, of which 9 were waited for; matrix products, arithmetic and copies ran while one was open for 0% of the time, Pallas kernels for 8%

profile of v3, /device:TPU:1, one launch (start us, length us, event | category | flops | bytes accessed | tf_op | source)
XLA Modules:
  0.0 110.4 jit_solution(12220228566829520096)
XLA Ops:
  0.6 2.8 %pack_state.1 = bf16[32,4,3,8,256]{4,3,2,1,0:T(8,128)(2,1)} custom-call(f32[4,128,512]{2,1,0:T(8,128)} %m1_ref.1, f32[4,128,512]{2,1,0:T(8,128)} %m2_ref.1, f32[4,128,512]{2,1,0:T(8,128)} %w_ref.1), custom_call_target="tpu_custom_call" | custom-call | tf_op jit(solution)/shard_map/pack_state/pallas_call | solution.py:71
  3.5 8.8 %all-to-all-start = ((bf16[32,4,3,8,256]{4,3,2,1,0:T(8,128)(2,1)}), bf16[32,4,3,8,256]{4,3,2,1,0:T(8,128)(2,1)}, u32[]{:S(2)}, u32[]{:S(2)}) async-start(bf16[32,4,3,8,256]{4,3,2,1,0:T(8,128)(2,1)} %pack_state.1), calls=%async_computation | async-start | bytes 3145728 | tf_op jit(solution)/shard_map/all_to_all | solution.py:283
  12.4 1.7 %collective-permute-start = (bf16[16,4,8,256]{3,2,1,0:T(8,128)(2,1)S(1)}, bf16[16,4,8,256]{3,2,1,0:T(8,128)(2,1)S(1)}, u32[]{:S(2)}, u32[]{:S(2)}) collective-permute-start(bf16[16,4,8,256]{3,2,1,0:T(8,128)(2,1)S(1)} %get-tuple-element.33), channel_id=1, source_target_pairs={{0,32},{32,64},{64,96},{96,0},{1,33},{33,65},{65,97},{97,1},{2,34}... | collective-permute-start | bytes 786440 | tf_op jit(solution)/shard_map/ppermute | solution.py:271
  14.1 2.2 %collective-permute-start.4 = (bf16[16,4,8,256]{3,2,1,0:T(8,128)(2,1)S(1)}, bf16[16,4,8,256]{3,2,1,0:T(8,128)(2,1)S(1)}, u32[]{:S(2)}, u32[]{:S(2)}) collective-permute-start(bf16[16,4,8,256]{3,2,1,0:T(8,128)(2,1)S(1)} %get-tuple-element.37), channel_id=1, source_target_pairs={{0,96},{32,0},{64,32},{96,64},{1,97},{33,1},{65,33},{97,65},{2,98}... | collective-permute-start | bytes 786440 | tf_op jit(solution)/shard_map/ppermute | solution.py:275
  16.7 2.7 %collective-permute-start.3 = (bf16[16,4,8,256]{3,2,1,0:T(8,128)(2,1)S(1)}, bf16[16,4,8,256]{3,2,1,0:T(8,128)(2,1)S(1)}, u32[]{:S(2)}, u32[]{:S(2)}) collective-permute-start(bf16[16,4,8,256]{3,2,1,0:T(8,128)(2,1)S(1)} %get-tuple-element.35), channel_id=1, source_target_pairs={{0,96},{32,0},{64,32},{96,64},{1,97},{33,1},{65,33},{97,65},{2,98}... | collective-permute-start | bytes 786440 | tf_op jit(solution)/shard_map/ppermute | solution.py:275
  19.4 3.4 %collective-permute-done = bf16[16,4,8,256]{3,2,1,0:T(8,128)(2,1)S(1)} collective-permute-done((bf16[16,4,8,256]{3,2,1,0:T(8,128)(2,1)S(1)}, bf16[16,4,8,256]{3,2,1,0:T(8,128)(2,1)S(1)}, u32[]{:S(2)}, u32[]{:S(2)}) %collective-permute-start) | collective-permute-done | bytes 262176 | tf_op jit(solution)/shard_map/ppermute | solution.py:271
  23.1 2.7 %collective-permute-start.5 = (bf16[16,4,8,256]{3,2,1,0:T(8,128)(2,1)S(1)}, bf16[16,4,8,256]{3,2,1,0:T(8,128)(2,1)S(1)}, u32[]{:S(2)}, u32[]{:S(2)}) collective-permute-start(bf16[16,4,8,256]{3,2,1,0:T(8,128)(2,1)S(1)} %add_convert_fusion), channel_id=1, source_target_pairs={{0,96},{32,0},{64,32},{96,64},{1,97},{33,1},{65,33},{97,65},{2,98}... | collective-permute-start | bytes 786440 | tf_op jit(solution)/shard_map/ppermute | solution.py:275
  25.8 2.6 %collective-permute-done.2.ub = bf16[16,4,8,256]{3,2,1,0:T(8,128)(2,1)S(1)} collective-permute-done((bf16[16,4,8,256]{3,2,1,0:T(8,128)(2,1)S(1)}, bf16[16,4,8,256]{3,2,1,0:T(8,128)(2,1)S(1)}, u32[]{:S(2)}, u32[]{:S(2)}) %collective-permute-start.2) | collective-permute-done | bytes 262176 | tf_op jit(solution)/shard_map/ppermute | solution.py:271
  28.4 5.6 %collective-permute-done.1.ua = bf16[16,4,8,256]{3,2,1,0:T(8,128)(2,1)S(1)} collective-permute-done((bf16[16,4,8,256]{3,2,1,0:T(8,128)(2,1)S(1)}, bf16[16,4,8,256]{3,2,1,0:T(8,128)(2,1)S(1)}, u32[]{:S(2)}, u32[]{:S(2)}) %collective-permute-start.1) | collective-permute-done | bytes 262176 | tf_op jit(solution)/shard_map/ppermute | solution.py:271
  36.0 6.8 %all-to-all-start.1 = ((bf16[32,4,8,256]{3,2,1,0:T(8,128)(2,1)}), bf16[32,4,8,256]{3,2,1,0:T(8,128)(2,1)S(1)}, u32[]{:S(2)}, u32[]{:S(2)}) async-start(bf16[32,4,8,256]{3,2,1,0:T(8,128)(2,1)} %sum_grad.1), calls=%async_computation.1 | async-start | bytes 1048576 | tf_op jit(solution)/shard_map/all_to_all | solution.py:283
  42.8 3.5 %route.1.table_ref = s32[192]{0:T(256)S(1)} custom-call(s32[104]{0:T(128)S(1)} %copy-done.2, s32[104]{0:T(128)S(1)} %copy-done.3), custom_call_target="tpu_custom_call" | custom-call | tf_op jit(solution)/shard_map/route/pallas_call | solution.py:49
  46.3 8.1 %all-to-all-done.1 = bf16[32,4,8,256]{3,2,1,0:T(8,128)(2,1)S(1)} async-done(((bf16[32,4,8,256]{3,2,1,0:T(8,128)(2,1)}), bf16[32,4,8,256]{3,2,1,0:T(8,128)(2,1)S(1)}, u32[]{:S(2)}, u32[]{:S(2)}) %all-to-all-start.1) | async-done | bytes 524320 | tf_op jit(solution)/shard_map/all_to_all | solution.py:283
  54.4 3.7 %update.1 = (bf16[32,6,8,256]{3,2,1,0:T(8,128)(2,1)S(1)}, bf16[32,6,2,8,256]{4,3,2,1,0:T(8,128)(2,1)S(1)}) custom-call(s32[192]{0:T(256)S(1)} %route.1.table_ref, bf16[128,3,8,256]{3,2,1,0:T(8,128)(2,1)} %bitcast.2.state_ref, bf16[128,8,256]{2,1,0:T(8,128)(2,1)S(1)} %bitcast.8), custom_call_target="tpu_custom_call" | custom-call | tf_op jit(solution)/shard_map/update/pallas_call | solution.py:167
  58.1 17.7 %all_to_all.20.w_ref = bf16[32,6,8,256]{3,2,1,0:T(8,128)(2,1)S(1)} all-to-all(bf16[32,6,8,256]{3,2,1,0:T(8,128)(2,1)S(1)} %get-tuple-element.45), channel_id=1, replica_groups=mesh['dp'=4,'expert'=32] {'expert'}, dimensions={0} | all-to-all | bytes 1572864 | tf_op jit(solution)/shard_map/all_to_all | solution.py:283
  75.8 3.8 %all-to-all-start.3 = ((bf16[32,6,2,8,256]{4,3,2,1,0:T(8,128)(2,1)}), bf16[32,6,2,8,256]{4,3,2,1,0:T(8,128)(2,1)S(1)}, u32[]{:S(2)}, u32[]{:S(2)}) async-start(bf16[32,6,2,8,256]{4,3,2,1,0:T(8,128)(2,1)} %copy-done.1), calls=%async_computation.3 | async-start | bytes 3145728 | tf_op jit(solution)/shard_map/all_to_all | solution.py:283
  80.7 1.9 %collective-permute-start.8 = (bf16[16,6,8,256]{3,2,1,0:T(8,128)(2,1)S(1)}, bf16[16,6,8,256]{3,2,1,0:T(8,128)(2,1)S(1)}, u32[]{:S(2)}, u32[]{:S(2)}) collective-permute-start(bf16[16,6,8,256]{3,2,1,0:T(8,128)(2,1)S(1)} %get-tuple-element.56), channel_id=1, source_target_pairs={{0,96},{32,0},{64,32},{96,64},{1,97},{33,1},{65,33},{97,65},{2,98}... | collective-permute-start | bytes 1179656 | tf_op jit(solution)/shard_map/ppermute | solution.py:275
  82.6 2.7 %collective-permute-start.10 = (bf16[16,6,8,256]{3,2,1,0:T(8,128)(2,1)S(1)}, bf16[16,6,8,256]{3,2,1,0:T(8,128)(2,1)S(1)}, u32[]{:S(2)}, u32[]{:S(2)}) collective-permute-start(bf16[16,6,8,256]{3,2,1,0:T(8,128)(2,1)S(1)} %get-tuple-element.57), channel_id=1, source_target_pairs={{0,96},{32,0},{64,32},{96,64},{1,97},{33,1},{65,33},{97,65},{2,98}... | collective-permute-start | bytes 1179656 | tf_op jit(solution)/shard_map/ppermute | solution.py:275
  85.3 6.3 %collective-permute-done.6.a_ref = bf16[16,6,8,256]{3,2,1,0:T(8,128)(2,1)S(1)} collective-permute-done((bf16[16,6,8,256]{3,2,1,0:T(8,128)(2,1)S(1)}, bf16[16,6,8,256]{3,2,1,0:T(8,128)(2,1)S(1)}, u32[]{:S(2)}, u32[]{:S(2)}) %collective-permute-start.6) | collective-permute-done | bytes 393248 | tf_op jit(solution)/shard_map/ppermute | solution.py:271
  91.6 2.7 %collective-permute-start.9 = (bf16[16,6,8,256]{3,2,1,0:T(8,128)(2,1)S(1)}, bf16[16,6,8,256]{3,2,1,0:T(8,128)(2,1)}, u32[]{:S(2)}, u32[]{:S(2)}) collective-permute-start(bf16[16,6,8,256]{3,2,1,0:T(8,128)(2,1)S(1)} %collective-permute-done.8.b_ref), channel_id=1, source_target_pairs={{0,96},{32,0},{64,32},{96,64},{1,97},{33,1},{65,33},{97,65},{2,98}... | collective-permute-start | bytes 1179656 | tf_op jit(solution)/shard_map/ppermute | solution.py:275
  94.3 1.5 %unpack_own.1 = (f32[6,128,512]{2,1,0:T(8,128)}, bf16[6,128,2048]{2,1,0:T(8,128)(2,1)}) custom-call(s32[1]{0:T(128)} %bitcast.me_ref, bf16[32,6,8,256]{3,2,1,0:T(8,128)(2,1)S(1)} %all_to_all.20.w_ref), custom_call_target="tpu_custom_call" | custom-call | tf_op jit(solution)/shard_map/unpack_own/pallas_call | solution.py:193
  95.8 4.3 %collective-permute-done.11.b_ref = bf16[16,6,8,256]{3,2,1,0:T(8,128)(2,1)S(1)} collective-permute-done((bf16[16,6,8,256]{3,2,1,0:T(8,128)(2,1)S(1)}, bf16[16,6,8,256]{3,2,1,0:T(8,128)(2,1)S(1)}, u32[]{:S(2)}, u32[]{:S(2)}) %collective-permute-start.11) | collective-permute-done | bytes 393248 | tf_op jit(solution)/shard_map/ppermute | solution.py:271
  102.3 1.8 %unpack_moments.1 = (f32[6,128,512]{2,1,0:T(8,128)}, f32[6,128,512]{2,1,0:T(8,128)}) custom-call(bf16[32,6,2,8,256]{4,3,2,1,0:T(8,128)(2,1)S(1)} %all-to-all-done.3.m_ref), custom_call_target="tpu_custom_call" | custom-call | tf_op jit(solution)/shard_map/unpack_moments/pallas_call | solution.py:225
  104.1 4.4 %collective-permute-done.7.a_ref = bf16[16,6,8,256]{3,2,1,0:T(8,128)(2,1)S(1)} collective-permute-done((bf16[16,6,8,256]{3,2,1,0:T(8,128)(2,1)S(1)}, bf16[16,6,8,256]{3,2,1,0:T(8,128)(2,1)S(1)}, u32[]{:S(2)}, u32[]{:S(2)}) %collective-permute-start.7) | collective-permute-done | bytes 393248 | tf_op jit(solution)/shard_map/ppermute | solution.py:271
  108.4 1.9 %unpack_block.5 = bf16[6,128,2048]{2,1,0:T(8,128)(2,1)} custom-call(s32[1]{0:T(128)} %bitcast.me_ref, bf16[16,6,8,256]{3,2,1,0:T(8,128)(2,1)S(1)} %collective-permute-done.7.a_ref, bf16[16,6,8,256]{3,2,1,0:T(8,128)(2,1)} %collective-permute-done.9.b_ref, bf16[6,128,2048]{2,1,0:T(8,128)(2,1)} %unpack_block.4.old_ref), custom_call_target="tpu_custom_call", output_to_operand_aliasing={{}: (3, {})} | custom-call | tf_op jit(solution)/shard_map/unpack_block/pallas_call | solution.py:251
  (29 shorter events, 6.1 us)
Async XLA Ops:
  3.4 8.8 %copy-start = (bf16[1,4,128,2048]{3,2,1,0:T(8,128)(2,1)S(1)}, bf16[1,4,128,2048]{3,2,1,0:T(8,128)(2,1)}, u32[]{:S(2)}) copy-start(bf16[1,4,128,2048]{3,2,1,0:T(8,128)(2,1)} %param.6) | copy-start | bytes 6291460
  3.5 31.5 %all-to-all-start = ((bf16[32,4,3,8,256]{4,3,2,1,0:T(8,128)(2,1)}), bf16[32,4,3,8,256]{4,3,2,1,0:T(8,128)(2,1)}, u32[]{:S(2)}, u32[]{:S(2)}) async-start(bf16[32,4,3,8,256]{4,3,2,1,0:T(8,128)(2,1)} %pack_state.1), calls=%async_computation | async-start | bytes 3145728 | tf_op jit(solution)/shard_map/all_to_all | solution.py:283
  12.4 10.4 %collective-permute-start = (bf16[16,4,8,256]{3,2,1,0:T(8,128)(2,1)S(1)}, bf16[16,4,8,256]{3,2,1,0:T(8,128)(2,1)S(1)}, u32[]{:S(2)}, u32[]{:S(2)}) collective-permute-start(bf16[16,4,8,256]{3,2,1,0:T(8,128)(2,1)S(1)} %get-tuple-element.33), channel_id=1, source_target_pairs={{0,32},{32,64},{64,96},{96,0},{1,33},{33,65},{65,97},{97,1},{2,34}... | collective-permute-start | bytes 786440 | tf_op jit(solution)/shard_map/ppermute | solution.py:271
  14.1 8.9 %collective-permute-start.4 = (bf16[16,4,8,256]{3,2,1,0:T(8,128)(2,1)S(1)}, bf16[16,4,8,256]{3,2,1,0:T(8,128)(2,1)S(1)}, u32[]{:S(2)}, u32[]{:S(2)}) collective-permute-start(bf16[16,4,8,256]{3,2,1,0:T(8,128)(2,1)S(1)} %get-tuple-element.37), channel_id=1, source_target_pairs={{0,96},{32,0},{64,32},{96,64},{1,97},{33,1},{65,33},{97,65},{2,98}... | collective-permute-start | bytes 786440 | tf_op jit(solution)/shard_map/ppermute | solution.py:275
  16.7 11.8 %collective-permute-start.2 = (bf16[16,4,8,256]{3,2,1,0:T(8,128)(2,1)S(1)}, bf16[16,4,8,256]{3,2,1,0:T(8,128)(2,1)S(1)}, u32[]{:S(2)}, u32[]{:S(2)}) collective-permute-start(bf16[16,4,8,256]{3,2,1,0:T(8,128)(2,1)S(1)} %get-tuple-element.34), channel_id=1, source_target_pairs={{0,32},{32,64},{64,96},{96,0},{1,33},{33,65},{65,97},{97,1},{2,34}... | collective-permute-start | bytes 786440 | tf_op jit(solution)/shard_map/ppermute | solution.py:271
  16.7 11.7 %collective-permute-start.3 = (bf16[16,4,8,256]{3,2,1,0:T(8,128)(2,1)S(1)}, bf16[16,4,8,256]{3,2,1,0:T(8,128)(2,1)S(1)}, u32[]{:S(2)}, u32[]{:S(2)}) collective-permute-start(bf16[16,4,8,256]{3,2,1,0:T(8,128)(2,1)S(1)} %get-tuple-element.35), channel_id=1, source_target_pairs={{0,96},{32,0},{64,32},{96,64},{1,97},{33,1},{65,33},{97,65},{2,98}... | collective-permute-start | bytes 786440 | tf_op jit(solution)/shard_map/ppermute | solution.py:275
  22.9 11.1 %collective-permute-start.1 = (bf16[16,4,8,256]{3,2,1,0:T(8,128)(2,1)S(1)}, bf16[16,4,8,256]{3,2,1,0:T(8,128)(2,1)S(1)}, u32[]{:S(2)}, u32[]{:S(2)}) collective-permute-start(bf16[16,4,8,256]{3,2,1,0:T(8,128)(2,1)S(1)} %add_convert_fusion.1), channel_id=1, source_target_pairs={{0,32},{32,64},{64,96},{96,0},{1,33},{33,65},{65,97},{97,1},{2,34}... | collective-permute-start | bytes 786440 | tf_op jit(solution)/shard_map/ppermute | solution.py:271
  23.1 11.0 %collective-permute-start.5 = (bf16[16,4,8,256]{3,2,1,0:T(8,128)(2,1)S(1)}, bf16[16,4,8,256]{3,2,1,0:T(8,128)(2,1)S(1)}, u32[]{:S(2)}, u32[]{:S(2)}) collective-permute-start(bf16[16,4,8,256]{3,2,1,0:T(8,128)(2,1)S(1)} %add_convert_fusion), channel_id=1, source_target_pairs={{0,96},{32,0},{64,32},{96,64},{1,97},{33,1},{65,33},{97,65},{2,98}... | collective-permute-start | bytes 786440 | tf_op jit(solution)/shard_map/ppermute | solution.py:275
  35.0 7.8 %copy-start.2 = (s32[104]{0:T(128)S(1)}, s32[104]{0:T(128)}, u32[]{:S(2)}) copy-start(s32[104]{0:T(128)} %old_ref.1) | copy-start | bytes 1252
  35.0 7.8 %copy-start.3 = (s32[104]{0:T(128)S(1)}, s32[104]{0:T(128)}, u32[]{:S(2)}) copy-start(s32[104]{0:T(128)} %new_ref.1) | copy-start | bytes 1252
  36.0 18.4 %all-to-all-start.1 = ((bf16[32,4,8,256]{3,2,1,0:T(8,128)(2,1)}), bf16[32,4,8,256]{3,2,1,0:T(8,128)(2,1)S(1)}, u32[]{:S(2)}, u32[]{:S(2)}) async-start(bf16[32,4,8,256]{3,2,1,0:T(8,128)(2,1)} %sum_grad.1), calls=%async_computation.1 | async-start | bytes 1048576 | tf_op jit(solution)/shard_map/all_to_all | solution.py:283
  58.1 17.7 %copy-start.1 = (bf16[32,6,2,8,256]{4,3,2,1,0:T(8,128)(2,1)}, bf16[32,6,2,8,256]{4,3,2,1,0:T(8,128)(2,1)S(1)}, u32[]{:S(2)}) copy-start(bf16[32,6,2,8,256]{4,3,2,1,0:T(8,128)(2,1)S(1)} %get-tuple-element.49) | copy-start | bytes 4718596
  75.8 26.5 %all-to-all-start.3 = ((bf16[32,6,2,8,256]{4,3,2,1,0:T(8,128)(2,1)}), bf16[32,6,2,8,256]{4,3,2,1,0:T(8,128)(2,1)S(1)}, u32[]{:S(2)}, u32[]{:S(2)}) async-start(bf16[32,6,2,8,256]{4,3,2,1,0:T(8,128)(2,1)} %copy-done.1), calls=%async_computation.3 | async-start | bytes 3145728 | tf_op jit(solution)/shard_map/all_to_all | solution.py:283
  79.7 11.9 %collective-permute-start.6 = (bf16[16,6,8,256]{3,2,1,0:T(8,128)(2,1)S(1)}, bf16[16,6,8,256]{3,2,1,0:T(8,128)(2,1)S(1)}, u32[]{:S(2)}, u32[]{:S(2)}) collective-permute-start(bf16[16,6,8,256]{3,2,1,0:T(8,128)(2,1)S(1)} %get-tuple-element.57), channel_id=1, source_target_pairs={{0,32},{32,64},{64,96},{96,0},{1,33},{33,65},{65,97},{97,1},{2,34}... | collective-permute-start | bytes 1179656 | tf_op jit(solution)/shard_map/ppermute | solution.py:271
  80.7 10.9 %collective-permute-start.8 = (bf16[16,6,8,256]{3,2,1,0:T(8,128)(2,1)S(1)}, bf16[16,6,8,256]{3,2,1,0:T(8,128)(2,1)S(1)}, u32[]{:S(2)}, u32[]{:S(2)}) collective-permute-start(bf16[16,6,8,256]{3,2,1,0:T(8,128)(2,1)S(1)} %get-tuple-element.56), channel_id=1, source_target_pairs={{0,96},{32,0},{64,32},{96,64},{1,97},{33,1},{65,33},{97,65},{2,98}... | collective-permute-start | bytes 1179656 | tf_op jit(solution)/shard_map/ppermute | solution.py:275
  82.6 17.4 %collective-permute-start.11 = (bf16[16,6,8,256]{3,2,1,0:T(8,128)(2,1)S(1)}, bf16[16,6,8,256]{3,2,1,0:T(8,128)(2,1)S(1)}, u32[]{:S(2)}, u32[]{:S(2)}) collective-permute-start(bf16[16,6,8,256]{3,2,1,0:T(8,128)(2,1)S(1)} %get-tuple-element.56), channel_id=1, source_target_pairs={{0,32},{32,64},{64,96},{96,0},{1,33},{33,65},{65,97},{97,1},{2,34}... | collective-permute-start | bytes 1179656 | tf_op jit(solution)/shard_map/ppermute | solution.py:271
  82.6 18.4 %collective-permute-start.10 = (bf16[16,6,8,256]{3,2,1,0:T(8,128)(2,1)S(1)}, bf16[16,6,8,256]{3,2,1,0:T(8,128)(2,1)S(1)}, u32[]{:S(2)}, u32[]{:S(2)}) collective-permute-start(bf16[16,6,8,256]{3,2,1,0:T(8,128)(2,1)S(1)} %get-tuple-element.57), channel_id=1, source_target_pairs={{0,96},{32,0},{64,32},{96,64},{1,97},{33,1},{65,33},{97,65},{2,98}... | collective-permute-start | bytes 1179656 | tf_op jit(solution)/shard_map/ppermute | solution.py:275
  91.6 16.9 %collective-permute-start.7 = (bf16[16,6,8,256]{3,2,1,0:T(8,128)(2,1)S(1)}, bf16[16,6,8,256]{3,2,1,0:T(8,128)(2,1)S(1)}, u32[]{:S(2)}, u32[]{:S(2)}) collective-permute-start(bf16[16,6,8,256]{3,2,1,0:T(8,128)(2,1)S(1)} %collective-permute-done.6.a_ref), channel_id=1, source_target_pairs={{0,32},{32,64},{64,96},{96,0},{1,33},{33,65},{65,97},{97,1},{2,34}... | collective-permute-start | bytes 1179656 | tf_op jit(solution)/shard_map/ppermute | solution.py:271
  91.6 16.8 %collective-permute-start.9 = (bf16[16,6,8,256]{3,2,1,0:T(8,128)(2,1)S(1)}, bf16[16,6,8,256]{3,2,1,0:T(8,128)(2,1)}, u32[]{:S(2)}, u32[]{:S(2)}) collective-permute-start(bf16[16,6,8,256]{3,2,1,0:T(8,128)(2,1)S(1)} %collective-permute-done.8.b_ref), channel_id=1, source_target_pairs={{0,96},{32,0},{64,32},{96,64},{1,97},{33,1},{65,33},{97,65},{2,98}... | collective-permute-start | bytes 1179656 | tf_op jit(solution)/shard_map/ppermute | solution.py:275

commit v4 on v3

--- a/solution.py
+++ b/solution.py
@@ -18,7 +18,10 @@
 VMEM = pl.BlockSpec(memory_space=pltpu.VMEM)
 
 
-def route_kernel(old_ref, new_ref, table_ref, old_count, new_count):
+def route_kernel(old_ref, new_ref, state_ref, table_ref, staged_ref, old_count, new_count, sem):
+    load = pltpu.make_async_copy(state_ref, staged_ref, sem)
+    load.start()
+
     def clear_counts(i, _):
         old_count[i] = 0
         new_count[i] = 0
@@ -42,19 +45,27 @@
         return 0
 
     lax.fori_loop(0, old_ref.shape[0], place, 0)
-
-
-def route(old_owner, new_owner):
+    load.wait()
+
+
+def route(old_owner, new_owner, state):
     smem = pl.BlockSpec(memory_space=pltpu.SMEM)
     return pl.pallas_call(
         route_kernel,
-        out_shape=jax.ShapeDtypeStruct((PEERS * NEW,), jnp.int32),
-        in_specs=[smem, smem],
-        out_specs=smem,
-        scratch_shapes=[pltpu.SMEM((PEERS,), jnp.int32), pltpu.SMEM((PEERS,), jnp.int32)],
+        out_shape=(
+            jax.ShapeDtypeStruct((PEERS * NEW,), jnp.int32),
+            jax.ShapeDtypeStruct(state.shape, state.dtype),
+        ),
+        in_specs=[smem, smem, pl.BlockSpec(memory_space=pl.ANY)],
+        out_specs=(smem, VMEM),
+        scratch_shapes=[
+            pltpu.SMEM((PEERS,), jnp.int32),
+            pltpu.SMEM((PEERS,), jnp.int32),
+            pltpu.SemaphoreType.DMA,
+        ],
         compiler_params=PARAMS,
         name="route",
-    )(old_owner, new_owner)
+    )(old_owner, new_owner, state)
 
 
 def pack_state_kernel(m1_ref, m2_ref, w_ref, out_ref):
@@ -159,7 +170,7 @@
             moments_ref[d, s, 1] = jnp.where(has, m2, 0.0).astype(BF16)
         return 0
 
-    lax.fori_loop(0, PEERS, owner, 0)
+    lax.fori_loop(0, PEERS, owner, 0, unroll=2)
 
 
 def update(table, state, grad):
@@ -296,10 +307,10 @@
     ua, db = send_up(add(up_a, far_up)), send_down(add(down_b, far_down))
     state, ua, ub, da, db = lax.optimization_barrier((state, ua, ub, da, db))
     grad = exchange(sum_grad(own_a, own_b, ua, ub, da, db))
-    table = route(old_owner, new_owner)
+    table, state = route(old_owner, new_owner, state.reshape(PEERS * OLD, 3, PR, PC))
     weight, moments = update(
         table,
-        state.reshape(PEERS * OLD, 3, PR, PC),
+        state,
         grad.reshape(PEERS * OLD, PR, PC),
     )
     weight = exchange(weight)

time: 111 us -> 110 us (level)
  Pallas kernels: 18.5 us -> 17.3 us
    pallas_call x1, Pallas kernels: 3.73 us -> 2.52 us  [update(): pl.pallas_call(update_kernel, out_shape=(jax.ShapeDtypeStruct((PEERS, NEW...]
where the time goes in v4:
time: 110 us; the launch traced here: 109 us
  starting transfers between devices  37.1 us (34%)
  waiting for transfers between devices  36.1 us (33%)
  blocking collectives  17.7 us (16%)
  Pallas kernels  17.3 us (16%)
    ppermute x6, waiting for transfers between devices, send_up(): return lax.ppermute(x, 'dp', UP)  26.6 us
    all_to_all x3, starting transfers between devices, exchange(): lax.all_to_all(values, 'expert', split_axis=0, concat_axis=0, tiled=True)  19.4 us
    all_to_all x1, blocking collectives, exchange(): lax.all_to_all(values, 'expert', split_axis=0, concat_axis=0, tiled=True)  17.7 us
    ppermute x6, starting transfers between devices, send_down(): return lax.ppermute(x, 'dp', DOWN)  14.8 us
    all_to_all x3, waiting for transfers between devices, exchange(): lax.all_to_all(values, 'expert', split_axis=0, concat_axis=0, tiled=True)  9.47 us
    pallas_call x3, Pallas kernels, unpack_block(): pl.pallas_call(unpack_block_kernel, grid_spec=pltpu.PrefetchScalarGridSpe...  3.74 us
    pallas_call x1, Pallas kernels, route(): pl.pallas_call(route_kernel, out_shape=(jax.ShapeDtypeStruct((PEERS * NEW...  3.51 us
    ppermute x6, starting transfers between devices, send_up(): return lax.ppermute(x, 'dp', UP)  2.89 us
  transfers between devices with their start and end apart: 15, of which 9 were waited for; matrix products, arithmetic and copies ran while one was open for 0% of the time, Pallas kernels for 8%

profile of v4, /device:TPU:1, one launch (start us, length us, event | category | flops | bytes accessed | tf_op | source)
XLA Modules:
  0.0 109.2 jit_solution(12957754853567822442)
XLA Ops:
  0.6 2.8 %pack_state.1 = bf16[32,4,3,8,256]{4,3,2,1,0:T(8,128)(2,1)} custom-call(f32[4,128,512]{2,1,0:T(8,128)} %m1_ref.1, f32[4,128,512]{2,1,0:T(8,128)} %m2_ref.1, f32[4,128,512]{2,1,0:T(8,128)} %w_ref.1), custom_call_target="tpu_custom_call" | custom-call | tf_op jit(solution)/shard_map/pack_state/pallas_call | solution.py:82
  3.5 8.8 %all-to-all-start = ((bf16[32,4,3,8,256]{4,3,2,1,0:T(8,128)(2,1)}), bf16[32,4,3,8,256]{4,3,2,1,0:T(8,128)(2,1)}, u32[]{:S(2)}, u32[]{:S(2)}) async-start(bf16[32,4,3,8,256]{4,3,2,1,0:T(8,128)(2,1)} %pack_state.1), calls=%async_computation | async-start | bytes 3145728 | tf_op jit(solution)/shard_map/all_to_all | solution.py:294
  12.4 1.7 %collective-permute-start = (bf16[16,4,8,256]{3,2,1,0:T(8,128)(2,1)S(1)}, bf16[16,4,8,256]{3,2,1,0:T(8,128)(2,1)S(1)}, u32[]{:S(2)}, u32[]{:S(2)}) collective-permute-start(bf16[16,4,8,256]{3,2,1,0:T(8,128)(2,1)S(1)} %get-tuple-element.35), channel_id=1, source_target_pairs={{0,32},{32,64},{64,96},{96,0},{1,33},{33,65},{65,97},{97,1},{2,34}... | collective-permute-start | bytes 786440 | tf_op jit(solution)/shard_map/ppermute | solution.py:282
  14.1 2.2 %collective-permute-start.4 = (bf16[16,4,8,256]{3,2,1,0:T(8,128)(2,1)S(1)}, bf16[16,4,8,256]{3,2,1,0:T(8,128)(2,1)S(1)}, u32[]{:S(2)}, u32[]{:S(2)}) collective-permute-start(bf16[16,4,8,256]{3,2,1,0:T(8,128)(2,1)S(1)} %get-tuple-element.39), channel_id=1, source_target_pairs={{0,96},{32,0},{64,32},{96,64},{1,97},{33,1},{65,33},{97,65},{2,98}... | collective-permute-start | bytes 786440 | tf_op jit(solution)/shard_map/ppermute | solution.py:286
  16.7 2.7 %collective-permute-start.3 = (bf16[16,4,8,256]{3,2,1,0:T(8,128)(2,1)S(1)}, bf16[16,4,8,256]{3,2,1,0:T(8,128)(2,1)S(1)}, u32[]{:S(2)}, u32[]{:S(2)}) collective-permute-start(bf16[16,4,8,256]{3,2,1,0:T(8,128)(2,1)S(1)} %get-tuple-element.37), channel_id=1, source_target_pairs={{0,96},{32,0},{64,32},{96,64},{1,97},{33,1},{65,33},{97,65},{2,98}... | collective-permute-start | bytes 786440 | tf_op jit(solution)/shard_map/ppermute | solution.py:286
  19.4 3.4 %collective-permute-done = bf16[16,4,8,256]{3,2,1,0:T(8,128)(2,1)S(1)} collective-permute-done((bf16[16,4,8,256]{3,2,1,0:T(8,128)(2,1)S(1)}, bf16[16,4,8,256]{3,2,1,0:T(8,128)(2,1)S(1)}, u32[]{:S(2)}, u32[]{:S(2)}) %collective-permute-start) | collective-permute-done | bytes 262176 | tf_op jit(solution)/shard_map/ppermute | solution.py:282
  23.1 2.7 %collective-permute-start.5 = (bf16[16,4,8,256]{3,2,1,0:T(8,128)(2,1)S(1)}, bf16[16,4,8,256]{3,2,1,0:T(8,128)(2,1)S(1)}, u32[]{:S(2)}, u32[]{:S(2)}) collective-permute-start(bf16[16,4,8,256]{3,2,1,0:T(8,128)(2,1)S(1)} %add_convert_fusion), channel_id=1, source_target_pairs={{0,96},{32,0},{64,32},{96,64},{1,97},{33,1},{65,33},{97,65},{2,98}... | collective-permute-start | bytes 786440 | tf_op jit(solution)/shard_map/ppermute | solution.py:286
  25.8 2.6 %collective-permute-done.2.ub = bf16[16,4,8,256]{3,2,1,0:T(8,128)(2,1)S(1)} collective-permute-done((bf16[16,4,8,256]{3,2,1,0:T(8,128)(2,1)S(1)}, bf16[16,4,8,256]{3,2,1,0:T(8,128)(2,1)S(1)}, u32[]{:S(2)}, u32[]{:S(2)}) %collective-permute-start.2) | collective-permute-done | bytes 262176 | tf_op jit(solution)/shard_map/ppermute | solution.py:282
  28.4 5.6 %collective-permute-done.1.ua = bf16[16,4,8,256]{3,2,1,0:T(8,128)(2,1)S(1)} collective-permute-done((bf16[16,4,8,256]{3,2,1,0:T(8,128)(2,1)S(1)}, bf16[16,4,8,256]{3,2,1,0:T(8,128)(2,1)S(1)}, u32[]{:S(2)}, u32[]{:S(2)}) %collective-permute-start.1) | collective-permute-done | bytes 262176 | tf_op jit(solution)/shard_map/ppermute | solution.py:282
  36.0 6.8 %all-to-all-start.1 = ((bf16[32,4,8,256]{3,2,1,0:T(8,128)(2,1)}), bf16[32,4,8,256]{3,2,1,0:T(8,128)(2,1)S(1)}, u32[]{:S(2)}, u32[]{:S(2)}) async-start(bf16[32,4,8,256]{3,2,1,0:T(8,128)(2,1)} %sum_grad.1), calls=%async_computation.1 | async-start | bytes 1048576 | tf_op jit(solution)/shard_map/all_to_all | solution.py:294
  42.8 3.5 %route.1 = (s32[192]{0:T(256)S(1)}, bf16[128,3,8,256]{3,2,1,0:T(8,128)(2,1)S(1)}) custom-call(s32[104]{0:T(128)S(1)} %copy-done.2, s32[104]{0:T(128)S(1)} %copy-done.3, bf16[128,3,8,256]{3,2,1,0:T(8,128)(2,1)} %bitcast.2.state_ref), custom_call_target="tpu_custom_call" | custom-call | tf_op jit(solution)/shard_map/route/pallas_call | solution.py:53
  46.3 8.1 %all-to-all-done.1 = bf16[32,4,8,256]{3,2,1,0:T(8,128)(2,1)S(1)} async-done(((bf16[32,4,8,256]{3,2,1,0:T(8,128)(2,1)}), bf16[32,4,8,256]{3,2,1,0:T(8,128)(2,1)S(1)}, u32[]{:S(2)}, u32[]{:S(2)}) %all-to-all-start.1) | async-done | bytes 524320 | tf_op jit(solution)/shard_map/all_to_all | solution.py:294
  54.4 2.5 %update.1 = (bf16[32,6,8,256]{3,2,1,0:T(8,128)(2,1)S(1)}, bf16[32,6,2,8,256]{4,3,2,1,0:T(8,128)(2,1)S(1)}) custom-call(s32[192]{0:T(256)S(1)} %get-tuple-element.41.table_ref, bf16[128,3,8,256]{3,2,1,0:T(8,128)(2,1)S(1)} %get-tuple-element.42.state_ref, bf16[128,8,256]{2,1,0:T(8,128)(2,1)S(1)} %bitcast.8), custom_call_target="tpu_custom_call" | custom-call | tf_op jit(solution)/shard_map/update/pallas_call | solution.py:178
  56.9 17.7 %all_to_all.20.w_ref = bf16[32,6,8,256]{3,2,1,0:T(8,128)(2,1)S(1)} all-to-all(bf16[32,6,8,256]{3,2,1,0:T(8,128)(2,1)S(1)} %get-tuple-element.49), channel_id=1, replica_groups=mesh['dp'=4,'expert'=32] {'expert'}, dimensions={0} | all-to-all | bytes 1572864 | tf_op jit(solution)/shard_map/all_to_all | solution.py:294
  74.6 3.8 %all-to-all-start.3 = ((bf16[32,6,2,8,256]{4,3,2,1,0:T(8,128)(2,1)}), bf16[32,6,2,8,256]{4,3,2,1,0:T(8,128)(2,1)S(1)}, u32[]{:S(2)}, u32[]{:S(2)}) async-start(bf16[32,6,2,8,256]{4,3,2,1,0:T(8,128)(2,1)} %copy-done.1), calls=%async_computation.3 | async-start | bytes 3145728 | tf_op jit(solution)/shard_map/all_to_all | solution.py:294
  79.5 1.9 %collective-permute-start.8 = (bf16[16,6,8,256]{3,2,1,0:T(8,128)(2,1)S(1)}, bf16[16,6,8,256]{3,2,1,0:T(8,128)(2,1)S(1)}, u32[]{:S(2)}, u32[]{:S(2)}) collective-permute-start(bf16[16,6,8,256]{3,2,1,0:T(8,128)(2,1)S(1)} %get-tuple-element.60), channel_id=1, source_target_pairs={{0,96},{32,0},{64,32},{96,64},{1,97},{33,1},{65,33},{97,65},{2,98}... | collective-permute-start | bytes 1179656 | tf_op jit(solution)/shard_map/ppermute | solution.py:286
  81.4 2.7 %collective-permute-start.10 = (bf16[16,6,8,256]{3,2,1,0:T(8,128)(2,1)S(1)}, bf16[16,6,8,256]{3,2,1,0:T(8,128)(2,1)S(1)}, u32[]{:S(2)}, u32[]{:S(2)}) collective-permute-start(bf16[16,6,8,256]{3,2,1,0:T(8,128)(2,1)S(1)} %get-tuple-element.61), channel_id=1, source_target_pairs={{0,96},{32,0},{64,32},{96,64},{1,97},{33,1},{65,33},{97,65},{2,98}... | collective-permute-start | bytes 1179656 | tf_op jit(solution)/shard_map/ppermute | solution.py:286
  84.1 6.3 %collective-permute-done.6.a_ref = bf16[16,6,8,256]{3,2,1,0:T(8,128)(2,1)S(1)} collective-permute-done((bf16[16,6,8,256]{3,2,1,0:T(8,128)(2,1)S(1)}, bf16[16,6,8,256]{3,2,1,0:T(8,128)(2,1)S(1)}, u32[]{:S(2)}, u32[]{:S(2)}) %collective-permute-start.6) | collective-permute-done | bytes 393248 | tf_op jit(solution)/shard_map/ppermute | solution.py:282
  90.4 2.7 %collective-permute-start.9 = (bf16[16,6,8,256]{3,2,1,0:T(8,128)(2,1)S(1)}, bf16[16,6,8,256]{3,2,1,0:T(8,128)(2,1)}, u32[]{:S(2)}, u32[]{:S(2)}) collective-permute-start(bf16[16,6,8,256]{3,2,1,0:T(8,128)(2,1)S(1)} %collective-permute-done.8.b_ref), channel_id=1, source_target_pairs={{0,96},{32,0},{64,32},{96,64},{1,97},{33,1},{65,33},{97,65},{2,98}... | collective-permute-start | bytes 1179656 | tf_op jit(solution)/shard_map/ppermute | solution.py:286
  93.1 1.5 %unpack_own.1 = (f32[6,128,512]{2,1,0:T(8,128)}, bf16[6,128,2048]{2,1,0:T(8,128)(2,1)}) custom-call(s32[1]{0:T(128)} %bitcast.me_ref, bf16[32,6,8,256]{3,2,1,0:T(8,128)(2,1)S(1)} %all_to_all.20.w_ref), custom_call_target="tpu_custom_call" | custom-call | tf_op jit(solution)/shard_map/unpack_own/pallas_call | solution.py:204
  94.5 4.3 %collective-permute-done.11.b_ref = bf16[16,6,8,256]{3,2,1,0:T(8,128)(2,1)S(1)} collective-permute-done((bf16[16,6,8,256]{3,2,1,0:T(8,128)(2,1)S(1)}, bf16[16,6,8,256]{3,2,1,0:T(8,128)(2,1)S(1)}, u32[]{:S(2)}, u32[]{:S(2)}) %collective-permute-start.11) | collective-permute-done | bytes 393248 | tf_op jit(solution)/shard_map/ppermute | solution.py:282
  101.1 1.8 %unpack_moments.1 = (f32[6,128,512]{2,1,0:T(8,128)}, f32[6,128,512]{2,1,0:T(8,128)}) custom-call(bf16[32,6,2,8,256]{4,3,2,1,0:T(8,128)(2,1)S(1)} %all-to-all-done.3.m_ref), custom_call_target="tpu_custom_call" | custom-call | tf_op jit(solution)/shard_map/unpack_moments/pallas_call | solution.py:236
  102.9 4.4 %collective-permute-done.7.a_ref = bf16[16,6,8,256]{3,2,1,0:T(8,128)(2,1)S(1)} collective-permute-done((bf16[16,6,8,256]{3,2,1,0:T(8,128)(2,1)S(1)}, bf16[16,6,8,256]{3,2,1,0:T(8,128)(2,1)S(1)}, u32[]{:S(2)}, u32[]{:S(2)}) %collective-permute-start.7) | collective-permute-done | bytes 393248 | tf_op jit(solution)/shard_map/ppermute | solution.py:282
  107.2 1.9 %unpack_block.5 = bf16[6,128,2048]{2,1,0:T(8,128)(2,1)} custom-call(s32[1]{0:T(128)} %bitcast.me_ref, bf16[16,6,8,256]{3,2,1,0:T(8,128)(2,1)S(1)} %collective-permute-done.7.a_ref, bf16[16,6,8,256]{3,2,1,0:T(8,128)(2,1)} %collective-permute-done.9.b_ref, bf16[6,128,2048]{2,1,0:T(8,128)(2,1)} %unpack_block.4.old_ref), custom_call_target="tpu_custom_call", output_to_operand_aliasing={{}: (3, {})} | custom-call | tf_op jit(solution)/shard_map/unpack_block/pallas_call | solution.py:262
  (29 shorter events, 6.1 us)
Async XLA Ops:
  3.4 8.8 %copy-start = (bf16[1,4,128,2048]{3,2,1,0:T(8,128)(2,1)S(1)}, bf16[1,4,128,2048]{3,2,1,0:T(8,128)(2,1)}, u32[]{:S(2)}) copy-start(bf16[1,4,128,2048]{3,2,1,0:T(8,128)(2,1)} %param.6) | copy-start | bytes 6291460
  3.5 31.5 %all-to-all-start = ((bf16[32,4,3,8,256]{4,3,2,1,0:T(8,128)(2,1)}), bf16[32,4,3,8,256]{4,3,2,1,0:T(8,128)(2,1)}, u32[]{:S(2)}, u32[]{:S(2)}) async-start(bf16[32,4,3,8,256]{4,3,2,1,0:T(8,128)(2,1)} %pack_state.1), calls=%async_computation | async-start | bytes 3145728 | tf_op jit(solution)/shard_map/all_to_all | solution.py:294
  12.4 10.4 %collective-permute-start = (bf16[16,4,8,256]{3,2,1,0:T(8,128)(2,1)S(1)}, bf16[16,4,8,256]{3,2,1,0:T(8,128)(2,1)S(1)}, u32[]{:S(2)}, u32[]{:S(2)}) collective-permute-start(bf16[16,4,8,256]{3,2,1,0:T(8,128)(2,1)S(1)} %get-tuple-element.35), channel_id=1, source_target_pairs={{0,32},{32,64},{64,96},{96,0},{1,33},{33,65},{65,97},{97,1},{2,34}... | collective-permute-start | bytes 786440 | tf_op jit(solution)/shard_map/ppermute | solution.py:282
  14.1 8.9 %collective-permute-start.4 = (bf16[16,4,8,256]{3,2,1,0:T(8,128)(2,1)S(1)}, bf16[16,4,8,256]{3,2,1,0:T(8,128)(2,1)S(1)}, u32[]{:S(2)}, u32[]{:S(2)}) collective-permute-start(bf16[16,4,8,256]{3,2,1,0:T(8,128)(2,1)S(1)} %get-tuple-element.39), channel_id=1, source_target_pairs={{0,96},{32,0},{64,32},{96,64},{1,97},{33,1},{65,33},{97,65},{2,98}... | collective-permute-start | bytes 786440 | tf_op jit(solution)/shard_map/ppermute | solution.py:286
  16.7 11.8 %collective-permute-start.2 = (bf16[16,4,8,256]{3,2,1,0:T(8,128)(2,1)S(1)}, bf16[16,4,8,256]{3,2,1,0:T(8,128)(2,1)S(1)}, u32[]{:S(2)}, u32[]{:S(2)}) collective-permute-start(bf16[16,4,8,256]{3,2,1,0:T(8,128)(2,1)S(1)} %get-tuple-element.36), channel_id=1, source_target_pairs={{0,32},{32,64},{64,96},{96,0},{1,33},{33,65},{65,97},{97,1},{2,34}... | collective-permute-start | bytes 786440 | tf_op jit(solution)/shard_map/ppermute | solution.py:282
  16.7 11.7 %collective-permute-start.3 = (bf16[16,4,8,256]{3,2,1,0:T(8,128)(2,1)S(1)}, bf16[16,4,8,256]{3,2,1,0:T(8,128)(2,1)S(1)}, u32[]{:S(2)}, u32[]{:S(2)}) collective-permute-start(bf16[16,4,8,256]{3,2,1,0:T(8,128)(2,1)S(1)} %get-tuple-element.37), channel_id=1, source_target_pairs={{0,96},{32,0},{64,32},{96,64},{1,97},{33,1},{65,33},{97,65},{2,98}... | collective-permute-start | bytes 786440 | tf_op jit(solution)/shard_map/ppermute | solution.py:286
  22.9 11.1 %collective-permute-start.1 = (bf16[16,4,8,256]{3,2,1,0:T(8,128)(2,1)S(1)}, bf16[16,4,8,256]{3,2,1,0:T(8,128)(2,1)S(1)}, u32[]{:S(2)}, u32[]{:S(2)}) collective-permute-start(bf16[16,4,8,256]{3,2,1,0:T(8,128)(2,1)S(1)} %add_convert_fusion.1), channel_id=1, source_target_pairs={{0,32},{32,64},{64,96},{96,0},{1,33},{33,65},{65,97},{97,1},{2,34}... | collective-permute-start | bytes 786440 | tf_op jit(solution)/shard_map/ppermute | solution.py:282
  23.1 11.0 %collective-permute-start.5 = (bf16[16,4,8,256]{3,2,1,0:T(8,128)(2,1)S(1)}, bf16[16,4,8,256]{3,2,1,0:T(8,128)(2,1)S(1)}, u32[]{:S(2)}, u32[]{:S(2)}) collective-permute-start(bf16[16,4,8,256]{3,2,1,0:T(8,128)(2,1)S(1)} %add_convert_fusion), channel_id=1, source_target_pairs={{0,96},{32,0},{64,32},{96,64},{1,97},{33,1},{65,33},{97,65},{2,98}... | collective-permute-start | bytes 786440 | tf_op jit(solution)/shard_map/ppermute | solution.py:286
  35.0 7.8 %copy-start.2 = (s32[104]{0:T(128)S(1)}, s32[104]{0:T(128)}, u32[]{:S(2)}) copy-start(s32[104]{0:T(128)} %old_ref.1) | copy-start | bytes 1252
  35.0 7.8 %copy-start.3 = (s32[104]{0:T(128)S(1)}, s32[104]{0:T(128)}, u32[]{:S(2)}) copy-start(s32[104]{0:T(128)} %new_ref.1) | copy-start | bytes 1252
  36.0 18.4 %all-to-all-start.1 = ((bf16[32,4,8,256]{3,2,1,0:T(8,128)(2,1)}), bf16[32,4,8,256]{3,2,1,0:T(8,128)(2,1)S(1)}, u32[]{:S(2)}, u32[]{:S(2)}) async-start(bf16[32,4,8,256]{3,2,1,0:T(8,128)(2,1)} %sum_grad.1), calls=%async_computation.1 | async-start | bytes 1048576 | tf_op jit(solution)/shard_map/all_to_all | solution.py:294
  56.9 17.7 %copy-start.1 = (bf16[32,6,2,8,256]{4,3,2,1,0:T(8,128)(2,1)}, bf16[32,6,2,8,256]{4,3,2,1,0:T(8,128)(2,1)S(1)}, u32[]{:S(2)}) copy-start(bf16[32,6,2,8,256]{4,3,2,1,0:T(8,128)(2,1)S(1)} %get-tuple-element.53) | copy-start | bytes 4718596
  74.6 26.5 %all-to-all-start.3 = ((bf16[32,6,2,8,256]{4,3,2,1,0:T(8,128)(2,1)}), bf16[32,6,2,8,256]{4,3,2,1,0:T(8,128)(2,1)S(1)}, u32[]{:S(2)}, u32[]{:S(2)}) async-start(bf16[32,6,2,8,256]{4,3,2,1,0:T(8,128)(2,1)} %copy-done.1), calls=%async_computation.3 | async-start | bytes 3145728 | tf_op jit(solution)/shard_map/all_to_all | solution.py:294
  78.5 11.9 %collective-permute-start.6 = (bf16[16,6,8,256]{3,2,1,0:T(8,128)(2,1)S(1)}, bf16[16,6,8,256]{3,2,1,0:T(8,128)(2,1)S(1)}, u32[]{:S(2)}, u32[]{:S(2)}) collective-permute-start(bf16[16,6,8,256]{3,2,1,0:T(8,128)(2,1)S(1)} %get-tuple-element.61), channel_id=1, source_target_pairs={{0,32},{32,64},{64,96},{96,0},{1,33},{33,65},{65,97},{97,1},{2,34}... | collective-permute-start | bytes 1179656 | tf_op jit(solution)/shard_map/ppermute | solution.py:282
  79.5 10.9 %collective-permute-start.8 = (bf16[16,6,8,256]{3,2,1,0:T(8,128)(2,1)S(1)}, bf16[16,6,8,256]{3,2,1,0:T(8,128)(2,1)S(1)}, u32[]{:S(2)}, u32[]{:S(2)}) collective-permute-start(bf16[16,6,8,256]{3,2,1,0:T(8,128)(2,1)S(1)} %get-tuple-element.60), channel_id=1, source_target_pairs={{0,96},{32,0},{64,32},{96,64},{1,97},{33,1},{65,33},{97,65},{2,98}... | collective-permute-start | bytes 1179656 | tf_op jit(solution)/shard_map/ppermute | solution.py:286
  81.4 17.4 %collective-permute-start.11 = (bf16[16,6,8,256]{3,2,1,0:T(8,128)(2,1)S(1)}, bf16[16,6,8,256]{3,2,1,0:T(8,128)(2,1)S(1)}, u32[]{:S(2)}, u32[]{:S(2)}) collective-permute-start(bf16[16,6,8,256]{3,2,1,0:T(8,128)(2,1)S(1)} %get-tuple-element.60), channel_id=1, source_target_pairs={{0,32},{32,64},{64,96},{96,0},{1,33},{33,65},{65,97},{97,1},{2,34}... | collective-permute-start | bytes 1179656 | tf_op jit(solution)/shard_map/ppermute | solution.py:282
  81.4 18.4 %collective-permute-start.10 = (bf16[16,6,8,256]{3,2,1,0:T(8,128)(2,1)S(1)}, bf16[16,6,8,256]{3,2,1,0:T(8,128)(2,1)S(1)}, u32[]{:S(2)}, u32[]{:S(2)}) collective-permute-start(bf16[16,6,8,256]{3,2,1,0:T(8,128)(2,1)S(1)} %get-tuple-element.61), channel_id=1, source_target_pairs={{0,96},{32,0},{64,32},{96,64},{1,97},{33,1},{65,33},{97,65},{2,98}... | collective-permute-start | bytes 1179656 | tf_op jit(solution)/shard_map/ppermute | solution.py:286
  90.4 16.9 %collective-permute-start.7 = (bf16[16,6,8,256]{3,2,1,0:T(8,128)(2,1)S(1)}, bf16[16,6,8,256]{3,2,1,0:T(8,128)(2,1)S(1)}, u32[]{:S(2)}, u32[]{:S(2)}) collective-permute-start(bf16[16,6,8,256]{3,2,1,0:T(8,128)(2,1)S(1)} %collective-permute-done.6.a_ref), channel_id=1, source_target_pairs={{0,32},{32,64},{64,96},{96,0},{1,33},{33,65},{65,97},{97,1},{2,34}... | collective-permute-start | bytes 1179656 | tf_op jit(solution)/shard_map/ppermute | solution.py:282
  90.4 16.8 %collective-permute-start.9 = (bf16[16,6,8,256]{3,2,1,0:T(8,128)(2,1)S(1)}, bf16[16,6,8,256]{3,2,1,0:T(8,128)(2,1)}, u32[]{:S(2)}, u32[]{:S(2)}) collective-permute-start(bf16[16,6,8,256]{3,2,1,0:T(8,128)(2,1)S(1)} %collective-permute-done.8.b_ref), channel_id=1, source_target_pairs={{0,96},{32,0},{64,32},{96,64},{1,97},{33,1},{65,33},{97,65},{2,98}... | collective-permute-start | bytes 1179656 | tf_op jit(solution)/shard_map/ppermute | solution.py:286

commit v5 on v4

--- a/solution.py
+++ b/solution.py
@@ -318,9 +318,10 @@
     wa, wb = weight[: PEERS // 2], weight[PEERS // 2 :]
     ua, da = send_up(wa), send_down(wa)
     ub, db = send_up(wb), send_down(wb)
-    fa, fb = send_up(ua), send_down(db)
     moments = exchange(moments)
     new_master, params = unpack_own(me, weight)
+    far_up, far_down, params = lax.optimization_barrier((ua, db, params))
+    fa, fb = send_up(far_up), send_down(far_down)
     params = unpack_block(me, ua, ub, params, 3)
     params = unpack_block(me, da, db, params, 1)
     new_first, new_second = unpack_moments(moments)

time: 110 us -> 109 us (level)
  no operation moved by 1% of the time
where the time goes in v5:
time: 109 us; the launch traced here: 108 us
  starting transfers between devices  37.1 us (34%)
  waiting for transfers between devices  36.1 us (33%)
  blocking collectives  17.7 us (16%)
  Pallas kernels  16.3 us (15%)
    ppermute x6, waiting for transfers between devices, send_up(): return lax.ppermute(x, 'dp', UP)  26.6 us
    all_to_all x3, starting transfers between devices, exchange(): lax.all_to_all(values, 'expert', split_axis=0, concat_axis=0, tiled=True)  19.4 us
    all_to_all x1, blocking collectives, exchange(): lax.all_to_all(values, 'expert', split_axis=0, concat_axis=0, tiled=True)  17.7 us
    ppermute x6, starting transfers between devices, send_down(): return lax.ppermute(x, 'dp', DOWN)  14.2 us
    all_to_all x3, waiting for transfers between devices, exchange(): lax.all_to_all(values, 'expert', split_axis=0, concat_axis=0, tiled=True)  9.47 us
    ppermute x6, starting transfers between devices, send_up(): return lax.ppermute(x, 'dp', UP)  3.53 us
    pallas_call x1, Pallas kernels, route(): pl.pallas_call(route_kernel, out_shape=(jax.ShapeDtypeStruct((PEERS * NEW...  3.51 us
    pallas_call x1, Pallas kernels, pack_state(): pl.pallas_call(pack_state_kernel, grid=(STEPS,), out_shape=jax.ShapeDtype...  2.82 us
  transfers between devices with their start and end apart: 15, of which 9 were waited for; matrix products, arithmetic and copies ran while one was open for 0% of the time, Pallas kernels for 8%

profile of v5, /device:TPU:1, one launch (start us, length us, event | category | flops | bytes accessed | tf_op | source)
XLA Modules:
  0.0 108.2 jit_solution(10535850871502688086)
XLA Ops:
  0.6 2.8 %pack_state.1 = bf16[32,4,3,8,256]{4,3,2,1,0:T(8,128)(2,1)} custom-call(f32[4,128,512]{2,1,0:T(8,128)} %m1_ref.1, f32[4,128,512]{2,1,0:T(8,128)} %m2_ref.1, f32[4,128,512]{2,1,0:T(8,128)} %w_ref.1), custom_call_target="tpu_custom_call" | custom-call | tf_op jit(solution)/shard_map/pack_state/pallas_call | solution.py:82
  3.5 8.8 %all-to-all-start = ((bf16[32,4,3,8,256]{4,3,2,1,0:T(8,128)(2,1)}), bf16[32,4,3,8,256]{4,3,2,1,0:T(8,128)(2,1)}, u32[]{:S(2)}, u32[]{:S(2)}) async-start(bf16[32,4,3,8,256]{4,3,2,1,0:T(8,128)(2,1)} %pack_state.1), calls=%async_computation | async-start | bytes 3145728 | tf_op jit(solution)/shard_map/all_to_all | solution.py:294
  12.4 1.7 %collective-permute-start = (bf16[16,4,8,256]{3,2,1,0:T(8,128)(2,1)S(1)}, bf16[16,4,8,256]{3,2,1,0:T(8,128)(2,1)S(1)}, u32[]{:S(2)}, u32[]{:S(2)}) collective-permute-start(bf16[16,4,8,256]{3,2,1,0:T(8,128)(2,1)S(1)} %get-tuple-element.38), channel_id=1, source_target_pairs={{0,32},{32,64},{64,96},{96,0},{1,33},{33,65},{65,97},{97,1},{2,34}... | collective-permute-start | bytes 786440 | tf_op jit(solution)/shard_map/ppermute | solution.py:282
  14.1 2.2 %collective-permute-start.4 = (bf16[16,4,8,256]{3,2,1,0:T(8,128)(2,1)S(1)}, bf16[16,4,8,256]{3,2,1,0:T(8,128)(2,1)S(1)}, u32[]{:S(2)}, u32[]{:S(2)}) collective-permute-start(bf16[16,4,8,256]{3,2,1,0:T(8,128)(2,1)S(1)} %get-tuple-element.42), channel_id=1, source_target_pairs={{0,96},{32,0},{64,32},{96,64},{1,97},{33,1},{65,33},{97,65},{2,98}... | collective-permute-start | bytes 786440 | tf_op jit(solution)/shard_map/ppermute | solution.py:286
  16.7 2.7 %collective-permute-start.3 = (bf16[16,4,8,256]{3,2,1,0:T(8,128)(2,1)S(1)}, bf16[16,4,8,256]{3,2,1,0:T(8,128)(2,1)S(1)}, u32[]{:S(2)}, u32[]{:S(2)}) collective-permute-start(bf16[16,4,8,256]{3,2,1,0:T(8,128)(2,1)S(1)} %get-tuple-element.40), channel_id=1, source_target_pairs={{0,96},{32,0},{64,32},{96,64},{1,97},{33,1},{65,33},{97,65},{2,98}... | collective-permute-start | bytes 786440 | tf_op jit(solution)/shard_map/ppermute | solution.py:286
  19.4 3.4 %collective-permute-done = bf16[16,4,8,256]{3,2,1,0:T(8,128)(2,1)S(1)} collective-permute-done((bf16[16,4,8,256]{3,2,1,0:T(8,128)(2,1)S(1)}, bf16[16,4,8,256]{3,2,1,0:T(8,128)(2,1)S(1)}, u32[]{:S(2)}, u32[]{:S(2)}) %collective-permute-start) | collective-permute-done | bytes 262176 | tf_op jit(solution)/shard_map/ppermute | solution.py:282
  23.1 2.7 %collective-permute-start.5 = (bf16[16,4,8,256]{3,2,1,0:T(8,128)(2,1)S(1)}, bf16[16,4,8,256]{3,2,1,0:T(8,128)(2,1)S(1)}, u32[]{:S(2)}, u32[]{:S(2)}) collective-permute-start(bf16[16,4,8,256]{3,2,1,0:T(8,128)(2,1)S(1)} %add_convert_fusion), channel_id=1, source_target_pairs={{0,96},{32,0},{64,32},{96,64},{1,97},{33,1},{65,33},{97,65},{2,98}... | collective-permute-start | bytes 786440 | tf_op jit(solution)/shard_map/ppermute | solution.py:286
  25.8 2.6 %collective-permute-done.2.ub = bf16[16,4,8,256]{3,2,1,0:T(8,128)(2,1)S(1)} collective-permute-done((bf16[16,4,8,256]{3,2,1,0:T(8,128)(2,1)S(1)}, bf16[16,4,8,256]{3,2,1,0:T(8,128)(2,1)S(1)}, u32[]{:S(2)}, u32[]{:S(2)}) %collective-permute-start.2) | collective-permute-done | bytes 262176 | tf_op jit(solution)/shard_map/ppermute | solution.py:282
  28.4 5.6 %collective-permute-done.1.ua = bf16[16,4,8,256]{3,2,1,0:T(8,128)(2,1)S(1)} collective-permute-done((bf16[16,4,8,256]{3,2,1,0:T(8,128)(2,1)S(1)}, bf16[16,4,8,256]{3,2,1,0:T(8,128)(2,1)S(1)}, u32[]{:S(2)}, u32[]{:S(2)}) %collective-permute-start.1) | collective-permute-done | bytes 262176 | tf_op jit(solution)/shard_map/ppermute | solution.py:282
  36.0 6.8 %all-to-all-start.1 = ((bf16[32,4,8,256]{3,2,1,0:T(8,128)(2,1)}), bf16[32,4,8,256]{3,2,1,0:T(8,128)(2,1)S(1)}, u32[]{:S(2)}, u32[]{:S(2)}) async-start(bf16[32,4,8,256]{3,2,1,0:T(8,128)(2,1)} %sum_grad.1), calls=%async_computation.1 | async-start | bytes 1048576 | tf_op jit(solution)/shard_map/all_to_all | solution.py:294
  42.8 3.5 %route.1 = (s32[192]{0:T(256)S(1)}, bf16[128,3,8,256]{3,2,1,0:T(8,128)(2,1)S(1)}) custom-call(s32[104]{0:T(128)S(1)} %copy-done.2, s32[104]{0:T(128)S(1)} %copy-done.3, bf16[128,3,8,256]{3,2,1,0:T(8,128)(2,1)} %bitcast.2.state_ref), custom_call_target="tpu_custom_call" | custom-call | tf_op jit(solution)/shard_map/route/pallas_call | solution.py:53
  46.3 8.1 %all-to-all-done.1 = bf16[32,4,8,256]{3,2,1,0:T(8,128)(2,1)S(1)} async-done(((bf16[32,4,8,256]{3,2,1,0:T(8,128)(2,1)}), bf16[32,4,8,256]{3,2,1,0:T(8,128)(2,1)S(1)}, u32[]{:S(2)}, u32[]{:S(2)}) %all-to-all-start.1) | async-done | bytes 524320 | tf_op jit(solution)/shard_map/all_to_all | solution.py:294
  54.4 2.5 %update.1 = (bf16[32,6,8,256]{3,2,1,0:T(8,128)(2,1)S(1)}, bf16[32,6,2,8,256]{4,3,2,1,0:T(8,128)(2,1)S(1)}) custom-call(s32[192]{0:T(256)S(1)} %get-tuple-element.44.table_ref, bf16[128,3,8,256]{3,2,1,0:T(8,128)(2,1)S(1)} %get-tuple-element.45.state_ref, bf16[128,8,256]{2,1,0:T(8,128)(2,1)S(1)} %bitcast.8), custom_call_target="tpu_custom_call" | custom-call | tf_op jit(solution)/shard_map/update/pallas_call | solution.py:178
  56.9 17.7 %all_to_all.20.w_ref = bf16[32,6,8,256]{3,2,1,0:T(8,128)(2,1)S(1)} all-to-all(bf16[32,6,8,256]{3,2,1,0:T(8,128)(2,1)S(1)} %get-tuple-element.52), channel_id=1, replica_groups=mesh['dp'=4,'expert'=32] {'expert'}, dimensions={0} | all-to-all | bytes 1572864 | tf_op jit(solution)/shard_map/all_to_all | solution.py:294
  74.6 3.8 %all-to-all-start.3 = ((bf16[32,6,2,8,256]{4,3,2,1,0:T(8,128)(2,1)}), bf16[32,6,2,8,256]{4,3,2,1,0:T(8,128)(2,1)S(1)}, u32[]{:S(2)}, u32[]{:S(2)}) async-start(bf16[32,6,2,8,256]{4,3,2,1,0:T(8,128)(2,1)} %copy-done.1), calls=%async_computation.3 | async-start | bytes 3145728 | tf_op jit(solution)/shard_map/all_to_all | solution.py:294
  78.5 1.0 collective-permute-start.6
  79.5 1.9 %collective-permute-start.7 = (bf16[16,6,8,256]{3,2,1,0:T(8,128)(2,1)S(1)}, bf16[16,6,8,256]{3,2,1,0:T(8,128)(2,1)S(1)}, u32[]{:S(2)}, u32[]{:S(2)}) collective-permute-start(bf16[16,6,8,256]{3,2,1,0:T(8,128)(2,1)S(1)} %get-tuple-element.66), channel_id=1, source_target_pairs={{0,96},{32,0},{64,32},{96,64},{1,97},{33,1},{65,33},{97,65},{2,98}... | collective-permute-start | bytes 1179656 | tf_op jit(solution)/shard_map/ppermute | solution.py:286
  81.4 1.5 %unpack_own.1 = (f32[6,128,512]{2,1,0:T(8,128)}, bf16[6,128,2048]{2,1,0:T(8,128)(2,1)}) custom-call(s32[1]{0:T(128)} %bitcast.me_ref, bf16[32,6,8,256]{3,2,1,0:T(8,128)(2,1)S(1)} %all_to_all.20.w_ref), custom_call_target="tpu_custom_call" | custom-call | tf_op jit(solution)/shard_map/unpack_own/pallas_call | solution.py:204
  82.9 2.7 %collective-permute-start.10 = (bf16[16,6,8,256]{3,2,1,0:T(8,128)(2,1)S(1)}, bf16[16,6,8,256]{3,2,1,0:T(8,128)(2,1)S(1)}, u32[]{:S(2)}, u32[]{:S(2)}) collective-permute-start(bf16[16,6,8,256]{3,2,1,0:T(8,128)(2,1)S(1)} %get-tuple-element.67), channel_id=1, source_target_pairs={{0,96},{32,0},{64,32},{96,64},{1,97},{33,1},{65,33},{97,65},{2,98}... | collective-permute-start | bytes 1179656 | tf_op jit(solution)/shard_map/ppermute | solution.py:286
  85.5 4.9 %collective-permute-done.6.a_ref = bf16[16,6,8,256]{3,2,1,0:T(8,128)(2,1)S(1)} collective-permute-done((bf16[16,6,8,256]{3,2,1,0:T(8,128)(2,1)S(1)}, bf16[16,6,8,256]{3,2,1,0:T(8,128)(2,1)S(1)}, u32[]{:S(2)}, u32[]{:S(2)}) %collective-permute-start.6) | collective-permute-done | bytes 393248 | tf_op jit(solution)/shard_map/ppermute | solution.py:282
  91.0 2.0 %collective-permute-start.9 = (bf16[16,6,8,256]{3,2,1,0:T(8,128)(2,1)S(1)}, bf16[16,6,8,256]{3,2,1,0:T(8,128)(2,1)S(1)}, u32[]{:S(2)}, u32[]{:S(2)}) collective-permute-start(bf16[16,6,8,256]{3,2,1,0:T(8,128)(2,1)S(1)} %collective-permute-done.7.b_ref), channel_id=1, source_target_pairs={{0,96},{32,0},{64,32},{96,64},{1,97},{33,1},{65,33},{97,65},{2,98}... | collective-permute-start | bytes 1179656 | tf_op jit(solution)/shard_map/ppermute | solution.py:286
  93.1 5.7 %collective-permute-done.11.b_ref = bf16[16,6,8,256]{3,2,1,0:T(8,128)(2,1)S(1)} collective-permute-done((bf16[16,6,8,256]{3,2,1,0:T(8,128)(2,1)S(1)}, bf16[16,6,8,256]{3,2,1,0:T(8,128)(2,1)S(1)}, u32[]{:S(2)}, u32[]{:S(2)}) %collective-permute-start.11) | collective-permute-done | bytes 393248 | tf_op jit(solution)/shard_map/ppermute | solution.py:282
  101.1 1.8 %unpack_moments.1 = (f32[6,128,512]{2,1,0:T(8,128)}, f32[6,128,512]{2,1,0:T(8,128)}) custom-call(bf16[32,6,2,8,256]{4,3,2,1,0:T(8,128)(2,1)S(1)} %all-to-all-done.3.m_ref), custom_call_target="tpu_custom_call" | custom-call | tf_op jit(solution)/shard_map/unpack_moments/pallas_call | solution.py:236
  102.9 4.4 %collective-permute-done.8.a_ref = bf16[16,6,8,256]{3,2,1,0:T(8,128)(2,1)S(1)} collective-permute-done((bf16[16,6,8,256]{3,2,1,0:T(8,128)(2,1)S(1)}, bf16[16,6,8,256]{3,2,1,0:T(8,128)(2,1)S(1)}, u32[]{:S(2)}, u32[]{:S(2)}) %collective-permute-start.8) | collective-permute-done | bytes 393248 | tf_op jit(solution)/shard_map/ppermute | solution.py:282
  (29 shorter events, 6.6 us)
Async XLA Ops:
  3.4 8.8 %copy-start = (bf16[1,4,128,2048]{3,2,1,0:T(8,128)(2,1)S(1)}, bf16[1,4,128,2048]{3,2,1,0:T(8,128)(2,1)}, u32[]{:S(2)}) copy-start(bf16[1,4,128,2048]{3,2,1,0:T(8,128)(2,1)} %param.6) | copy-start | bytes 6291460
  3.5 31.5 %all-to-all-start = ((bf16[32,4,3,8,256]{4,3,2,1,0:T(8,128)(2,1)}), bf16[32,4,3,8,256]{4,3,2,1,0:T(8,128)(2,1)}, u32[]{:S(2)}, u32[]{:S(2)}) async-start(bf16[32,4,3,8,256]{4,3,2,1,0:T(8,128)(2,1)} %pack_state.1), calls=%async_computation | async-start | bytes 3145728 | tf_op jit(solution)/shard_map/all_to_all | solution.py:294
  12.4 10.4 %collective-permute-start = (bf16[16,4,8,256]{3,2,1,0:T(8,128)(2,1)S(1)}, bf16[16,4,8,256]{3,2,1,0:T(8,128)(2,1)S(1)}, u32[]{:S(2)}, u32[]{:S(2)}) collective-permute-start(bf16[16,4,8,256]{3,2,1,0:T(8,128)(2,1)S(1)} %get-tuple-element.38), channel_id=1, source_target_pairs={{0,32},{32,64},{64,96},{96,0},{1,33},{33,65},{65,97},{97,1},{2,34}... | collective-permute-start | bytes 786440 | tf_op jit(solution)/shard_map/ppermute | solution.py:282
  14.1 8.9 %collective-permute-start.4 = (bf16[16,4,8,256]{3,2,1,0:T(8,128)(2,1)S(1)}, bf16[16,4,8,256]{3,2,1,0:T(8,128)(2,1)S(1)}, u32[]{:S(2)}, u32[]{:S(2)}) collective-permute-start(bf16[16,4,8,256]{3,2,1,0:T(8,128)(2,1)S(1)} %get-tuple-element.42), channel_id=1, source_target_pairs={{0,96},{32,0},{64,32},{96,64},{1,97},{33,1},{65,33},{97,65},{2,98}... | collective-permute-start | bytes 786440 | tf_op jit(solution)/shard_map/ppermute | solution.py:286
  16.7 11.8 %collective-permute-start.2 = (bf16[16,4,8,256]{3,2,1,0:T(8,128)(2,1)S(1)}, bf16[16,4,8,256]{3,2,1,0:T(8,128)(2,1)S(1)}, u32[]{:S(2)}, u32[]{:S(2)}) collective-permute-start(bf16[16,4,8,256]{3,2,1,0:T(8,128)(2,1)S(1)} %get-tuple-element.39), channel_id=1, source_target_pairs={{0,32},{32,64},{64,96},{96,0},{1,33},{33,65},{65,97},{97,1},{2,34}... | collective-permute-start | bytes 786440 | tf_op jit(solution)/shard_map/ppermute | solution.py:282
  16.7 11.7 %collective-permute-start.3 = (bf16[16,4,8,256]{3,2,1,0:T(8,128)(2,1)S(1)}, bf16[16,4,8,256]{3,2,1,0:T(8,128)(2,1)S(1)}, u32[]{:S(2)}, u32[]{:S(2)}) collective-permute-start(bf16[16,4,8,256]{3,2,1,0:T(8,128)(2,1)S(1)} %get-tuple-element.40), channel_id=1, source_target_pairs={{0,96},{32,0},{64,32},{96,64},{1,97},{33,1},{65,33},{97,65},{2,98}... | collective-permute-start | bytes 786440 | tf_op jit(solution)/shard_map/ppermute | solution.py:286
  22.9 11.1 %collective-permute-start.1 = (bf16[16,4,8,256]{3,2,1,0:T(8,128)(2,1)S(1)}, bf16[16,4,8,256]{3,2,1,0:T(8,128)(2,1)S(1)}, u32[]{:S(2)}, u32[]{:S(2)}) collective-permute-start(bf16[16,4,8,256]{3,2,1,0:T(8,128)(2,1)S(1)} %add_convert_fusion.1), channel_id=1, source_target_pairs={{0,32},{32,64},{64,96},{96,0},{1,33},{33,65},{65,97},{97,1},{2,34}... | collective-permute-start | bytes 786440 | tf_op jit(solution)/shard_map/ppermute | solution.py:282
  23.1 11.0 %collective-permute-start.5 = (bf16[16,4,8,256]{3,2,1,0:T(8,128)(2,1)S(1)}, bf16[16,4,8,256]{3,2,1,0:T(8,128)(2,1)S(1)}, u32[]{:S(2)}, u32[]{:S(2)}) collective-permute-start(bf16[16,4,8,256]{3,2,1,0:T(8,128)(2,1)S(1)} %add_convert_fusion), channel_id=1, source_target_pairs={{0,96},{32,0},{64,32},{96,64},{1,97},{33,1},{65,33},{97,65},{2,98}... | collective-permute-start | bytes 786440 | tf_op jit(solution)/shard_map/ppermute | solution.py:286
  35.0 7.8 %copy-start.2 = (s32[104]{0:T(128)S(1)}, s32[104]{0:T(128)}, u32[]{:S(2)}) copy-start(s32[104]{0:T(128)} %old_ref.1) | copy-start | bytes 1252
  35.0 7.8 %copy-start.3 = (s32[104]{0:T(128)S(1)}, s32[104]{0:T(128)}, u32[]{:S(2)}) copy-start(s32[104]{0:T(128)} %new_ref.1) | copy-start | bytes 1252
  36.0 18.4 %all-to-all-start.1 = ((bf16[32,4,8,256]{3,2,1,0:T(8,128)(2,1)}), bf16[32,4,8,256]{3,2,1,0:T(8,128)(2,1)S(1)}, u32[]{:S(2)}, u32[]{:S(2)}) async-start(bf16[32,4,8,256]{3,2,1,0:T(8,128)(2,1)} %sum_grad.1), calls=%async_computation.1 | async-start | bytes 1048576 | tf_op jit(solution)/shard_map/all_to_all | solution.py:294
  56.9 17.7 %copy-start.1 = (bf16[32,6,2,8,256]{4,3,2,1,0:T(8,128)(2,1)}, bf16[32,6,2,8,256]{4,3,2,1,0:T(8,128)(2,1)S(1)}, u32[]{:S(2)}) copy-start(bf16[32,6,2,8,256]{4,3,2,1,0:T(8,128)(2,1)S(1)} %get-tuple-element.59) | copy-start | bytes 4718596
  74.6 26.5 %all-to-all-start.3 = ((bf16[32,6,2,8,256]{4,3,2,1,0:T(8,128)(2,1)}), bf16[32,6,2,8,256]{4,3,2,1,0:T(8,128)(2,1)S(1)}, u32[]{:S(2)}, u32[]{:S(2)}) async-start(bf16[32,6,2,8,256]{4,3,2,1,0:T(8,128)(2,1)} %copy-done.1), calls=%async_computation.3 | async-start | bytes 3145728 | tf_op jit(solution)/shard_map/all_to_all | solution.py:294
  78.5 11.9 %collective-permute-start.6 = (bf16[16,6,8,256]{3,2,1,0:T(8,128)(2,1)S(1)}, bf16[16,6,8,256]{3,2,1,0:T(8,128)(2,1)S(1)}, u32[]{:S(2)}, u32[]{:S(2)}) collective-permute-start(bf16[16,6,8,256]{3,2,1,0:T(8,128)(2,1)S(1)} %get-tuple-element.67), channel_id=1, source_target_pairs={{0,32},{32,64},{64,96},{96,0},{1,33},{33,65},{65,97},{97,1},{2,34}... | collective-permute-start | bytes 1179656 | tf_op jit(solution)/shard_map/ppermute | solution.py:282
  79.5 10.9 %collective-permute-start.7 = (bf16[16,6,8,256]{3,2,1,0:T(8,128)(2,1)S(1)}, bf16[16,6,8,256]{3,2,1,0:T(8,128)(2,1)S(1)}, u32[]{:S(2)}, u32[]{:S(2)}) collective-permute-start(bf16[16,6,8,256]{3,2,1,0:T(8,128)(2,1)S(1)} %get-tuple-element.66), channel_id=1, source_target_pairs={{0,96},{32,0},{64,32},{96,64},{1,97},{33,1},{65,33},{97,65},{2,98}... | collective-permute-start | bytes 1179656 | tf_op jit(solution)/shard_map/ppermute | solution.py:286
  82.9 16.0 %collective-permute-start.11 = (bf16[16,6,8,256]{3,2,1,0:T(8,128)(2,1)S(1)}, bf16[16,6,8,256]{3,2,1,0:T(8,128)(2,1)S(1)}, u32[]{:S(2)}, u32[]{:S(2)}) collective-permute-start(bf16[16,6,8,256]{3,2,1,0:T(8,128)(2,1)S(1)} %get-tuple-element.66), channel_id=1, source_target_pairs={{0,32},{32,64},{64,96},{96,0},{1,33},{33,65},{65,97},{97,1},{2,34}... | collective-permute-start | bytes 1179656 | tf_op jit(solution)/shard_map/ppermute | solution.py:282
  82.9 16.9 %collective-permute-start.10 = (bf16[16,6,8,256]{3,2,1,0:T(8,128)(2,1)S(1)}, bf16[16,6,8,256]{3,2,1,0:T(8,128)(2,1)S(1)}, u32[]{:S(2)}, u32[]{:S(2)}) collective-permute-start(bf16[16,6,8,256]{3,2,1,0:T(8,128)(2,1)S(1)} %get-tuple-element.67), channel_id=1, source_target_pairs={{0,96},{32,0},{64,32},{96,64},{1,97},{33,1},{65,33},{97,65},{2,98}... | collective-permute-start | bytes 1179656 | tf_op jit(solution)/shard_map/ppermute | solution.py:286
  90.4 16.8 %collective-permute-start.8 = (bf16[16,6,8,256]{3,2,1,0:T(8,128)(2,1)S(1)}, bf16[16,6,8,256]{3,2,1,0:T(8,128)(2,1)S(1)}, u32[]{:S(2)}, u32[]{:S(2)}) collective-permute-start(bf16[16,6,8,256]{3,2,1,0:T(8,128)(2,1)S(1)} %collective-permute-done.6.a_ref), channel_id=1, source_target_pairs={{0,32},{32,64},{64,96},{96,0},{1,33},{33,65},{65,97},{97,1},{2,34}... | collective-permute-start | bytes 1179656 | tf_op jit(solution)/shard_map/ppermute | solution.py:282
  91.0 16.2 %collective-permute-start.9 = (bf16[16,6,8,256]{3,2,1,0:T(8,128)(2,1)S(1)}, bf16[16,6,8,256]{3,2,1,0:T(8,128)(2,1)S(1)}, u32[]{:S(2)}, u32[]{:S(2)}) collective-permute-start(bf16[16,6,8,256]{3,2,1,0:T(8,128)(2,1)S(1)} %collective-permute-done.7.b_ref), channel_id=1, source_target_pairs={{0,96},{32,0},{64,32},{96,64},{1,97},{33,1},{65,33},{97,65},{2,98}... | collective-permute-start | bytes 1179656 | tf_op jit(solution)/shard_map/ppermute | solution.py:286

commit v6 on v5

--- a/solution.py
+++ b/solution.py
@@ -130,7 +130,7 @@
     for h, refs in enumerate(((own_a, ua, da), (own_b, ub, db))):
         for j in range(half):
             own, up, down = (ref[j].astype(F32) for ref in refs)
-            out_ref[h * half + j] = (own + up + down).astype(BF16)
+            out_ref[PEERS - 1 - (h * half + j)] = (own + up + down).astype(BF16)
 
 
 def sum_grad(*halves):
@@ -160,12 +160,12 @@
             row = table_ref[d * NEW + s]
             has = row >= 0
             row = jnp.maximum(row, 0)
-            gradient = grad_ref[row].astype(F32)
+            gradient = grad_ref[row ^ ((PEERS - 1) * OLD)].astype(F32)
             m1 = state_ref[row, 0].astype(F32)
             m2 = state_ref[row, 1].astype(F32)
             w = state_ref[row, 2].astype(F32)
             w, m1, m2 = adam_step(gradient, m1, m2, w)
-            weight_ref[d, s] = jnp.where(has, w, 0.0).astype(BF16)
+            weight_ref[PEERS - 1 - d, s] = jnp.where(has, w, 0.0).astype(BF16)
             moments_ref[d, s, 0] = jnp.where(has, m1, 0.0).astype(BF16)
             moments_ref[d, s, 1] = jnp.where(has, m2, 0.0).astype(BF16)
         return 0
@@ -194,7 +194,7 @@
     for r in range(w_out.shape[1] // PR):
         for c in range(2):
             rows, lanes = slice(r * PR, (r + 1) * PR), slice(c * PC, (c + 1) * PC)
-            piece = w_ref[first + 2 * r + c]
+            piece = w_ref[PEERS - 1 - (first + 2 * r + c)]
             w_out[:, rows, lanes] = piece.astype(F32)
             out_ref[:, rows, lanes] = piece
 
@@ -252,7 +252,7 @@
         for r in range(out_ref.shape[1] // PR):
             for c in range(2):
                 rows, lanes = slice(r * PR, (r + 1) * PR), slice(c * PC, (c + 1) * PC)
-                out_ref[:, rows, lanes] = ref[2 * r + c]
+                out_ref[:, rows, lanes] = ref[PEERS // 2 - 1 - (2 * r + c)]
 
     pl.when(half == 0)(lambda: copy(a_ref))
     pl.when(half == 1)(lambda: copy(b_ref))
@@ -292,6 +292,11 @@
 
 def exchange(values):
     return lax.all_to_all(values, "expert", split_axis=0, concat_axis=0, tiled=True)
+
+
+def exchange_backward(values):
+    order = [list(range(PEERS - 1, -1, -1))]
+    return lax.all_to_all(values, "expert", split_axis=0, concat_axis=0, tiled=True, axis_index_groups=order)
 
 
 def shards(grad_parts, first_moment, second_moment, master_weight, old_owner, new_owner):
@@ -306,16 +311,16 @@
     ub, da = send_up(up_b), send_down(down_a)
     ua, db = send_up(add(up_a, far_up)), send_down(add(down_b, far_down))
     state, ua, ub, da, db = lax.optimization_barrier((state, ua, ub, da, db))
-    grad = exchange(sum_grad(own_a, own_b, ua, ub, da, db))
+    grad = exchange_backward(sum_grad(own_a, own_b, ua, ub, da, db))
     table, state = route(old_owner, new_owner, state.reshape(PEERS * OLD, 3, PR, PC))
     weight, moments = update(
         table,
         state,
         grad.reshape(PEERS * OLD, PR, PC),
     )
-    weight = exchange(weight)
+    weight = exchange_backward(weight)
     weight, moments = lax.optimization_barrier((weight, moments))
-    wa, wb = weight[: PEERS // 2], weight[PEERS // 2 :]
+    wb, wa = weight[: PEERS // 2], weight[PEERS // 2 :]
     ua, da = send_up(wa), send_down(wa)
     ub, db = send_up(wb), send_down(wb)
     moments = exchange(moments)

time: 109 us -> 108 us (level)
  waiting for transfers between devices: 36.1 us -> 32.3 us
  starting transfers between devices: 37.1 us -> 39.7 us
    all_to_all x3 -> x2, waiting for transfers between devices: 9.47 us -> 1.39 us  [exchange(): lax.all_to_all(values, 'expert', split_axis=0, concat_axis=0, tiled=True)]
    all_to_all x0 -> x1, starting transfers between devices: none -> 7.98 us  [exchange_backward(): lax.all_to_all(values, 'expert', split_axis=0, concat_axis=0, tiled=True,...]
    all_to_all x3 -> x2, starting transfers between devices: 19.4 us -> 14 us  [exchange(): lax.all_to_all(values, 'expert', split_axis=0, concat_axis=0, tiled=True)]
    all_to_all x0 -> x1, waiting for transfers between devices: none -> 4.34 us  [exchange_backward(): lax.all_to_all(values, 'expert', split_axis=0, concat_axis=0, tiled=True,...]
where the time goes in v6:
time: 108 us; the launch traced here: 107 us
  starting transfers between devices  39.7 us (37%)
  waiting for transfers between devices  32.3 us (30%)
  blocking collectives  17.7 us (16%)
  Pallas kernels  16.3 us (15%)
    ppermute x6, waiting for transfers between devices, send_up(): return lax.ppermute(x, 'dp', UP)  26.6 us
    all_to_all x1, blocking collectives, exchange_backward(): lax.all_to_all(values, 'expert', split_axis=0, concat_axis=0, tiled=True,...  17.7 us
    ppermute x6, starting transfers between devices, send_down(): return lax.ppermute(x, 'dp', DOWN)  14.2 us
    all_to_all x2, starting transfers between devices, exchange(): lax.all_to_all(values, 'expert', split_axis=0, concat_axis=0, tiled=True)  14 us
    all_to_all x1, starting transfers between devices, exchange_backward(): lax.all_to_all(values, 'expert', split_axis=0, concat_axis=0, tiled=True,...  7.98 us
    all_to_all x1, waiting for transfers between devices, exchange_backward(): lax.all_to_all(values, 'expert', split_axis=0, concat_axis=0, tiled=True,...  4.34 us
    ppermute x6, starting transfers between devices, send_up(): return lax.ppermute(x, 'dp', UP)  3.53 us
    pallas_call x1, Pallas kernels, route(): pl.pallas_call(route_kernel, out_shape=(jax.ShapeDtypeStruct((PEERS * NEW...  3.51 us
  transfers between devices with their start and end apart: 15, of which 9 were waited for; matrix products, arithmetic and copies ran while one was open for 0% of the time, Pallas kernels for 8%

profile of v6, /device:TPU:1, one launch (start us, length us, event | category | flops | bytes accessed | tf_op | source)
XLA Modules:
  0.0 107.1 jit_solution(18424319568642957244)
XLA Ops:
  0.6 2.8 %pack_state.1 = bf16[32,4,3,8,256]{4,3,2,1,0:T(8,128)(2,1)} custom-call(f32[4,128,512]{2,1,0:T(8,128)} %m1_ref.1, f32[4,128,512]{2,1,0:T(8,128)} %m2_ref.1, f32[4,128,512]{2,1,0:T(8,128)} %w_ref.1), custom_call_target="tpu_custom_call" | custom-call | tf_op jit(solution)/shard_map/pack_state/pallas_call | solution.py:82
  3.5 8.8 %all-to-all-start = ((bf16[32,4,3,8,256]{4,3,2,1,0:T(8,128)(2,1)}), bf16[32,4,3,8,256]{4,3,2,1,0:T(8,128)(2,1)}, u32[]{:S(2)}, u32[]{:S(2)}) async-start(bf16[32,4,3,8,256]{4,3,2,1,0:T(8,128)(2,1)} %pack_state.1), calls=%async_computation | async-start | bytes 3145728 | tf_op jit(solution)/shard_map/all_to_all | solution.py:294
  12.4 1.7 %collective-permute-start = (bf16[16,4,8,256]{3,2,1,0:T(8,128)(2,1)S(1)}, bf16[16,4,8,256]{3,2,1,0:T(8,128)(2,1)S(1)}, u32[]{:S(2)}, u32[]{:S(2)}) collective-permute-start(bf16[16,4,8,256]{3,2,1,0:T(8,128)(2,1)S(1)} %get-tuple-element.38), channel_id=1, source_target_pairs={{0,32},{32,64},{64,96},{96,0},{1,33},{33,65},{65,97},{97,1},{2,34}... | collective-permute-start | bytes 786440 | tf_op jit(solution)/shard_map/ppermute | solution.py:282
  14.1 2.2 %collective-permute-start.4 = (bf16[16,4,8,256]{3,2,1,0:T(8,128)(2,1)S(1)}, bf16[16,4,8,256]{3,2,1,0:T(8,128)(2,1)S(1)}, u32[]{:S(2)}, u32[]{:S(2)}) collective-permute-start(bf16[16,4,8,256]{3,2,1,0:T(8,128)(2,1)S(1)} %get-tuple-element.42), channel_id=1, source_target_pairs={{0,96},{32,0},{64,32},{96,64},{1,97},{33,1},{65,33},{97,65},{2,98}... | collective-permute-start | bytes 786440 | tf_op jit(solution)/shard_map/ppermute | solution.py:286
  16.7 2.7 %collective-permute-start.3 = (bf16[16,4,8,256]{3,2,1,0:T(8,128)(2,1)S(1)}, bf16[16,4,8,256]{3,2,1,0:T(8,128)(2,1)S(1)}, u32[]{:S(2)}, u32[]{:S(2)}) collective-permute-start(bf16[16,4,8,256]{3,2,1,0:T(8,128)(2,1)S(1)} %get-tuple-element.40), channel_id=1, source_target_pairs={{0,96},{32,0},{64,32},{96,64},{1,97},{33,1},{65,33},{97,65},{2,98}... | collective-permute-start | bytes 786440 | tf_op jit(solution)/shard_map/ppermute | solution.py:286
  19.4 3.4 %collective-permute-done = bf16[16,4,8,256]{3,2,1,0:T(8,128)(2,1)S(1)} collective-permute-done((bf16[16,4,8,256]{3,2,1,0:T(8,128)(2,1)S(1)}, bf16[16,4,8,256]{3,2,1,0:T(8,128)(2,1)S(1)}, u32[]{:S(2)}, u32[]{:S(2)}) %collective-permute-start) | collective-permute-done | bytes 262176 | tf_op jit(solution)/shard_map/ppermute | solution.py:282
  23.1 2.7 %collective-permute-start.5 = (bf16[16,4,8,256]{3,2,1,0:T(8,128)(2,1)S(1)}, bf16[16,4,8,256]{3,2,1,0:T(8,128)(2,1)S(1)}, u32[]{:S(2)}, u32[]{:S(2)}) collective-permute-start(bf16[16,4,8,256]{3,2,1,0:T(8,128)(2,1)S(1)} %add_convert_fusion), channel_id=1, source_target_pairs={{0,96},{32,0},{64,32},{96,64},{1,97},{33,1},{65,33},{97,65},{2,98}... | collective-permute-start | bytes 786440 | tf_op jit(solution)/shard_map/ppermute | solution.py:286
  25.8 2.6 %collective-permute-done.2.ub = bf16[16,4,8,256]{3,2,1,0:T(8,128)(2,1)S(1)} collective-permute-done((bf16[16,4,8,256]{3,2,1,0:T(8,128)(2,1)S(1)}, bf16[16,4,8,256]{3,2,1,0:T(8,128)(2,1)S(1)}, u32[]{:S(2)}, u32[]{:S(2)}) %collective-permute-start.2) | collective-permute-done | bytes 262176 | tf_op jit(solution)/shard_map/ppermute | solution.py:282
  28.4 5.6 %collective-permute-done.1.ua = bf16[16,4,8,256]{3,2,1,0:T(8,128)(2,1)S(1)} collective-permute-done((bf16[16,4,8,256]{3,2,1,0:T(8,128)(2,1)S(1)}, bf16[16,4,8,256]{3,2,1,0:T(8,128)(2,1)S(1)}, u32[]{:S(2)}, u32[]{:S(2)}) %collective-permute-start.1) | collective-permute-done | bytes 262176 | tf_op jit(solution)/shard_map/ppermute | solution.py:282
  36.0 8.0 %all-to-all-start.1 = ((bf16[32,4,8,256]{3,2,1,0:T(8,128)(2,1)}), bf16[32,4,8,256]{3,2,1,0:T(8,128)(2,1)S(1)}, u32[]{:S(2)}, u32[]{:S(2)}) async-start(bf16[32,4,8,256]{3,2,1,0:T(8,128)(2,1)} %sum_grad.1), calls=%async_computation.1 | async-start | bytes 1048576 | tf_op jit(solution)/shard_map/all_to_all | solution.py:299
  44.0 3.5 %route.1 = (s32[192]{0:T(256)S(1)}, bf16[128,3,8,256]{3,2,1,0:T(8,128)(2,1)S(1)}) custom-call(s32[104]{0:T(128)S(1)} %copy-done.2, s32[104]{0:T(128)S(1)} %copy-done.3, bf16[128,3,8,256]{3,2,1,0:T(8,128)(2,1)} %bitcast.2.state_ref), custom_call_target="tpu_custom_call" | custom-call | tf_op jit(solution)/shard_map/route/pallas_call | solution.py:53
  47.5 4.3 %all-to-all-done.1 = bf16[32,4,8,256]{3,2,1,0:T(8,128)(2,1)S(1)} async-done(((bf16[32,4,8,256]{3,2,1,0:T(8,128)(2,1)}), bf16[32,4,8,256]{3,2,1,0:T(8,128)(2,1)S(1)}, u32[]{:S(2)}, u32[]{:S(2)}) %all-to-all-start.1) | async-done | bytes 524320 | tf_op jit(solution)/shard_map/all_to_all | solution.py:299
  51.8 2.5 %update.1 = (bf16[32,6,8,256]{3,2,1,0:T(8,128)(2,1)S(1)}, bf16[32,6,2,8,256]{4,3,2,1,0:T(8,128)(2,1)S(1)}) custom-call(s32[192]{0:T(256)S(1)} %get-tuple-element.44.table_ref, bf16[128,3,8,256]{3,2,1,0:T(8,128)(2,1)S(1)} %get-tuple-element.45.state_ref, bf16[128,8,256]{2,1,0:T(8,128)(2,1)S(1)} %bitcast.8), custom_call_target="tpu_custom_call" | custom-call | tf_op jit(solution)/shard_map/update/pallas_call | solution.py:178
  54.4 17.7 %all_to_all.20.w_ref = bf16[32,6,8,256]{3,2,1,0:T(8,128)(2,1)S(1)} all-to-all(bf16[32,6,8,256]{3,2,1,0:T(8,128)(2,1)S(1)} %get-tuple-element.52), channel_id=1, replica_groups={{31,30,29,28,27,26,25,24,23,22,21,20,19,18,17,16,15,14,13,12,11,10,9,8,..., dimensions={0} | all-to-all | bytes 1572864 | tf_op jit(solution)/shard_map/all_to_all | solution.py:299
  72.1 5.3 %all-to-all-start.3 = ((bf16[32,6,2,8,256]{4,3,2,1,0:T(8,128)(2,1)}), bf16[32,6,2,8,256]{4,3,2,1,0:T(8,128)(2,1)S(1)}, u32[]{:S(2)}, u32[]{:S(2)}) async-start(bf16[32,6,2,8,256]{4,3,2,1,0:T(8,128)(2,1)} %copy-done.1), calls=%async_computation.3 | async-start | bytes 3145728 | tf_op jit(solution)/shard_map/all_to_all | solution.py:294
  77.4 1.0 collective-permute-start.6
  78.4 1.9 %collective-permute-start.7 = (bf16[16,6,8,256]{3,2,1,0:T(8,128)(2,1)S(1)}, bf16[16,6,8,256]{3,2,1,0:T(8,128)(2,1)S(1)}, u32[]{:S(2)}, u32[]{:S(2)}) collective-permute-start(bf16[16,6,8,256]{3,2,1,0:T(8,128)(2,1)S(1)} %get-tuple-element.66), channel_id=1, source_target_pairs={{0,96},{32,0},{64,32},{96,64},{1,97},{33,1},{65,33},{97,65},{2,98}... | collective-permute-start | bytes 1179656 | tf_op jit(solution)/shard_map/ppermute | solution.py:286
  80.3 1.5 %unpack_own.1 = (f32[6,128,512]{2,1,0:T(8,128)}, bf16[6,128,2048]{2,1,0:T(8,128)(2,1)}) custom-call(s32[1]{0:T(128)} %bitcast.me_ref, bf16[32,6,8,256]{3,2,1,0:T(8,128)(2,1)S(1)} %all_to_all.20.w_ref), custom_call_target="tpu_custom_call" | custom-call | tf_op jit(solution)/shard_map/unpack_own/pallas_call | solution.py:204
  81.8 2.7 %collective-permute-start.10 = (bf16[16,6,8,256]{3,2,1,0:T(8,128)(2,1)S(1)}, bf16[16,6,8,256]{3,2,1,0:T(8,128)(2,1)S(1)}, u32[]{:S(2)}, u32[]{:S(2)}) collective-permute-start(bf16[16,6,8,256]{3,2,1,0:T(8,128)(2,1)S(1)} %get-tuple-element.67), channel_id=1, source_target_pairs={{0,96},{32,0},{64,32},{96,64},{1,97},{33,1},{65,33},{97,65},{2,98}... | collective-permute-start | bytes 1179656 | tf_op jit(solution)/shard_map/ppermute | solution.py:286
  84.5 4.8 %collective-permute-done.6.a_ref = bf16[16,6,8,256]{3,2,1,0:T(8,128)(2,1)S(1)} collective-permute-done((bf16[16,6,8,256]{3,2,1,0:T(8,128)(2,1)S(1)}, bf16[16,6,8,256]{3,2,1,0:T(8,128)(2,1)S(1)}, u32[]{:S(2)}, u32[]{:S(2)}) %collective-permute-start.6) | collective-permute-done | bytes 393248 | tf_op jit(solution)/shard_map/ppermute | solution.py:282
  89.9 2.0 %collective-permute-start.9 = (bf16[16,6,8,256]{3,2,1,0:T(8,128)(2,1)S(1)}, bf16[16,6,8,256]{3,2,1,0:T(8,128)(2,1)S(1)}, u32[]{:S(2)}, u32[]{:S(2)}) collective-permute-start(bf16[16,6,8,256]{3,2,1,0:T(8,128)(2,1)S(1)} %collective-permute-done.7.b_ref), channel_id=1, source_target_pairs={{0,96},{32,0},{64,32},{96,64},{1,97},{33,1},{65,33},{97,65},{2,98}... | collective-permute-start | bytes 1179656 | tf_op jit(solution)/shard_map/ppermute | solution.py:286
  92.0 5.7 %collective-permute-done.11.b_ref = bf16[16,6,8,256]{3,2,1,0:T(8,128)(2,1)S(1)} collective-permute-done((bf16[16,6,8,256]{3,2,1,0:T(8,128)(2,1)S(1)}, bf16[16,6,8,256]{3,2,1,0:T(8,128)(2,1)S(1)}, u32[]{:S(2)}, u32[]{:S(2)}) %collective-permute-start.11) | collective-permute-done | bytes 393248 | tf_op jit(solution)/shard_map/ppermute | solution.py:282
  100.0 1.8 %unpack_moments.1 = (f32[6,128,512]{2,1,0:T(8,128)}, f32[6,128,512]{2,1,0:T(8,128)}) custom-call(bf16[32,6,2,8,256]{4,3,2,1,0:T(8,128)(2,1)S(1)} %all-to-all-done.3.m_ref), custom_call_target="tpu_custom_call" | custom-call | tf_op jit(solution)/shard_map/unpack_moments/pallas_call | solution.py:236
  101.8 4.4 %collective-permute-done.8.a_ref = bf16[16,6,8,256]{3,2,1,0:T(8,128)(2,1)S(1)} collective-permute-done((bf16[16,6,8,256]{3,2,1,0:T(8,128)(2,1)S(1)}, bf16[16,6,8,256]{3,2,1,0:T(8,128)(2,1)S(1)}, u32[]{:S(2)}, u32[]{:S(2)}) %collective-permute-start.8) | collective-permute-done | bytes 393248 | tf_op jit(solution)/shard_map/ppermute | solution.py:282
  (29 shorter events, 6.6 us)
Async XLA Ops:
  3.4 8.8 %copy-start = (bf16[1,4,128,2048]{3,2,1,0:T(8,128)(2,1)S(1)}, bf16[1,4,128,2048]{3,2,1,0:T(8,128)(2,1)}, u32[]{:S(2)}) copy-start(bf16[1,4,128,2048]{3,2,1,0:T(8,128)(2,1)} %param.6) | copy-start | bytes 6291460
  3.5 31.5 %all-to-all-start = ((bf16[32,4,3,8,256]{4,3,2,1,0:T(8,128)(2,1)}), bf16[32,4,3,8,256]{4,3,2,1,0:T(8,128)(2,1)}, u32[]{:S(2)}, u32[]{:S(2)}) async-start(bf16[32,4,3,8,256]{4,3,2,1,0:T(8,128)(2,1)} %pack_state.1), calls=%async_computation | async-start | bytes 3145728 | tf_op jit(solution)/shard_map/all_to_all | solution.py:294
  12.4 10.4 %collective-permute-start = (bf16[16,4,8,256]{3,2,1,0:T(8,128)(2,1)S(1)}, bf16[16,4,8,256]{3,2,1,0:T(8,128)(2,1)S(1)}, u32[]{:S(2)}, u32[]{:S(2)}) collective-permute-start(bf16[16,4,8,256]{3,2,1,0:T(8,128)(2,1)S(1)} %get-tuple-element.38), channel_id=1, source_target_pairs={{0,32},{32,64},{64,96},{96,0},{1,33},{33,65},{65,97},{97,1},{2,34}... | collective-permute-start | bytes 786440 | tf_op jit(solution)/shard_map/ppermute | solution.py:282
  14.1 8.9 %collective-permute-start.4 = (bf16[16,4,8,256]{3,2,1,0:T(8,128)(2,1)S(1)}, bf16[16,4,8,256]{3,2,1,0:T(8,128)(2,1)S(1)}, u32[]{:S(2)}, u32[]{:S(2)}) collective-permute-start(bf16[16,4,8,256]{3,2,1,0:T(8,128)(2,1)S(1)} %get-tuple-element.42), channel_id=1, source_target_pairs={{0,96},{32,0},{64,32},{96,64},{1,97},{33,1},{65,33},{97,65},{2,98}... | collective-permute-start | bytes 786440 | tf_op jit(solution)/shard_map/ppermute | solution.py:286
  16.7 11.8 %collective-permute-start.2 = (bf16[16,4,8,256]{3,2,1,0:T(8,128)(2,1)S(1)}, bf16[16,4,8,256]{3,2,1,0:T(8,128)(2,1)S(1)}, u32[]{:S(2)}, u32[]{:S(2)}) collective-permute-start(bf16[16,4,8,256]{3,2,1,0:T(8,128)(2,1)S(1)} %get-tuple-element.39), channel_id=1, source_target_pairs={{0,32},{32,64},{64,96},{96,0},{1,33},{33,65},{65,97},{97,1},{2,34}... | collective-permute-start | bytes 786440 | tf_op jit(solution)/shard_map/ppermute | solution.py:282
  16.7 11.7 %collective-permute-start.3 = (bf16[16,4,8,256]{3,2,1,0:T(8,128)(2,1)S(1)}, bf16[16,4,8,256]{3,2,1,0:T(8,128)(2,1)S(1)}, u32[]{:S(2)}, u32[]{:S(2)}) collective-permute-start(bf16[16,4,8,256]{3,2,1,0:T(8,128)(2,1)S(1)} %get-tuple-element.40), channel_id=1, source_target_pairs={{0,96},{32,0},{64,32},{96,64},{1,97},{33,1},{65,33},{97,65},{2,98}... | collective-permute-start | bytes 786440 | tf_op jit(solution)/shard_map/ppermute | solution.py:286
  22.9 11.1 %collective-permute-start.1 = (bf16[16,4,8,256]{3,2,1,0:T(8,128)(2,1)S(1)}, bf16[16,4,8,256]{3,2,1,0:T(8,128)(2,1)S(1)}, u32[]{:S(2)}, u32[]{:S(2)}) collective-permute-start(bf16[16,4,8,256]{3,2,1,0:T(8,128)(2,1)S(1)} %add_convert_fusion.1), channel_id=1, source_target_pairs={{0,32},{32,64},{64,96},{96,0},{1,33},{33,65},{65,97},{97,1},{2,34}... | collective-permute-start | bytes 786440 | tf_op jit(solution)/shard_map/ppermute | solution.py:282
  23.1 11.0 %collective-permute-start.5 = (bf16[16,4,8,256]{3,2,1,0:T(8,128)(2,1)S(1)}, bf16[16,4,8,256]{3,2,1,0:T(8,128)(2,1)S(1)}, u32[]{:S(2)}, u32[]{:S(2)}) collective-permute-start(bf16[16,4,8,256]{3,2,1,0:T(8,128)(2,1)S(1)} %add_convert_fusion), channel_id=1, source_target_pairs={{0,96},{32,0},{64,32},{96,64},{1,97},{33,1},{65,33},{97,65},{2,98}... | collective-permute-start | bytes 786440 | tf_op jit(solution)/shard_map/ppermute | solution.py:286
  35.0 9.0 %copy-start.2 = (s32[104]{0:T(128)S(1)}, s32[104]{0:T(128)}, u32[]{:S(2)}) copy-start(s32[104]{0:T(128)} %old_ref.1) | copy-start | bytes 1252
  35.0 9.0 %copy-start.3 = (s32[104]{0:T(128)S(1)}, s32[104]{0:T(128)}, u32[]{:S(2)}) copy-start(s32[104]{0:T(128)} %new_ref.1) | copy-start | bytes 1252
  36.0 15.9 %all-to-all-start.1 = ((bf16[32,4,8,256]{3,2,1,0:T(8,128)(2,1)}), bf16[32,4,8,256]{3,2,1,0:T(8,128)(2,1)S(1)}, u32[]{:S(2)}, u32[]{:S(2)}) async-start(bf16[32,4,8,256]{3,2,1,0:T(8,128)(2,1)} %sum_grad.1), calls=%async_computation.1 | async-start | bytes 1048576 | tf_op jit(solution)/shard_map/all_to_all | solution.py:299
  54.4 17.7 %copy-start.1 = (bf16[32,6,2,8,256]{4,3,2,1,0:T(8,128)(2,1)}, bf16[32,6,2,8,256]{4,3,2,1,0:T(8,128)(2,1)S(1)}, u32[]{:S(2)}) copy-start(bf16[32,6,2,8,256]{4,3,2,1,0:T(8,128)(2,1)S(1)} %get-tuple-element.59) | copy-start | bytes 4718596
  72.1 27.9 %all-to-all-start.3 = ((bf16[32,6,2,8,256]{4,3,2,1,0:T(8,128)(2,1)}), bf16[32,6,2,8,256]{4,3,2,1,0:T(8,128)(2,1)S(1)}, u32[]{:S(2)}, u32[]{:S(2)}) async-start(bf16[32,6,2,8,256]{4,3,2,1,0:T(8,128)(2,1)} %copy-done.1), calls=%async_computation.3 | async-start | bytes 3145728 | tf_op jit(solution)/shard_map/all_to_all | solution.py:294
  77.4 11.9 %collective-permute-start.6 = (bf16[16,6,8,256]{3,2,1,0:T(8,128)(2,1)S(1)}, bf16[16,6,8,256]{3,2,1,0:T(8,128)(2,1)S(1)}, u32[]{:S(2)}, u32[]{:S(2)}) collective-permute-start(bf16[16,6,8,256]{3,2,1,0:T(8,128)(2,1)S(1)} %get-tuple-element.67), channel_id=1, source_target_pairs={{0,32},{32,64},{64,96},{96,0},{1,33},{33,65},{65,97},{97,1},{2,34}... | collective-permute-start | bytes 1179656 | tf_op jit(solution)/shard_map/ppermute | solution.py:282
  78.4 10.9 %collective-permute-start.7 = (bf16[16,6,8,256]{3,2,1,0:T(8,128)(2,1)S(1)}, bf16[16,6,8,256]{3,2,1,0:T(8,128)(2,1)S(1)}, u32[]{:S(2)}, u32[]{:S(2)}) collective-permute-start(bf16[16,6,8,256]{3,2,1,0:T(8,128)(2,1)S(1)} %get-tuple-element.66), channel_id=1, source_target_pairs={{0,96},{32,0},{64,32},{96,64},{1,97},{33,1},{65,33},{97,65},{2,98}... | collective-permute-start | bytes 1179656 | tf_op jit(solution)/shard_map/ppermute | solution.py:286
  81.8 16.0 %collective-permute-start.11 = (bf16[16,6,8,256]{3,2,1,0:T(8,128)(2,1)S(1)}, bf16[16,6,8,256]{3,2,1,0:T(8,128)(2,1)S(1)}, u32[]{:S(2)}, u32[]{:S(2)}) collective-permute-start(bf16[16,6,8,256]{3,2,1,0:T(8,128)(2,1)S(1)} %get-tuple-element.66), channel_id=1, source_target_pairs={{0,32},{32,64},{64,96},{96,0},{1,33},{33,65},{65,97},{97,1},{2,34}... | collective-permute-start | bytes 1179656 | tf_op jit(solution)/shard_map/ppermute | solution.py:282
  81.8 16.9 %collective-permute-start.10 = (bf16[16,6,8,256]{3,2,1,0:T(8,128)(2,1)S(1)}, bf16[16,6,8,256]{3,2,1,0:T(8,128)(2,1)S(1)}, u32[]{:S(2)}, u32[]{:S(2)}) collective-permute-start(bf16[16,6,8,256]{3,2,1,0:T(8,128)(2,1)S(1)} %get-tuple-element.67), channel_id=1, source_target_pairs={{0,96},{32,0},{64,32},{96,64},{1,97},{33,1},{65,33},{97,65},{2,98}... | collective-permute-start | bytes 1179656 | tf_op jit(solution)/shard_map/ppermute | solution.py:286
  89.3 16.8 %collective-permute-start.8 = (bf16[16,6,8,256]{3,2,1,0:T(8,128)(2,1)S(1)}, bf16[16,6,8,256]{3,2,1,0:T(8,128)(2,1)S(1)}, u32[]{:S(2)}, u32[]{:S(2)}) collective-permute-start(bf16[16,6,8,256]{3,2,1,0:T(8,128)(2,1)S(1)} %collective-permute-done.6.a_ref), channel_id=1, source_target_pairs={{0,32},{32,64},{64,96},{96,0},{1,33},{33,65},{65,97},{97,1},{2,34}... | collective-permute-start | bytes 1179656 | tf_op jit(solution)/shard_map/ppermute | solution.py:282
  89.9 16.2 %collective-permute-start.9 = (bf16[16,6,8,256]{3,2,1,0:T(8,128)(2,1)S(1)}, bf16[16,6,8,256]{3,2,1,0:T(8,128)(2,1)S(1)}, u32[]{:S(2)}, u32[]{:S(2)}) collective-permute-start(bf16[16,6,8,256]{3,2,1,0:T(8,128)(2,1)S(1)} %collective-permute-done.7.b_ref), channel_id=1, source_target_pairs={{0,96},{32,0},{64,32},{96,64},{1,97},{33,1},{65,33},{97,65},{2,98}... | collective-permute-start | bytes 1179656 | tf_op jit(solution)/shard_map/ppermute | solution.py:286
